TPU v7x, 512 devices: a whole 4x4x16 slice. The times are simulated.
512 devices in a mesh: pair: 32 (over y, x, core), aux: 16 (over z).
Axes of the slice: x: 4, y: 4, z: 16, core: 2. Of those that a mesh axis runs over, the one named last changes fastest.
Arguments:
- integrals: bfloat16 [8192, 256, 64], P(('pair', 'aux')), may hold values from -6 to 6
- amplitudes: bfloat16 [8192, 64, 64], P(('pair', 'aux')), may hold values from -0.75 to 0.75
- pno_density: bfloat16 [8192, 64, 64], P(('pair', 'aux')), may hold values from -6 to 6
- pno_coef: bfloat16 [8192, 256, 64], P(('pair', 'aux')), may hold values from -0.75 to 0.75
- pao_blocks: int32 [8192, 2], P(('pair', 'aux')), may hold values from 0 to 5, all different within a row
- aux_slice: int32 [8192, 2], P(('pair', 'aux')), may hold values from 0 to 15, all different within a row; in each aligned block of 16 rows (0 to 15, 16 to 31, ...) at most 4 rows name the same one
- aux_offset: int32 [8192, 2], P(('pair', 'aux')), may hold values from 0 to 3
Outputs:
- aux_density: float32 [8192, 768], P('aux', 'pair')
- virtual_density: float32 [768, 768], P('aux', 'pair')
Inputs may be any that keep to these rules, and one draw needn't show every extreme that they name: `pao_blocks`: the 2 blocks of a pair are different. `aux_slice`: the 2 slices of a pair are different; among the pairs of one device no slice is named more than 4 times, and in every draw some device names some slice exactly 4 times.
All inputs are finite; a program needn't handle non-finite values.
Results may differ from a plain program's by a relative error of at most 0.0041.
Values may be sent and summed in bfloat16 or wider, within the bound.
No kernel may reach another device: no remote copies, remote signals or barrier semaphores. Data moves between devices by JAX's collectives and lax.ppermute only.
A program may use at most 64 MiB of HBM per device.

v0:
```python
import math

import jax
import jax.numpy as jnp
from jax import lax
from jax.sharding import PartitionSpec as P

NBLK = 6
ABPO = 4


def split_up(array, dim, length):
    before, after = (array.shape[:dim], array.shape[dim + 1 :])
    return jnp.moveaxis(array.reshape(*before, length, -1, *after), dim, 0)


def sum_at_owner(array, axis, dim):
    blocks = split_up(array, dim, lax.axis_size(axis))
    arrived = lax.all_to_all(blocks, axis, split_axis=0, concat_axis=0, tiled=True)
    return arrived.sum(axis=0)


def on_device(integrals, amplitudes, pno_density, pno_coef, pao_blocks, aux_slice, aux_offset):
    n_pair = lax.axis_size("pair")
    n_aux = lax.axis_size("aux")
    pair_count, domain_rows, pno_rank = pno_coef.shape
    aux_dom = aux_slice.shape[1]
    pao_dom = pao_blocks.shape[1]
    pao_block = domain_rows // pao_dom
    aux_block = integrals.shape[1] // aux_dom
    ao_count = NBLK * pao_block
    capacity = max(2, 2 * pair_count * aux_dom // n_aux)
    out_scale = 1.0 / math.sqrt(pair_count * n_pair)
    slot_count = pair_count * aux_dom
    three_index = jnp.einsum(
        "pqr,prs->pqs", integrals, amplitudes, preferred_element_type=jnp.float32
    ).astype(jnp.bfloat16)
    owners = aux_slice.reshape(slot_count)
    owner_hot = (owners[:, None] == jnp.arange(n_aux, dtype=jnp.int32)[None, :]).astype(jnp.int32)
    before = jnp.cumsum(owner_hot, 0) - owner_hot
    slot_rank = jnp.sum(before * owner_hot, 1)
    target = owners * capacity + slot_rank
    routing = jnp.arange(n_aux * capacity, dtype=jnp.int32)[:, None] == target[None, :]
    labels = (
        jnp.concatenate(
            [aux_offset.reshape(slot_count, 1), jnp.repeat(pao_blocks, aux_dom, axis=0)], 1
        )
        + 1
    )
    label_buffer = (jnp.dot(routing.astype(jnp.int32), labels) - 1).reshape(
        n_aux, capacity, 1 + pao_dom
    )
    routing_bf = routing.astype(jnp.bfloat16)
    index_flat = three_index.reshape(slot_count, aux_block * pno_rank)
    index_buffer = jnp.dot(routing_bf, index_flat, preferred_element_type=jnp.float32).astype(
        jnp.bfloat16
    )
    index_buffer = index_buffer.reshape(n_aux, capacity, aux_block, pno_rank)
    pair_routing = (
        routing.reshape(n_aux * capacity, pair_count, aux_dom).sum(-1).astype(jnp.bfloat16)
    )
    coef_flat = pno_coef.reshape(pair_count, domain_rows * pno_rank)
    coef_buffer = jnp.dot(pair_routing, coef_flat, preferred_element_type=jnp.float32).astype(
        jnp.bfloat16
    )
    coef_buffer = coef_buffer.reshape(n_aux, capacity, domain_rows, pno_rank)
    index_part = lax.all_to_all(index_buffer, "aux", split_axis=0, concat_axis=0, tiled=True)
    coef_part = lax.all_to_all(coef_buffer, "aux", split_axis=0, concat_axis=0, tiled=True)
    label_part = lax.all_to_all(label_buffer, "aux", split_axis=0, concat_axis=0, tiled=True)
    back = jnp.einsum(
        "ncxr,ncyr->ncxy", index_part, coef_part, preferred_element_type=jnp.float32
    ).astype(jnp.bfloat16)
    got_labels = label_part
    received_count = n_aux * capacity
    pieces = back.reshape(received_count, aux_block, pao_dom, pao_block)
    got_labels = got_labels.reshape(received_count, 1 + pao_dom)
    offset_hot = got_labels[:, 0:1] == jnp.arange(ABPO, dtype=jnp.int32)[None, :]
    column_hot = got_labels[:, 1:, None] == jnp.arange(NBLK, dtype=jnp.int32)[None, None, :]
    placement = (offset_hot[:, None, :, None] & column_hot[:, :, None, :]).astype(jnp.bfloat16)
    gamma_part = jnp.einsum(
        "sxhy,shok->oxky", pieces, placement, preferred_element_type=jnp.float32
    )
    gamma_part = gamma_part.reshape(ABPO * aux_block, ao_count)
    aux_density = lax.psum_scatter(gamma_part, "pair", scatter_dimension=1, tiled=True) * out_scale
    weighted = jnp.einsum(
        "pyr,prs->pys", pno_coef, pno_density, preferred_element_type=jnp.float32
    ).astype(jnp.bfloat16)
    block_hot = (pao_blocks[:, :, None] == jnp.arange(NBLK, dtype=jnp.int32)[None, None, :]).astype(
        jnp.bfloat16
    )
    weighted_rows = jnp.einsum(
        "pak,paxr->kxpr",
        block_hot,
        weighted.reshape(pair_count, pao_dom, pao_block, pno_rank),
        preferred_element_type=jnp.float32,
    ).astype(jnp.bfloat16)
    weighted_rows = weighted_rows.reshape(ao_count, pair_count * pno_rank)
    coef_rows = jnp.einsum(
        "pak,paxr->kxpr",
        block_hot,
        pno_coef.reshape(pair_count, pao_dom, pao_block, pno_rank),
        preferred_element_type=jnp.float32,
    ).astype(jnp.bfloat16)
    coef_rows = coef_rows.reshape(ao_count, pair_count * pno_rank)
    virt_part = lax.dot_general(
        weighted_rows, coef_rows, (((1,), (1,)), ((), ())), preferred_element_type=jnp.float32
    )
    row_owned = sum_at_owner(virt_part, "aux", 0)
    virtual_density = sum_at_owner(row_owned, "pair", 1)
    return (aux_density, virtual_density * out_scale)


def solution(mesh):
    in_specs = (
        P(("pair", "aux"), None, None),
        P(("pair", "aux"), None, None),
        P(("pair", "aux"), None, None),
        P(("pair", "aux"), None, None),
        P(("pair", "aux"), None),
        P(("pair", "aux"), None),
        P(("pair", "aux"), None),
    )
    out_specs = (P("aux", "pair"), P("aux", "pair"))
    return jax.shard_map(
        on_device, mesh=mesh, in_specs=in_specs, out_specs=out_specs, check_vma=False
    )
```

profile of v0, /device:TPU:1, one launch (start us, length us, event | category | flops | bytes accessed | tf_op | source)
XLA Modules:
  0.0 343.5 jit_solution(4236853298096751434)
XLA Ops:
  7.2 0.8 copy.74
  8.2 0.2 select_reduce_fusion
  8.4 0.8 broadcast_in_dim.2
  9.3 0.8 copy.75
  10.1 0.1 convolution_add_fusion
  10.4 0.6 copy.76
  11.0 15.7 %all-to-all-start = ((s32[16,4,3]{1,2,0:T(4,128)}), s32[16,4,3]{1,2,0:T(4,128)S(1)}, u32[]{:S(2)}, u32[]{:S(2)}) async-start(s32[16,4,3]{1,2,0:T(4,128)} %copy.76), calls=%async_computation | async-start | bytes 65536 | tf_op jit(solution)/shard_map/all_to_all | solution.py:69
  26.8 1.3 convolution_convert_fusion.5
  28.1 0.5 copy.79
  28.5 0.8 reshape.103
  29.4 1.4 convolution_convert_fusion.1
  30.8 3.3 reshape.104
  34.1 1.6 copy.80
  35.7 2.5 all-to-all-done
  38.2 9.0 %all-to-all-start.1 = ((bf16[16,4,128,64]{2,3,1,0:T(8,128)(2,1)}), bf16[16,4,128,64]{2,3,1,0:T(8,128)(2,1)}, u32[]{:S(2)}, u32[]{:S(2)}) async-start(bf16[16,4,128,64]{2,3,1,0:T(8,128)(2,1)} %copy.80), calls=%async_computation.1 | async-start | bytes 2097152 | tf_op jit(solution)/shard_map/all_to_all | solution.py:67
  47.4 0.5 copy.82
  47.9 1.6 reshape.105
  49.6 1.8 convolution_convert_fusion
  51.4 5.5 %reshape.106 = bf16[16,4,256,64]{3,2,1,0:T(8,128)(2,1)} reshape(bf16[64,16384]{1,0:T(8,128)(2,1)S(1)} %convolution_convert_fusion) | data formatting | bytes 4194304 | tf_op jit(solution)/shard_map/reshape | solution.py:66
  56.9 4.8 %copy.83 = bf16[16,4,256,64]{2,3,1,0:T(8,128)(2,1)} copy(bf16[16,4,256,64]{3,2,1,0:T(8,128)(2,1)} %reshape.106) | data formatting | bytes 4194304 | tf_op jit(solution)/shard_map/reshape | solution.py:66
  61.7 29.9 %all-to-all-done.1 = bf16[16,4,128,64]{2,3,1,0:T(8,128)(2,1)} async-done(((bf16[16,4,128,64]{2,3,1,0:T(8,128)(2,1)}), bf16[16,4,128,64]{2,3,1,0:T(8,128)(2,1)}, u32[]{:S(2)}, u32[]{:S(2)}) %all-to-all-start.1) | async-done | bytes 1048608 | tf_op jit(solution)/shard_map/all_to_all | solution.py:67
  91.6 13.7 %all-to-all-start.2 = ((bf16[16,4,256,64]{2,3,1,0:T(8,128)(2,1)}), bf16[16,4,256,64]{2,3,1,0:T(8,128)(2,1)S(1)}, u32[]{:S(2)}, u32[]{:S(2)}) async-start(bf16[16,4,256,64]{2,3,1,0:T(8,128)(2,1)} %copy.83), calls=%async_computation.2 | async-start | bytes 4194304 | tf_op jit(solution)/shard_map/all_to_all | solution.py:68
  105.4 0.9 reshape.110
  106.3 1.2 convolution_convert_fusion.4
  107.5 1.2 reshape.109
  108.7 2.2 convert_bitcast_fusion
  110.8 4.5 %copy.88 = bf16[6,128,16,64]{3,2,1,0:T(8,128)(2,1)} copy(bf16[6,128,16,64]{1,0,3,2:T(8,128)(2,1)} %convert_bitcast_fusion) | data formatting | bytes 3145728 | tf_op jit(solution)/shard_map/convert_element_type | solution.py:96
  115.3 5.4 %dot_general.40 = bf16[16,48,1024]{2,1,0:T(8,128)(2,1)} reshape(bf16[6,128,16,64]{3,2,1,0:T(8,128)(2,1)} %copy.88) | data formatting | bytes 3145728 | tf_op jit(solution)/shard_map/dot_general | solution.py:105
  120.8 1.3 convolution_convert_fusion.3
  122.2 2.8 fusion.3
  125.0 72.1 %all-to-all-done.2 = bf16[16,4,256,64]{2,3,1,0:T(8,128)(2,1)S(1)} async-done(((bf16[16,4,256,64]{2,3,1,0:T(8,128)(2,1)}), bf16[16,4,256,64]{2,3,1,0:T(8,128)(2,1)S(1)}, u32[]{:S(2)}, u32[]{:S(2)}) %all-to-all-start.2) | async-done | bytes 2097184 | tf_op jit(solution)/shard_map/all_to_all | solution.py:68
  197.2 1.3 copy-done.1
  198.5 11.1 %all-to-all-start.3 = ((f32[16,48,768]{2,1,0:T(8,128)}), f32[16,48,768]{2,1,0:T(8,128)S(1)}, u32[]{:S(2)}, u32[]{:S(2)}) async-start(f32[16,48,768]{2,1,0:T(8,128)} %fusion.3), calls=%async_computation.4 | async-start | bytes 4718592 | tf_op jit(solution)/shard_map/all_to_all | solution.py:19
  209.7 0.3 reduce-scatter.2.cloned.1.call-start
  210.1 5.1 %convolution_convert_fusion.2 = bf16[16,4,128,256]{3,2,1,0:T(8,128)(2,1)} fusion(bf16[16,4,128,64]{2,3,1,0:T(8,128)(2,1)} %all-to-all-done.1, bf16[16,4,256,64]{2,3,1,0:T(8,128)(2,1)} %copy-done.1), kind=kOutput, calls=%fused_computation.5 | convolution fusion | flops 270532608 | bytes 7340032 | tf_op jit(solution)/shard_map/ncxr,ncyr->ncxy/dot_general | solution.py:70
  215.2 6.9 %reshape.107 = bf16[64,128,2,128]{3,2,1,0:T(2,128)(2,1)} reshape(bf16[16,4,128,256]{3,2,1,0:T(8,128)(2,1)} %convolution_convert_fusion.2) | data formatting | bytes 8388608 | tf_op jit(solution)/shard_map/reshape | solution.py:75
  222.2 6.9 %fusion = f32[4,6,128,128,1]{3,1,4,2,0:T(8,128)S(1)} fusion(bf16[64,128,2,128]{3,2,1,0:T(2,128)(2,1)} %reshape.107, pred[64,2,6]{0,2,1:T(8,128)(4,1)S(1)} %iota_compare_fusion.8, pred[64,4]{0,1:T(4,128)(4,1)S(1)} %iota_compare_fusion.9), kind=kOutput, calls=%fused_computation.2 | convolution fusion | flops 100666368 | bytes 5768192 | tf_op jit(solution)/shard_map/sxhy,shok->oxky/dot_general | solution.py:80
  229.0 1.5 copy.110
  230.5 3.0 copy.97
  233.6 79.2 %all-to-all-done.3 = f32[16,48,768]{2,1,0:T(8,128)S(1)} async-done(((f32[16,48,768]{2,1,0:T(8,128)}), f32[16,48,768]{2,1,0:T(8,128)S(1)}, u32[]{:S(2)}, u32[]{:S(2)}) %all-to-all-start.3) | async-done | bytes 2359328 | tf_op jit(solution)/shard_map/all_to_all | solution.py:19
  312.9 0.2 copy.90
  313.1 0.4 reshape.119
  313.5 19.4 %all_to_all.25 = f32[32,1,1152]{2,1,0:T(1,128)S(1)} all-to-all(f32[32,1,1152]{2,1,0:T(1,128)S(1)} %reshape.119), channel_id=1, replica_groups=mesh['pair'=32,'aux'=16] {'pair'}, dimensions={0} | all-to-all | bytes 294912 | tf_op jit(solution)/shard_map/all_to_all | solution.py:19
  332.9 0.5 broadcast.40
  333.4 1.0 reduce
  334.4 0.2 reshape.120
  334.6 0.6 broadcast_multiply_fusion.1
  335.2 1.4 broadcast_multiply_fusion
  (37 shorter events, 1.3 us)
Async XLA Ops:
  7.2 19.6 %copy-start = (bf16[16,256,64]{1,2,0:T(8,128)(2,1)S(1)}, bf16[16,256,64]{1,2,0:T(8,128)(2,1)}, u32[]{:S(2)}) copy-start(bf16[16,256,64]{1,2,0:T(8,128)(2,1)} %param.7) | copy-start | bytes 1572868
  11.0 27.2 %all-to-all-start = ((s32[16,4,3]{1,2,0:T(4,128)}), s32[16,4,3]{1,2,0:T(4,128)S(1)}, u32[]{:S(2)}, u32[]{:S(2)}) async-start(s32[16,4,3]{1,2,0:T(4,128)} %copy.76), calls=%async_computation | async-start | bytes 65536 | tf_op jit(solution)/shard_map/all_to_all | solution.py:69
  34.0 13.4 %copy-start.2 = (bf16[16,256,64]{1,2,0:T(8,128)(2,1)S(1)}, bf16[16,256,64]{1,2,0:T(8,128)(2,1)}, u32[]{:S(2)}) copy-start(bf16[16,256,64]{1,2,0:T(8,128)(2,1)} %param.10) | copy-start | bytes 1572868
  38.2 53.4 %all-to-all-start.1 = ((bf16[16,4,128,64]{2,3,1,0:T(8,128)(2,1)}), bf16[16,4,128,64]{2,3,1,0:T(8,128)(2,1)}, u32[]{:S(2)}, u32[]{:S(2)}) async-start(bf16[16,4,128,64]{2,3,1,0:T(8,128)(2,1)} %copy.80), calls=%async_computation.1 | async-start | bytes 2097152 | tf_op jit(solution)/shard_map/all_to_all | solution.py:67
  47.2 2.3 copy-start.6
  61.7 43.6 %copy-start.7 = (s32[16,2]{0,1:T(2,128)S(1)}, s32[16,2]{0,1:T(2,128)}, u32[]{:S(2)}) copy-start(s32[16,2]{0,1:T(2,128)} %param.11) | copy-start | bytes 388
  61.7 44.7 %copy-start.5 = (bf16[16,64,64]{2,1,0:T(8,128)(2,1)S(1)}, bf16[16,64,64]{2,1,0:T(8,128)(2,1)}, u32[]{:S(2)}) copy-start(bf16[16,64,64]{2,1,0:T(8,128)(2,1)} %param.9) | copy-start | bytes 393220
  91.6 105.6 %all-to-all-start.2 = ((bf16[16,4,256,64]{2,3,1,0:T(8,128)(2,1)}), bf16[16,4,256,64]{2,3,1,0:T(8,128)(2,1)S(1)}, u32[]{:S(2)}, u32[]{:S(2)}) async-start(bf16[16,4,256,64]{2,3,1,0:T(8,128)(2,1)} %copy.83), calls=%async_computation.2 | async-start | bytes 4194304 | tf_op jit(solution)/shard_map/all_to_all | solution.py:68
  115.3 5.4 %copy-start.3 = (bf16[16,2,128,64]{2,1,3,0:T(2,128)(2,1)S(1)}, bf16[16,2,128,64]{2,1,3,0:T(2,128)(2,1)}, u32[]{:S(2)}) copy-start(bf16[16,2,128,64]{2,1,3,0:T(2,128)(2,1)} %reshape.110) | copy-start | bytes 1572868
  120.8 1.4 copy-start.4
  197.2 1.3 copy-start.1
  198.5 114.3 %all-to-all-start.3 = ((f32[16,48,768]{2,1,0:T(8,128)}), f32[16,48,768]{2,1,0:T(8,128)S(1)}, u32[]{:S(2)}, u32[]{:S(2)}) async-start(f32[16,48,768]{2,1,0:T(8,128)} %fusion.3), calls=%async_computation.4 | async-start | bytes 4718592 | tf_op jit(solution)/shard_map/all_to_all | solution.py:19
  209.7 125.6 %reduce-scatter.2.cloned.1.call-start = ((), (), s32[]{:S(2)}) async-start(), calls=%async_computation.6 | async-start | bytes 1622016 | tf_op jit(solution)/shard_map/reduce_scatter | solution.py:84
Sparse Core Ops, SparseCore 0:
  233.7 101.3 reduce-scatter.1
where the time goes:
time: 345 us; the launch traced here: 343 us
  waiting for transfers between devices  184 us (53%)
  starting transfers between devices  49.9 us (14%)
  local copies, waits for them, and re-layouts  48.4 us (14%)
  matrix products  24.1 us (7%)
  blocking collectives  19.4 us (6%)
  between operations  14.3 us (4%)
  other arithmetic  3.59 us (1%)
    all_to_all x1, waiting for transfers between devices, sum_at_owner(): lax.all_to_all(blocks, axis, split_axis=0, concat_axis=0, tiled=True)  79.2 us
    all_to_all x1, waiting for transfers between devices, on_device(): lax.all_to_all(coef_buffer, 'aux', split_axis=0, concat_axis=0, tiled=True)  72.1 us
    all_to_all x1, waiting for transfers between devices, on_device(): lax.all_to_all(index_buffer, 'aux', split_axis=0, concat_axis=0, tiled=True)  29.9 us
    all_to_all x1, blocking collectives, sum_at_owner(): lax.all_to_all(blocks, axis, split_axis=0, concat_axis=0, tiled=True)  19.4 us
    all_to_all x1, starting transfers between devices, on_device(): lax.all_to_all(label_buffer, 'aux', split_axis=0, concat_axis=0, tiled=True)  15.7 us
    all_to_all x1, starting transfers between devices, on_device(): lax.all_to_all(coef_buffer, 'aux', split_axis=0, concat_axis=0, tiled=True)  13.7 us
    all_to_all x1, starting transfers between devices, sum_at_owner(): lax.all_to_all(blocks, axis, split_axis=0, concat_axis=0, tiled=True)  11.1 us
    reshape x2, local copies, waits for them, and re-layouts, on_device(): coef_buffer = coef_buffer.reshape(n_aux, capacity, domain_rows, pno_rank)  10.3 us
  transfers between devices with their start and end apart: 5, of which 4 were waited for; matrix products, arithmetic and copies ran while one was open for 20% of the time, Pallas kernels for 0%

commit v1 on v0

v1 whole, which is shorter than its diff:
```python
import math

import jax
import jax.numpy as jnp
from jax import lax
from jax.experimental import pallas as pl
from jax.experimental.pallas import tpu as pltpu
from jax.sharding import Mesh
from jax.sharding import PartitionSpec as P

NBLK = 6
ABPO = 4
BF = jnp.bfloat16
F32 = jnp.float32
PAIRS = 16
GROUP = 64
ROWS1 = 208
ROWS2 = 120
ROWS3 = 24
VMEM = pltpu.CompilerParams(vmem_limit_bytes=56 * 1024 * 1024)


def dot00(a, b):
    return lax.dot_general(a, b, (((0,), (0,)), ((), ())), preferred_element_type=F32)


def dot10(a, b):
    return lax.dot_general(a, b, (((1,), (0,)), ((), ())), preferred_element_type=F32)


def local_kernel(
    blocks, owners, offsets, ints, amps, dens, coef, out, pieces, weighted_rows, coef_rows, virt
):
    weighted_rows[...] = jnp.zeros(weighted_rows.shape, BF)
    coef_rows[...] = jnp.zeros(coef_rows.shape, BF)
    lane = lax.broadcasted_iota(jnp.int32, (1, 128), 1) % 64
    slice_row = jnp.zeros((1, 128), F32)
    block_row = jnp.zeros((1, 128), F32)
    offset_row = jnp.zeros((1, 128), F32)
    for p in range(PAIRS):
        c = coef[p]
        weighted = dot00(dens[p], c).astype(BF)
        three_index = dot00(amps[p], ints[p]).astype(BF)
        piece = dot00(c, three_index)
        for h in range(2):
            at = pl.ds(pl.multiple_of(blocks[h, p] * 128, 128), 128)
            weighted_rows[64 * p : 64 * p + 64, at] = weighted[:, 128 * h : 128 * h + 128]
            coef_rows[64 * p : 64 * p + 64, at] = c[:, 128 * h : 128 * h + 128]
            for k in range(2):
                slot = 4 * p + 2 * h + k
                pieces[pl.ds(slot, 128, 64), :] = piece[
                    128 * h : 128 * h + 128, 128 * k : 128 * k + 128
                ]
                here = lane == slot
                slice_row = jnp.where(here, owners[k, p].astype(F32), slice_row)
                block_row = jnp.where(here, blocks[h, p].astype(F32), block_row)
                offset_row = jnp.where(here, offsets[k, p].astype(F32), offset_row)
    sub = lax.broadcasted_iota(jnp.int32, (8, 128), 0)
    labels = jnp.where(sub == 0, slice_row, jnp.where(sub == 1, block_row, offset_row))
    virt[...] = dot00(coef_rows[...], weighted_rows[...])
    for g in range(GROUP):
        out[g, 0:128, :] = pieces[128 * g : 128 * g + 128, :].astype(BF)
        first, half = 24 * (g // 2), 384 * (g % 2)
        tiles = [
            virt[first + 8 * i : first + 8 * i + 8, half + 128 * j : half + 128 * j + 128]
            for i in range(3)
            for j in range(3)
        ]
        out[g, 128:ROWS1, :] = jnp.concatenate(tiles + [labels], 0).astype(BF)


def place_kernel(got, out, hot, acc):
    lane = lax.broadcasted_iota(jnp.int32, (1, 128), 1)
    cell = lax.broadcasted_iota(jnp.int32, (384, 128), 0)
    for i in range(GROUP // 2):
        first = got[2 * i, 200:208, :].astype(F32)
        second = got[2 * i + 1, 200:208, :].astype(F32)
        both = jnp.where(lane < 64, first, second)
        target = both[0:1] * 24.0 + both[1:2] * 4.0 + both[2:3]
        hot[:, 128 * i : 128 * i + 128] = (cell == target.astype(jnp.int32)).astype(BF)
    data = jnp.concatenate(
        [got[:, 0:64, :].reshape(4096, 128), got[:, 64:128, :].reshape(4096, 128)], 1
    )
    acc[...] = dot10(hot[...], data)
    total = got[0, 128:200, :].astype(F32)
    for g in range(1, GROUP):
        total = total + got[g, 128:200, :].astype(F32)
    lanes8 = lax.broadcasted_iota(jnp.int32, (8, 128), 1)
    windows = [[], [], [], []]
    for i in range(3):
        a, b, c = (total[24 * i + 8 * j : 24 * i + 8 * j + 8] for j in range(3))
        windows[0].append(a)
        windows[1].append(jnp.where(lanes8 < 32, pltpu.roll(a, 32, 1), pltpu.roll(b, 32, 1)))
        windows[2].append(jnp.where(lanes8 < 64, pltpu.roll(b, 64, 1), pltpu.roll(c, 64, 1)))
        windows[3].append(pltpu.roll(c, 96, 1))
    for z in range(8):
        rows = [acc[48 * z : 48 * z + 48, 0:128], acc[48 * z : 48 * z + 48, 128:256]]
        out[z] = jnp.concatenate(rows + windows[z % 4], 0).astype(BF)


def column_kernel(place, got, out):
    total = got[0].astype(F32)
    for z in range(1, 8):
        total = total + got[z].astype(F32)
    sub = lax.broadcasted_iota(jnp.int32, (8, 128), 0)
    lane = lax.broadcasted_iota(jnp.int32, (8, 128), 1)
    tiles = []
    for i in range(6):
        a, b = total[8 * i : 8 * i + 8], total[48 + 8 * i : 56 + 8 * i]
        tiles.append(jnp.where(sub < 4, a, pltpu.roll(b, 4, 0)))
        tiles.append(jnp.where(sub < 4, pltpu.roll(a, 4, 0), b))
    column = 2 * place[0]
    virt = [total[96:104], total[104:112], total[112:120]]
    for low in range(2):
        v0, v1, v2 = virt
        if low:
            v0, v1, v2 = (pltpu.roll(v, 80, 1) for v in virt)
        packed = [jnp.where(lane < 64, v0, pltpu.roll(v1, 64, 1)), v2]
        for p in range(32):
            b_first, b_last = (24 * p) // 128, (24 * p + 23) // 128
            tile = tiles[6 * low + b_first]
            if b_last != b_first:
                tile = jnp.where(column >= 24 * p - 128 * b_first, tile, tiles[6 * low + b_last])
            out[2 * p + low] = jnp.concatenate([tile] + packed, 0).astype(BF)


def final_kernel(place, got, aux_out, virt_out, *, scale):
    p = place[0]
    for j in range(12):
        tile = got[lax.rem(12 * p + j, 64), 0:8, :].astype(F32) * scale
        for y in range(2):
            for o in range(ABPO):
                aux_out[2 * j + y : 2 * j + y + 1, 128 * o : 128 * o + 128] = tile[
                    4 * y + o : 4 * y + o + 1
                ]
    both = got[2 * p + place[1], 8:24, :].astype(F32) * scale
    virt_out[0:8, :] = both[0:8, 0:48]
    virt_out[8:16, :] = pltpu.roll(both[0:8], 64, 1)[:, 0:48]
    virt_out[16:24, :] = both[8:16, 0:48]


def call(body, ins, outs, scalars, scratch=()):
    smem = pl.BlockSpec(memory_space=pltpu.SMEM)
    vmem = pl.BlockSpec(memory_space=pltpu.VMEM)
    return pl.pallas_call(
        body,
        in_specs=[smem] * len(scalars) + [vmem] * len(ins),
        out_specs=[vmem] * len(outs),
        out_shape=outs,
        scratch_shapes=scratch,
        compiler_params=VMEM,
    )(*scalars, *ins)


def on_device(integrals, amplitudes, pno_density, pno_coef, pao_blocks, aux_slice, aux_offset):
    pair = lax.axis_index("pair")
    low = lax.axis_index("low")
    high = lax.axis_index("high")
    scale = 1.0 / math.sqrt(PAIRS * 32)
    sds = jax.ShapeDtypeStruct
    (sent,) = call(
        local_kernel,
        [
            jnp.swapaxes(integrals, 1, 2),
            amplitudes,
            pno_density,
            jnp.swapaxes(pno_coef, 1, 2),
        ],
        [sds((GROUP, ROWS1, 128), BF)],
        [pao_blocks.T, aux_slice.T, aux_offset.T],
        [
            pltpu.VMEM((8192, 128), F32),
            pltpu.VMEM((1024, 768), BF),
            pltpu.VMEM((1024, 768), BF),
            pltpu.VMEM((768, 768), F32),
        ],
    )
    got = lax.all_to_all(sent, ("pair", "low"), split_axis=0, concat_axis=0, tiled=True)
    (sent,) = call(
        place_kernel,
        [got],
        [sds((8, ROWS2, 128), BF)],
        [],
        [pltpu.VMEM((384, 4096), BF), pltpu.VMEM((384, 256), F32)],
    )
    got = lax.all_to_all(sent, "high", split_axis=0, concat_axis=0, tiled=True)
    (sent,) = call(
        column_kernel, [got], [sds((GROUP, ROWS3, 128), BF)], [(2 * pair + low).reshape(1)]
    )
    got = lax.all_to_all(sent, ("pair", "low"), split_axis=0, concat_axis=0, tiled=True)
    aux, virt = call(
        lambda *refs: final_kernel(*refs, scale=scale),
        [got],
        [sds((24, 512), F32), sds((24, 48), F32)],
        [jnp.stack([pair, high // 4]).astype(jnp.int32)],
    )
    return aux.T, virt.T


def solution(mesh):
    split = Mesh(mesh.devices.reshape(32, 8, 2), ("pair", "high", "low"))
    every = ("pair", "high", "low")
    in_specs = (P(every, None, None),) * 4 + (P(every, None),) * 3
    out_specs = (P(("high", "low"), "pair"),) * 2
    return jax.shard_map(
        on_device, mesh=split, in_specs=in_specs, out_specs=out_specs, check_vma=False
    )
```

time: 345 us -> 122 us (0.35)
  waiting for transfers between devices: 184 us -> 25.9 us
  local copies, waits for them, and re-layouts: 48.4 us -> 1.45 us
  blocking collectives: 19.4 us -> 54.4 us
  starting transfers between devices: 49.9 us -> 22.6 us
  matrix products: 24.1 us -> 0 us
  Pallas kernels: 0 us -> 16.3 us
  between operations: 14.3 us -> 0.66 us
    all_to_all x4 -> x2, waiting for transfers between devices: 184 us -> 25.9 us  [the longest x1 15.6 us: on_device(): got = lax.all_to_all(sent, 'high', split_axis=0, concat_axis=0, tiled=True)]
    all_to_all x1, blocking collectives: 19.4 us -> 54.4 us  [on_device(): lax.all_to_all(sent, ('pair', 'low'), split_axis=0, concat_axis=0, tiled=...]
    reshape x16 -> x0, local copies, waits for them, and re-layouts: 30.8 us -> none  [the longest x2 10.3 us: on_device(): coef_buffer = coef_buffer.reshape(n_aux, capacity, domain_rows, pno_rank)]
    all_to_all x4 -> x2, starting transfers between devices: 49.6 us -> 22.6 us  [the longest x1 12.4 us: on_device(): got = lax.all_to_all(sent, 'high', split_axis=0, concat_axis=0, tiled=True)]
    dot_general x10 -> x0, matrix products: 24.1 us -> none  [the longest x1 6.85 us: on_device(): jnp.einsum('sxhy,shok->oxky', pieces, placement, preferred_element_type=j...]
    pallas_call x0 -> x4, Pallas kernels: none -> 16.3 us  [call(): pl.pallas_call(body, in_specs=[smem] * len(scalars) + [vmem] * len(ins),...]
    dot_general x1 -> x0, local copies, waits for them, and re-layouts: 5.44 us -> none  [on_device(): lax.dot_general(weighted_rows, coef_rows, (((1,), (1,)), ((), ())), prefe...]
    convert_element_type x2 -> x0, local copies, waits for them, and re-layouts: 4.97 us -> none  [the longest x1 4.49 us: on_device(): weighted_rows = jnp.einsum('pak,paxr->kxpr', block_hot, weighted.reshape(...]
  transfers between devices with their start and end apart: 5 -> 2, of which waited for: 4 -> 2; matrix products, arithmetic and copies ran while one was open for 20% -> 1% of each run, Pallas kernels for 0% -> 0%
where the time goes in v1:
time: 122 us
  blocking collectives  54.4 us (45%)
  waiting for transfers between devices  25.9 us (21%)
  starting transfers between devices  22.6 us (19%)
  Pallas kernels  16.3 us (13%)
  local copies, waits for them, and re-layouts  1.45 us (1%)
    all_to_all x1, blocking collectives, on_device(): lax.all_to_all(sent, ('pair', 'low'), split_axis=0, concat_axis=0, tiled=...  54.4 us
    pallas_call x4, Pallas kernels, call(): pl.pallas_call(body, in_specs=[smem] * len(scalars) + [vmem] * len(ins),...  16.3 us
    all_to_all x1, waiting for transfers between devices, on_device(): got = lax.all_to_all(sent, 'high', split_axis=0, concat_axis=0, tiled=True)  15.6 us
    all_to_all x1, starting transfers between devices, on_device(): got = lax.all_to_all(sent, 'high', split_axis=0, concat_axis=0, tiled=True)  12.4 us
    all_to_all x1, waiting for transfers between devices, on_device(): lax.all_to_all(sent, ('pair', 'low'), split_axis=0, concat_axis=0, tiled=...  10.3 us
    all_to_all x1, starting transfers between devices, on_device(): lax.all_to_all(sent, ('pair', 'low'), split_axis=0, concat_axis=0, tiled=...  10.2 us
  transfers between devices with their start and end apart: 2, of which 2 were waited for; matrix products, arithmetic and copies ran while one was open for 1% of the time, Pallas kernels for 0%

profile of v1, /device:TPU:1, one launch (start us, length us, event | category | flops | bytes accessed | tf_op | source)
XLA Modules:
  0.0 122.0 jit_solution(10549244159419578923)
XLA Ops:
  0.6 8.7 %shard_map.86 = bf16[64,208,128]{2,1,0:T(8,128)(2,1)} custom-call(s32[2,16]{1,0:T(2,128)} %bitcast.12, s32[2,16]{1,0:T(2,128)} %bitcast.13, s32[2,16]{1,0:T(2,128)} %bitcast.14, bf16[16,64,256]{2,1,0:T(8,128)(2,1)} %bitcast.10, bf16[16,64,64]{2,1,0:T(8,128)(2,1)} %amps.1, bf16[16,64,64]{2,1,0:T(8,128)(2,1)} %dens.1, bf16[16,64,256]{2,1,0:T(8,128)(2,1)} %bitcast.11), custom_call_target="tpu_custom_call" | custom-call | tf_op jit(solution)/shard_map/pallas_call | solution.py:145
  9.4 54.4 %all_to_all.15.got = bf16[64,208,128]{2,1,0:T(8,128)(2,1)} all-to-all(bf16[64,208,128]{2,1,0:T(8,128)(2,1)} %shard_map.86), channel_id=1, replica_groups=mesh['pair'=32,'high'=8,'low'=2] {'pair','low'}, dimensions={0} | all-to-all | bytes 6815744 | tf_op jit(solution)/shard_map/all_to_all | solution.py:178
  63.8 4.0 %shard_map.87 = bf16[8,120,128]{2,1,0:T(8,128)(2,1)} custom-call(bf16[64,208,128]{2,1,0:T(8,128)(2,1)} %all_to_all.15.got), custom_call_target="tpu_custom_call" | custom-call | tf_op jit(solution)/shard_map/pallas_call | solution.py:145
  67.8 12.4 %all-to-all-start.1 = ((bf16[8,120,128]{2,1,0:T(8,128)(2,1)}), bf16[8,120,128]{2,1,0:T(8,128)(2,1)S(1)}, u32[]{:S(2)}, u32[]{:S(2)}) async-start(bf16[8,120,128]{2,1,0:T(8,128)(2,1)} %shard_map.87), calls=%async_computation.1 | async-start | bytes 491520 | tf_op jit(solution)/shard_map/all_to_all | solution.py:186
  80.2 15.6 %all-to-all-done.1.got = bf16[8,120,128]{2,1,0:T(8,128)(2,1)S(1)} async-done(((bf16[8,120,128]{2,1,0:T(8,128)(2,1)}), bf16[8,120,128]{2,1,0:T(8,128)(2,1)S(1)}, u32[]{:S(2)}, u32[]{:S(2)}) %all-to-all-start.1) | async-done | bytes 245792 | tf_op jit(solution)/shard_map/all_to_all | solution.py:186
  95.8 0.0 copy-start.1
  95.8 0.7 copy-done.1
  96.5 1.9 %shard_map.88 = bf16[64,24,128]{2,1,0:T(8,128)(2,1)} custom-call(s32[1]{0:T(128)} %bitcast.2.place, bf16[8,120,128]{2,1,0:T(8,128)(2,1)} %copy-done.1), custom_call_target="tpu_custom_call" | custom-call | tf_op jit(solution)/shard_map/pallas_call | solution.py:145
  98.3 10.2 %all-to-all-start.2 = ((bf16[64,24,128]{2,1,0:T(8,128)(2,1)}), bf16[64,24,128]{2,1,0:T(8,128)(2,1)S(1)}, u32[]{:S(2)}, u32[]{:S(2)}) async-start(bf16[64,24,128]{2,1,0:T(8,128)(2,1)} %shard_map.88), calls=%async_computation.2 | async-start | bytes 786432 | tf_op jit(solution)/shard_map/all_to_all | solution.py:190
  108.6 0.6 pad_add_fusion.refs_0_
  109.2 10.3 %all-to-all-done.2.refs_1_ = bf16[64,24,128]{2,1,0:T(8,128)(2,1)S(1)} async-done(((bf16[64,24,128]{2,1,0:T(8,128)(2,1)}), bf16[64,24,128]{2,1,0:T(8,128)(2,1)S(1)}, u32[]{:S(2)}, u32[]{:S(2)}) %all-to-all-start.2) | async-done | bytes 393248 | tf_op jit(solution)/shard_map/all_to_all | solution.py:190
  119.5 0.0 copy-start
  119.5 0.8 copy-done
  120.3 1.7 %shard_map.89 = (f32[24,512]{1,0:T(8,128)}, f32[24,48]{1,0:T(8,128)}) custom-call(s32[2]{0:T(128)} %pad_add_fusion.refs_0_, bf16[64,24,128]{2,1,0:T(8,128)(2,1)} %copy-done), custom_call_target="tpu_custom_call" | custom-call | tf_op jit(solution)/shard_map/pallas_call | solution.py:145
Async XLA Ops:
  67.8 28.0 %all-to-all-start.1 = ((bf16[8,120,128]{2,1,0:T(8,128)(2,1)}), bf16[8,120,128]{2,1,0:T(8,128)(2,1)S(1)}, u32[]{:S(2)}, u32[]{:S(2)}) async-start(bf16[8,120,128]{2,1,0:T(8,128)(2,1)} %shard_map.87), calls=%async_computation.1 | async-start | bytes 491520 | tf_op jit(solution)/shard_map/all_to_all | solution.py:186
  95.8 0.7 copy-start.1
  98.3 21.2 %all-to-all-start.2 = ((bf16[64,24,128]{2,1,0:T(8,128)(2,1)}), bf16[64,24,128]{2,1,0:T(8,128)(2,1)S(1)}, u32[]{:S(2)}, u32[]{:S(2)}) async-start(bf16[64,24,128]{2,1,0:T(8,128)(2,1)} %shard_map.88), calls=%async_computation.2 | async-start | bytes 786432 | tf_op jit(solution)/shard_map/all_to_all | solution.py:190
  119.5 0.8 copy-start

commit v2 on v1

v2 whole, which is shorter than its diff:
```python
import math

import jax
import jax.numpy as jnp
from jax import lax
from jax.experimental import pallas as pl
from jax.experimental.pallas import tpu as pltpu
from jax.sharding import Mesh
from jax.sharding import PartitionSpec as P

NBLK = 6
ABPO = 4
BF = jnp.bfloat16
F32 = jnp.float32
PAIRS = 16
GROUP = 64
ROWS1 = 168
ROWS2 = 112
ROWS3 = 16
VMEM = pltpu.CompilerParams(vmem_limit_bytes=40 * 1024 * 1024)


def dot00(a, b):
    return lax.dot_general(a, b, (((0,), (0,)), ((), ())), preferred_element_type=F32)


def dot10(a, b):
    return lax.dot_general(a, b, (((1,), (0,)), ((), ())), preferred_element_type=F32)


def virtual_kernel(blocks, core, dens, coef, mine, other, weighted_rows, coef_rows):
    weighted_rows[...] = jnp.zeros(weighted_rows.shape, BF)
    coef_rows[...] = jnp.zeros(coef_rows.shape, BF)
    for p in range(PAIRS):
        c = coef[p]
        weighted = dot00(dens[p], c).astype(BF)
        for h in range(2):
            at = pl.ds(pl.multiple_of(blocks[h, p] * 128, 128), 128)
            weighted_rows[64 * p : 64 * p + 64, at] = weighted[:, 128 * h : 128 * h + 128]
            coef_rows[64 * p : 64 * p + 64, at] = c[:, 128 * h : 128 * h + 128]
    left = coef_rows[...]
    other_half = pl.ds(pl.multiple_of(384 * (1 - core[0]), 128), 384)
    other[...] = dot00(left, weighted_rows[:, other_half]).astype(BF)
    my_half = pl.ds(pl.multiple_of(384 * core[0], 128), 384)
    mine[...] = dot00(left, weighted_rows[:, my_half])


def piece_kernel(ints, amps, coef, out, pieces, rounded, sems):
    for p in range(PAIRS):
        three_index = dot00(amps[p], ints[p]).astype(BF)
        piece = dot00(coef[p], three_index)
        for h in range(2):
            for k in range(2):
                pieces[pl.ds(4 * p + 2 * h + k, 128, 64), :] = piece[
                    128 * h : 128 * h + 128, 128 * k : 128 * k + 128
                ]
    copies = []
    for i in range(8):
        for g in range(8 * i, 8 * i + 8):
            rounded[g] = pieces[128 * g : 128 * g + 128, :].astype(BF)
        copies.append(
            pltpu.make_async_copy(
                rounded.at[8 * i : 8 * i + 8], out.at[8 * i : 8 * i + 8, 0:128], sems.at[i]
            )
        )
        copies[-1].start()
    for copy in copies:
        copy.wait()


def rest_kernel(blocks, owners, offsets, filled, mine, other, out, rows, sem):
    lane = lax.broadcasted_iota(jnp.int32, (1, 128), 1) % 64
    slice_row = jnp.zeros((1, 128), F32)
    block_row = jnp.zeros((1, 128), F32)
    offset_row = jnp.zeros((1, 128), F32)
    for p in range(PAIRS):
        for h in range(2):
            for k in range(2):
                here = lane == 4 * p + 2 * h + k
                slice_row = jnp.where(here, owners[k, p].astype(F32), slice_row)
                block_row = jnp.where(here, blocks[h, p].astype(F32), block_row)
                offset_row = jnp.where(here, offsets[k, p].astype(F32), offset_row)
    sub = lax.broadcasted_iota(jnp.int32, (8, 128), 0)
    top = sub < 4
    labels = jnp.where(sub == 4, slice_row, jnp.where(sub == 5, block_row, offset_row))
    for i in range(GROUP // 2):
        both = mine[24 * i : 24 * i + 24, :] + other[24 * i : 24 * i + 24, :].astype(F32)
        first = [both[0:8, 128 * j : 128 * j + 128] for j in range(3)]
        mid = [both[8:16, 128 * j : 128 * j + 128] for j in range(3)]
        last = [both[16:24, 128 * j : 128 * j + 128] for j in range(3)]
        moved = [pltpu.roll(m, 4, 0) for m in mid]
        even = first + [jnp.where(top, mid[0], moved[1]), jnp.where(top, mid[2], labels)]
        odd = last + [jnp.where(top, moved[0], mid[1]), jnp.where(top, moved[2], labels)]
        rows[2 * i] = jnp.concatenate(even, 0).astype(BF)
        rows[2 * i + 1] = jnp.concatenate(odd, 0).astype(BF)
    copy = pltpu.make_async_copy(rows, out.at[:, 128:ROWS1], sem)
    copy.start()
    copy.wait()


def place_kernel(got, out, hot, acc):
    lane = lax.broadcasted_iota(jnp.int32, (1, 128), 1)
    cell = lax.broadcasted_iota(jnp.int32, (384, 128), 0)
    for i in range(GROUP // 2):
        first = got[2 * i, 160:168, :].astype(F32)
        second = got[2 * i + 1, 160:168, :].astype(F32)
        both = jnp.where(lane < 64, first, second)
        target = both[4:5] * 24.0 + both[5:6] * 4.0 + both[6:7]
        hot[:, 128 * i : 128 * i + 128] = (cell == target.astype(jnp.int32)).astype(BF)
    data = jnp.concatenate(
        [got[:, 0:64, :].reshape(4096, 128), got[:, 64:128, :].reshape(4096, 128)], 1
    )
    acc[...] = dot10(hot[...], data)
    lanes8 = lax.broadcasted_iota(jnp.int32, (8, 128), 1)
    for half in range(2):
        mine = [g for g in range(GROUP) if (g // 2) % 2 == half]
        total = got[mine[0], 128:168, :].astype(F32)
        for g in mine[1:]:
            total = total + got[g, 128:168, :].astype(F32)
        whole = [total[0:8], total[8:16], total[16:24]]
        part = [total[24:32], pltpu.roll(total[24:32], 4, 0), total[32:40]]
        for z in range(4):
            at = 4 * half + z
            rows = [acc[48 * at : 48 * at + 48, 0:128], acc[48 * at : 48 * at + 48, 128:256]]
            for a, b, c in (whole, part):
                if z == 0:
                    rows.append(a)
                elif z == 1:
                    rows.append(
                        jnp.where(lanes8 < 32, pltpu.roll(a, 32, 1), pltpu.roll(b, 32, 1))
                    )
                elif z == 2:
                    rows.append(
                        jnp.where(lanes8 < 64, pltpu.roll(b, 64, 1), pltpu.roll(c, 64, 1))
                    )
                else:
                    rows.append(pltpu.roll(c, 96, 1))
            out[at] = jnp.concatenate(rows, 0).astype(BF)


def column_kernel(place, got, out):
    total = got[0].astype(F32)
    for z in range(1, 8):
        total = total + got[z].astype(F32)
    sub = lax.broadcasted_iota(jnp.int32, (8, 128), 0)
    lane = lax.broadcasted_iota(jnp.int32, (8, 128), 1)
    tiles = []
    for i in range(6):
        a, b = total[8 * i : 8 * i + 8], total[48 + 8 * i : 56 + 8 * i]
        tiles.append(jnp.where(sub < 4, a, pltpu.roll(b, 4, 0)))
        tiles.append(jnp.where(sub < 4, pltpu.roll(a, 4, 0), b))
    column = 2 * place[0]
    whole, part = total[96:104], total[104:112]
    packed = [
        jnp.where(lane < 64, whole, pltpu.roll(part, 64, 1)),
        jnp.where(lane < 64, pltpu.roll(whole, 80, 1), pltpu.roll(part, 16, 1)),
    ]
    for low in range(2):
        for p in range(32):
            b_first, b_last = (24 * p) // 128, (24 * p + 23) // 128
            tile = tiles[6 * low + b_first]
            if b_last != b_first:
                tile = jnp.where(column >= 24 * p - 128 * b_first, tile, tiles[6 * low + b_last])
            out[2 * p + low] = jnp.concatenate([tile, packed[low]], 0).astype(BF)


def final_kernel(place, got, aux_out, virt_out, *, scale):
    p = place[0]
    for j in range(12):
        tile = got[lax.rem(12 * p + j, 64), 0:8, :].astype(F32) * scale
        for y in range(2):
            for o in range(ABPO):
                aux_out[2 * j + y : 2 * j + y + 1, 128 * o : 128 * o + 128] = tile[
                    4 * y + o : 4 * y + o + 1
                ]
    sub = lax.broadcasted_iota(jnp.int32, (8, 128), 0)
    first = got[2 * p, 8:16, :].astype(F32) * scale
    last = got[2 * p + 1, 8:16, :].astype(F32) * scale
    mid = jnp.where(sub < 4, pltpu.roll(first, 64, 1), pltpu.roll(pltpu.roll(last, 64, 1), 4, 0))
    virt_out[0:8, :] = first[:, 0:48]
    virt_out[8:16, :] = mid[:, 0:48]
    virt_out[16:24, :] = last[:, 0:48]


def in_vmem(x):
    return pltpu.with_memory_space_constraint(x, pltpu.VMEM)


def call(body, ins, outs, scalars, scratch=(), in_place=None, anywhere=False):
    smem = pl.BlockSpec(memory_space=pltpu.SMEM)
    vmem = pl.BlockSpec(memory_space=pltpu.VMEM)
    hbm = pl.BlockSpec(memory_space=pl.ANY)
    in_specs = [smem] * len(scalars) + [vmem] * len(ins)
    operands = [*scalars, *ins]
    aliases = {}
    if in_place is not None:
        in_specs.insert(len(scalars), hbm)
        operands.insert(len(scalars), in_place)
        aliases = {len(scalars): 0}
    return pl.pallas_call(
        body,
        in_specs=in_specs,
        out_specs=[hbm if anywhere else vmem] * len(outs),
        out_shape=outs,
        scratch_shapes=scratch,
        input_output_aliases=aliases,
        compiler_params=VMEM,
    )(*operands)


def on_device(integrals, amplitudes, pno_density, pno_coef, pao_blocks, aux_slice, aux_offset):
    pair = lax.axis_index("pair")
    low = lax.axis_index("low")
    scale = 1.0 / math.sqrt(PAIRS * 32)
    sds = jax.ShapeDtypeStruct
    coef = jnp.swapaxes(pno_coef, 1, 2)
    blocks = pao_blocks.T
    mine, other = call(
        virtual_kernel,
        [pno_density, coef],
        [sds((768, 384), F32), sds((768, 384), BF)],
        [blocks, (pair % 2).reshape(1)],
        [pltpu.VMEM((1024, 768), BF), pltpu.VMEM((1024, 768), BF)],
    )
    other = lax.ppermute(other, "pair", [(i, i ^ 1) for i in range(32)])
    (filled,) = call(
        piece_kernel,
        [jnp.swapaxes(integrals, 1, 2), amplitudes, coef],
        [sds((GROUP, ROWS1, 128), BF)],
        [],
        [
            pltpu.VMEM((8192, 128), F32),
            pltpu.VMEM((GROUP, 128, 128), BF),
            pltpu.SemaphoreType.DMA((8,)),
        ],
        anywhere=True,
    )
    (sent,) = call(
        rest_kernel,
        [mine, other],
        [sds((GROUP, ROWS1, 128), BF)],
        [blocks, aux_slice.T, aux_offset.T],
        [pltpu.VMEM((GROUP, ROWS1 - 128, 128), BF), pltpu.SemaphoreType.DMA(())],
        in_place=filled,
        anywhere=True,
    )
    got = lax.all_to_all(sent, ("pair", "low"), split_axis=0, concat_axis=0, tiled=True)
    (sent,) = call(
        place_kernel,
        [in_vmem(got)],
        [sds((8, ROWS2, 128), BF)],
        [],
        [pltpu.VMEM((384, 4096), BF), pltpu.VMEM((384, 256), F32)],
    )
    got = lax.all_to_all(sent, "high", split_axis=0, concat_axis=0, tiled=True)
    (sent,) = call(
        column_kernel,
        [in_vmem(got)],
        [sds((GROUP, ROWS3, 128), BF)],
        [(2 * pair + low).reshape(1)],
    )
    got = lax.all_to_all(sent, ("pair", "low"), split_axis=0, concat_axis=0, tiled=True)
    aux, virt = call(
        lambda *refs: final_kernel(*refs, scale=scale),
        [in_vmem(got)],
        [sds((24, 512), F32), sds((24, 48), F32)],
        [pair.reshape(1)],
    )
    return aux.T, virt.T


def solution(mesh):
    split = Mesh(mesh.devices.reshape(32, 8, 2), ("pair", "high", "low"))
    every = ("pair", "high", "low")
    in_specs = (P(every, None, None),) * 4 + (P(every, None),) * 3
    out_specs = (P(("high", "low"), "pair"),) * 2
    return jax.shard_map(
        on_device, mesh=split, in_specs=in_specs, out_specs=out_specs, check_vma=False
    )
```

time: 122 us -> 114 us (0.934)
  waiting for transfers between devices: 25.9 us -> 16.7 us
  Pallas kernels: 16.3 us -> 10.6 us
  local copies, waits for them, and re-layouts: 1.45 us -> 5.71 us
  blocking collectives: 54.4 us -> 57.2 us
    all_to_all x1 -> x0, waiting for transfers between devices: 10.3 us -> none  [on_device(): lax.all_to_all(sent, ('pair', 'low'), split_axis=0, concat_axis=0, tiled=...]
    all_to_all x1 -> x0, starting transfers between devices: 10.2 us -> none  [on_device(): lax.all_to_all(sent, ('pair', 'low'), split_axis=0, concat_axis=0, tiled=...]
    ppermute x0 -> x1, starting transfers between devices: none -> 8.79 us  [on_device(): other = lax.ppermute(other, 'pair', [(i, i ^ 1) for i in range(32)])]
    pallas_call x4 -> x6, Pallas kernels: 16.3 us -> 10.6 us  [call(): pl.pallas_call(body, in_specs=in_specs, out_specs=[hbm if anywhere else v...]
    unnamed x4 -> x18, local copies, waits for them, and re-layouts: 1.45 us -> 5.71 us
    all_to_all x1 -> x2, blocking collectives: 54.4 us -> 57.2 us  [on_device(): lax.all_to_all(sent, ('pair', 'low'), split_axis=0, concat_axis=0, tiled=...]
    all_to_all x1, starting transfers between devices: 12.4 us -> 13.9 us  [on_device(): got = lax.all_to_all(sent, 'high', split_axis=0, concat_axis=0, tiled=True)]
  transfers between devices with their start and end apart: 2 -> 2, of which waited for: 2 -> 1; matrix products, arithmetic and copies ran while one was open for 1% -> 0% of each run, Pallas kernels for 0% -> 4%
where the time goes in v2:
time: 114 us
  blocking collectives  57.2 us (50%)
  starting transfers between devices  22.7 us (20%)
  waiting for transfers between devices  16.7 us (15%)
  Pallas kernels  10.6 us (9%)
  local copies, waits for them, and re-layouts  5.71 us (5%)
    all_to_all x2, blocking collectives, on_device(): lax.all_to_all(sent, ('pair', 'low'), split_axis=0, concat_axis=0, tiled=...  57.2 us
    all_to_all x1, waiting for transfers between devices, on_device(): got = lax.all_to_all(sent, 'high', split_axis=0, concat_axis=0, tiled=True)  16.7 us
    all_to_all x1, starting transfers between devices, on_device(): got = lax.all_to_all(sent, 'high', split_axis=0, concat_axis=0, tiled=True)  13.9 us
    pallas_call x6, Pallas kernels, call(): pl.pallas_call(body, in_specs=in_specs, out_specs=[hbm if anywhere else v...  10.6 us
    ppermute x1, starting transfers between devices, on_device(): other = lax.ppermute(other, 'pair', [(i, i ^ 1) for i in range(32)])  8.79 us
    unnamed x18, local copies, waits for them, and re-layouts  5.71 us
  transfers between devices with their start and end apart: 2, of which 1 were waited for; matrix products, arithmetic and copies ran while one was open for 0% of the time, Pallas kernels for 4%

profile of v2, /device:TPU:1, one launch (start us, length us, event | category | flops | bytes accessed | tf_op | source)
XLA Modules:
  0.0 113.6 jit_solution(14269452733703687517)
XLA Ops:
  0.6 0.0 copy-start.6
  0.6 0.0 copy-start.8
  0.7 0.0 copy-start.7
  0.7 0.0 copy-start
  0.7 1.0 copy-done
  1.7 0.0 copy-start.4
  1.7 0.9 copy-done.4
  2.7 0.0 copy-start.5
  2.7 0.7 copy-done.5
  3.4 2.9 %shard_map.87 = (f32[768,384]{1,0:T(8,128)S(1)}, bf16[768,384]{1,0:T(8,128)(2,1)S(1)}) custom-call(s32[2,16]{1,0:T(2,128)S(1)} %bitcast.13, s32[1]{0:T(128)} %bitcast.7.core, bf16[16,64,64]{2,1,0:T(8,128)(2,1)S(1)} %copy-done.4, bf16[16,64,256]{2,1,0:T(8,128)(2,1)S(1)} %bitcast.10), custom_call_target="tpu_custom_call" | custom-call | tf_op jit(solution)/shard_map/pallas_call | solution.py:200
  6.2 8.8 %collective-permute-start = (bf16[768,384]{1,0:T(8,128)(2,1)S(1)}, bf16[768,384]{1,0:T(8,128)(2,1)S(1)}, u32[]{:S(2)}, u32[]{:S(2)}) collective-permute-start(bf16[768,384]{1,0:T(8,128)(2,1)S(1)} %get-tuple-element.7), channel_id=1, source_target_pairs={{0,16},{16,0},{32,48},{48,32},{64,80},{80,64},{96,112},{112,96},{1... | collective-permute-start | bytes 1769480 | tf_op jit(solution)/shard_map/ppermute | solution.py:225
  15.0 0.0 copy-start.1
  15.0 1.0 copy-done.1
  16.1 0.0 copy-start.2
  16.1 1.0 copy-done.2
  17.1 0.0 copy-start.3
  17.1 0.9 copy-done.3
  18.0 4.2 %shard_map.86.filled = bf16[64,168,128]{2,1,0:T(8,128)(2,1)S(1)} custom-call(bf16[16,64,256]{2,1,0:T(8,128)(2,1)S(1)} %bitcast.12, bf16[16,64,64]{2,1,0:T(8,128)(2,1)S(1)} %copy-done.3, bf16[16,64,256]{2,1,0:T(8,128)(2,1)S(1)} %bitcast.11), custom_call_target="tpu_custom_call" | custom-call | tf_op jit(solution)/shard_map/pallas_call | solution.py:200
  22.3 0.0 collective-permute-done.other
  22.3 0.0 copy-done.6
  22.3 0.0 copy-done.8
  22.3 0.0 copy-done.7
  22.3 0.9 shard_map.88
  23.2 39.1 %all_to_all.15.got = bf16[64,168,128]{2,1,0:T(8,128)(2,1)S(1)} all-to-all(bf16[64,168,128]{2,1,0:T(8,128)(2,1)S(1)} %shard_map.88), channel_id=1, replica_groups=mesh['pair'=32,'high'=8,'low'=2] {'pair','low'}, dimensions={0} | all-to-all | bytes 5505024 | tf_op jit(solution)/shard_map/all_to_all | solution.py:247
  62.3 1.9 %shard_map.89 = bf16[8,112,128]{2,1,0:T(8,128)(2,1)} custom-call(bf16[64,168,128]{2,1,0:T(8,128)(2,1)S(1)} %all_to_all.15.got), custom_call_target="tpu_custom_call" | custom-call | tf_op jit(solution)/shard_map/pallas_call | solution.py:200
  64.2 13.9 %all-to-all-start.1 = ((bf16[8,112,128]{2,1,0:T(8,128)(2,1)}), bf16[8,112,128]{2,1,0:T(8,128)(2,1)S(1)}, u32[]{:S(2)}, u32[]{:S(2)}) async-start(bf16[8,112,128]{2,1,0:T(8,128)(2,1)} %shard_map.89), calls=%async_computation.1 | async-start | bytes 458752 | tf_op jit(solution)/shard_map/all_to_all | solution.py:255
  78.2 16.7 %all-to-all-done.1.got = bf16[8,112,128]{2,1,0:T(8,128)(2,1)S(1)} async-done(((bf16[8,112,128]{2,1,0:T(8,128)(2,1)}), bf16[8,112,128]{2,1,0:T(8,128)(2,1)S(1)}, u32[]{:S(2)}, u32[]{:S(2)}) %all-to-all-start.1) | async-done | bytes 229408 | tf_op jit(solution)/shard_map/all_to_all | solution.py:255
  94.8 0.1 shard_map.90
  94.9 18.0 %all_to_all.16.refs_1_ = bf16[64,16,128]{2,1,0:T(8,128)(2,1)S(1)} all-to-all(bf16[64,16,128]{2,1,0:T(8,128)(2,1)S(1)} %shard_map.90), channel_id=1, replica_groups=mesh['pair'=32,'high'=8,'low'=2] {'pair','low'}, dimensions={0} | all-to-all | bytes 524288 | tf_op jit(solution)/shard_map/all_to_all | solution.py:262
  113.0 0.7 shard_map.91
Async XLA Ops:
  0.6 21.6 %copy-start.6 = (s32[16,2]{0,1:T(2,128)S(1)}, s32[16,2]{0,1:T(2,128)}, u32[]{:S(2)}) copy-start(s32[16,2]{0,1:T(2,128)} %param.11) | copy-start | bytes 388
  0.6 21.6 %copy-start.8 = (s32[16,2]{0,1:T(2,128)S(1)}, s32[16,2]{0,1:T(2,128)}, u32[]{:S(2)}) copy-start(s32[16,2]{0,1:T(2,128)} %param.13) | copy-start | bytes 388
  0.7 21.6 %copy-start.7 = (s32[16,2]{0,1:T(2,128)S(1)}, s32[16,2]{0,1:T(2,128)}, u32[]{:S(2)}) copy-start(s32[16,2]{0,1:T(2,128)} %param.12) | copy-start | bytes 388
  0.7 1.0 copy-start
  1.7 0.9 copy-start.4
  2.7 0.7 copy-start.5
  6.2 16.0 %collective-permute-start = (bf16[768,384]{1,0:T(8,128)(2,1)S(1)}, bf16[768,384]{1,0:T(8,128)(2,1)S(1)}, u32[]{:S(2)}, u32[]{:S(2)}) collective-permute-start(bf16[768,384]{1,0:T(8,128)(2,1)S(1)} %get-tuple-element.7), channel_id=1, source_target_pairs={{0,16},{16,0},{32,48},{48,32},{64,80},{80,64},{96,112},{112,96},{1... | collective-permute-start | bytes 1769480 | tf_op jit(solution)/shard_map/ppermute | solution.py:225
  15.0 1.0 copy-start.1
  16.1 1.0 copy-start.2
  17.1 0.9 copy-start.3
  64.2 30.6 %all-to-all-start.1 = ((bf16[8,112,128]{2,1,0:T(8,128)(2,1)}), bf16[8,112,128]{2,1,0:T(8,128)(2,1)S(1)}, u32[]{:S(2)}, u32[]{:S(2)}) async-start(bf16[8,112,128]{2,1,0:T(8,128)(2,1)} %shard_map.89), calls=%async_computation.1 | async-start | bytes 458752 | tf_op jit(solution)/shard_map/all_to_all | solution.py:255

commit v3 on v1

v3 whole, which is shorter than its diff:
```python
import math

import jax
import jax.numpy as jnp
from jax import lax
from jax.experimental import pallas as pl
from jax.experimental.pallas import tpu as pltpu
from jax.sharding import Mesh
from jax.sharding import PartitionSpec as P

NBLK = 6
ABPO = 4
BF = jnp.bfloat16
F32 = jnp.float32
PAIRS = 16
GROUP = 64
ROWS1 = 136
ROWS2 = 120
ROWS3 = 24
BITS = (0, 1, 3, 2, 4)
VMEM = pltpu.CompilerParams(vmem_limit_bytes=20 * 1024 * 1024)


def dot00(a, b):
    return lax.dot_general(a, b, (((0,), (0,)), ((), ())), preferred_element_type=F32)


def dot10(a, b):
    return lax.dot_general(a, b, (((1,), (0,)), ((), ())), preferred_element_type=F32)


def piece_kernel(
    ints_in, amps_in, coef_in, blocks_in, owners_in, offsets_in,
    out, token, coef, ints, amps, pieces, rounded, blocks, owners, offsets, sems, sends,
):
    pairs_in = [
        (blocks_in, blocks), (owners_in, owners), (offsets_in, offsets), (amps_in, amps)
    ]
    for i in range(4):
        four = slice(4 * i, 4 * i + 4)
        pairs_in += [(ints_in.at[four], ints.at[four]), (coef_in.at[four], coef.at[four])]
    copies = [pltpu.make_async_copy(*pair, sems.at[i]) for i, pair in enumerate(pairs_in)]
    for copy in copies:
        copy.start()
    for copy in copies[:4]:
        copy.wait()
    lane = lax.broadcasted_iota(jnp.int32, (1, 128), 1) % 64
    slice_row = jnp.zeros((1, 128), F32)
    block_row = jnp.zeros((1, 128), F32)
    offset_row = jnp.zeros((1, 128), F32)
    for p in range(PAIRS):
        if p % 4 == 0:
            copies[4 + p // 2].wait()
            copies[5 + p // 2].wait()
        three_index = dot00(amps[p], ints[p]).astype(BF)
        piece = dot00(coef[p], three_index)
        for h in range(2):
            for k in range(2):
                slot = 4 * p + 2 * h + k
                pieces[pl.ds(slot, 128, 64), :] = piece[
                    128 * h : 128 * h + 128, 128 * k : 128 * k + 128
                ]
                here = lane == slot
                slice_row = jnp.where(here, owners[k, p].astype(F32), slice_row)
                block_row = jnp.where(here, blocks[h, p].astype(F32), block_row)
                offset_row = jnp.where(here, offsets[k, p].astype(F32), offset_row)
    sub = lax.broadcasted_iota(jnp.int32, (8, 128), 0)
    labels = jnp.where(sub == 0, slice_row, jnp.where(sub == 1, block_row, offset_row))
    token[...] = labels
    labels = labels.astype(BF)
    copies = []
    for i in range(8):
        eight = slice(8 * i, 8 * i + 8)
        for g in range(8 * i, 8 * i + 8):
            rounded[g, 0:128, :] = pieces[128 * g : 128 * g + 128, :].astype(BF)
            rounded[g, 128:ROWS1, :] = labels
        copies.append(pltpu.make_async_copy(rounded.at[eight], out.at[eight], sends.at[i]))
        copies[-1].start()
    for copy in copies:
        copy.wait()


def virtual_kernel(
    bit, dens_in, coef_in, blocks_in, token,
    mine, other, weighted_rows, coef_rows, virt, dens, coef, blocks, sems,
):
    pairs_in = [(dens_in, dens), (coef_in, coef), (blocks_in, blocks)]
    copies = [pltpu.make_async_copy(*pair, sems.at[i]) for i, pair in enumerate(pairs_in)]
    for copy in copies:
        copy.start()
    weighted_rows[...] = jnp.zeros(weighted_rows.shape, BF)
    coef_rows[...] = jnp.zeros(coef_rows.shape, BF)
    for copy in copies:
        copy.wait()
    for p in range(PAIRS):
        c = coef[p]
        weighted = dot00(dens[p], c).astype(BF)
        for h in range(2):
            at = pl.ds(pl.multiple_of(blocks[h, p] * 128, 128), 128)
            weighted_rows[64 * p : 64 * p + 64, at] = weighted[:, 128 * h : 128 * h + 128]
            coef_rows[64 * p : 64 * p + 64, at] = c[:, 128 * h : 128 * h + 128]
    virt[...] = dot00(coef_rows[...], weighted_rows[...])
    for i in range(16):
        mine[i] = virt[pl.ds(pl.multiple_of(48 * i + 24 * bit[0], 8), 24), :]
        away = virt[pl.ds(pl.multiple_of(48 * i + 24 * (1 - bit[0]), 8), 24), :]
        other[i] = away.astype(BF)


def halve_kernel(bit, mine, got, kept, other, *, after):
    for i in range(kept.shape[0]):
        first = (i // after) * 2 * after + i % after
        keep = first + after * bit[0]
        away = first + after * (1 - bit[0])
        kept[i] = mine[keep] + got[keep].astype(F32)
        other[i] = (mine[away] + got[away].astype(F32)).astype(other.dtype)


def place_kernel(got, mine, other, out, hot, acc):
    lane = lax.broadcasted_iota(jnp.int32, (1, 128), 1)
    cell = lax.broadcasted_iota(jnp.int32, (384, 128), 0)
    for i in range(GROUP // 2):
        first = got[2 * i, 128:136, :].astype(F32)
        second = got[2 * i + 1, 128:136, :].astype(F32)
        both = jnp.where(lane < 64, first, second)
        target = both[0:1] * 24.0 + both[1:2] * 4.0 + both[2:3]
        hot[:, 128 * i : 128 * i + 128] = (cell == target.astype(jnp.int32)).astype(BF)
    data = jnp.concatenate(
        [got[:, 0:64, :].reshape(4096, 128), got[:, 64:128, :].reshape(4096, 128)], 1
    )
    acc[...] = dot10(hot[...], data)
    lanes8 = lax.broadcasted_iota(jnp.int32, (8, 128), 1)
    virt = mine[0] + other[0].astype(F32)
    for z in range(8):
        rows = [acc[48 * z : 48 * z + 48, 0:128], acc[48 * z : 48 * z + 48, 128:256]]
        for i in range(3):
            a, b, c = (
                virt[8 * i : 8 * i + 8, 384 * (z // 4) + 128 * j : 384 * (z // 4) + 128 * j + 128]
                for j in range(3)
            )
            if z % 4 == 0:
                rows.append(a)
            elif z % 4 == 1:
                rows.append(jnp.where(lanes8 < 32, pltpu.roll(a, 32, 1), pltpu.roll(b, 32, 1)))
            elif z % 4 == 2:
                rows.append(jnp.where(lanes8 < 64, pltpu.roll(b, 64, 1), pltpu.roll(c, 64, 1)))
            else:
                rows.append(pltpu.roll(c, 96, 1))
        out[z] = jnp.concatenate(rows, 0).astype(BF)


def column_kernel(place, got, out):
    total = got[0].astype(F32)
    for z in range(1, 8):
        total = total + got[z].astype(F32)
    sub = lax.broadcasted_iota(jnp.int32, (8, 128), 0)
    lane = lax.broadcasted_iota(jnp.int32, (8, 128), 1)
    tiles = []
    for i in range(6):
        a, b = total[8 * i : 8 * i + 8], total[48 + 8 * i : 56 + 8 * i]
        tiles.append(jnp.where(sub < 4, a, pltpu.roll(b, 4, 0)))
        tiles.append(jnp.where(sub < 4, pltpu.roll(a, 4, 0), b))
    column = 2 * place[0]
    virt = [total[96 + 8 * i : 104 + 8 * i] for i in range(3)]
    packed = []
    for shift in (0, 80):
        v0, v1, v2 = (pltpu.roll(v, shift, 1) if shift else v for v in virt)
        packed.append([jnp.where(lane < 64, v0, pltpu.roll(v1, 64, 1)), v2])
    for low in range(2):
        for p in range(32):
            b_first, b_last = (24 * p) // 128, (24 * p + 23) // 128
            tile = tiles[6 * low + b_first]
            if b_last != b_first:
                tile = jnp.where(column >= 24 * p - 128 * b_first, tile, tiles[6 * low + b_last])
            out[2 * p + low] = jnp.concatenate([tile] + packed[low], 0).astype(BF)


def final_kernel(place, got, aux_out, virt_out, *, scale):
    p = place[0]
    for j in range(12):
        tile = got[lax.rem(12 * p + j, 64), 0:8, :].astype(F32) * scale
        for y in range(2):
            for o in range(ABPO):
                aux_out[2 * j + y : 2 * j + y + 1, 128 * o : 128 * o + 128] = tile[
                    4 * y + o : 4 * y + o + 1
                ]
    both = (got[2 * p, 8:24, :].astype(F32) + got[2 * p + 1, 8:24, :].astype(F32)) * scale
    virt_out[0:8, :] = both[0:8, 0:48]
    virt_out[8:16, :] = pltpu.roll(both[0:8], 64, 1)[:, 0:48]
    virt_out[16:24, :] = both[8:16, 0:48]


def in_vmem(x):
    return pltpu.with_memory_space_constraint(x, pltpu.VMEM)


def in_hbm(x):
    return pltpu.with_memory_space_constraint(x, pltpu.HBM)


def call(body, ins, outs, scalars=(), scratch=(), held=(), far=0):
    smem = pl.BlockSpec(memory_space=pltpu.SMEM)
    vmem = pl.BlockSpec(memory_space=pltpu.VMEM)
    hbm = pl.BlockSpec(memory_space=pltpu.HBM)
    return pl.pallas_call(
        body,
        in_specs=[smem] * len(scalars) + [hbm] * len(held) + [vmem] * len(ins),
        out_specs=[hbm] * far + [vmem] * (len(outs) - far),
        out_shape=outs,
        scratch_shapes=scratch,
        compiler_params=VMEM,
    )(*scalars, *map(in_hbm, held), *map(in_vmem, ins))


def on_device(integrals, amplitudes, pno_density, pno_coef, pao_blocks, aux_slice, aux_offset):
    pair = lax.axis_index("pair")
    low = lax.axis_index("low")
    scale = 1.0 / math.sqrt(PAIRS * 32)
    sds = jax.ShapeDtypeStruct
    coef, blocks = jnp.swapaxes(pno_coef, 1, 2), pao_blocks.T
    names = pltpu.SMEM((2, PAIRS), jnp.int32)
    sent, token = call(
        piece_kernel,
        [],
        [pltpu.HBM((GROUP, ROWS1, 128), BF), sds((8, 128), F32)],
        scratch=[
            pltpu.VMEM((PAIRS, 64, 256), BF),
            pltpu.VMEM((PAIRS, 64, 256), BF),
            pltpu.VMEM((PAIRS, 64, 64), BF),
            pltpu.VMEM((8192, 128), F32),
            pltpu.VMEM((GROUP, ROWS1, 128), BF),
            names,
            names,
            names,
            pltpu.SemaphoreType.DMA((12,)),
            pltpu.SemaphoreType.DMA((8,)),
        ],
        held=[jnp.swapaxes(integrals, 1, 2), amplitudes, coef, blocks, aux_slice.T, aux_offset.T],
        far=1,
    )
    got = lax.all_to_all(sent, ("pair", "low"), split_axis=0, concat_axis=0, tiled=True)
    bits = [((pair >> b) & 1).reshape(1) for b in BITS]
    mine, other = call(
        virtual_kernel,
        [token],
        [sds((16, 24, 768), F32), sds((16, 24, 768), BF)],
        [bits[0]],
        [
            pltpu.VMEM((1024, 768), BF),
            pltpu.VMEM((1024, 768), BF),
            pltpu.VMEM((768, 768), F32),
            pltpu.VMEM((PAIRS, 64, 64), BF),
            pltpu.VMEM((PAIRS, 64, 256), BF),
            names,
            pltpu.SemaphoreType.DMA((3,)),
        ],
        held=[pno_density, coef, blocks],
    )
    left = [4, 3, 2, 1]
    for i in range(5):
        other = lax.ppermute(other, "pair", [(q, q ^ (1 << BITS[i])) for q in range(32)])
        if i == 4:
            break
        after = 2 ** sum(b < BITS[i + 1] for b in left)
        left.remove(BITS[i + 1])
        kept = mine.shape[0] // 2
        mine, other = call(
            lambda *refs, after=after: halve_kernel(*refs, after=after),
            [mine, other],
            [sds((kept, 24, 768), F32), sds((kept, 24, 768), BF if kept > 2 else F32)],
            [bits[i + 1]],
        )
    (sent,) = call(
        place_kernel,
        [got, mine, other],
        [sds((8, ROWS2, 128), BF)],
        scratch=[pltpu.VMEM((384, 4096), BF), pltpu.VMEM((384, 256), F32)],
    )
    got = lax.all_to_all(sent, "high", split_axis=0, concat_axis=0, tiled=True)
    (sent,) = call(
        column_kernel,
        [got],
        [sds((GROUP, ROWS3, 128), BF)],
        [(2 * pair + low).reshape(1)],
    )
    got = lax.all_to_all(sent, ("pair", "low"), split_axis=0, concat_axis=0, tiled=True)
    aux, virt = call(
        lambda *refs: final_kernel(*refs, scale=scale),
        [got],
        [sds((24, 512), F32), sds((24, 48), F32)],
        [pair.reshape(1)],
    )
    return aux.T, virt.T


def solution(mesh):
    split = Mesh(mesh.devices.reshape(32, 8, 2), ("pair", "high", "low"))
    every = ("pair", "high", "low")
    in_specs = (P(every, None, None),) * 4 + (P(every, None),) * 3
    out_specs = (P(("high", "low"), "pair"),) * 2
    return jax.shard_map(
        on_device, mesh=split, in_specs=in_specs, out_specs=out_specs, check_vma=False
    )
```

time: 122 us -> 129 us (1.057)
  blocking collectives: 54.4 us -> 24.5 us
  starting transfers between devices: 22.6 us -> 42.4 us
  waiting for transfers between devices: 25.9 us -> 43.5 us
    all_to_all x1, blocking collectives: 54.4 us -> 24.5 us  [on_device(): lax.all_to_all(sent, ('pair', 'low'), split_axis=0, concat_axis=0, tiled=...]
    ppermute x0 -> x5, waiting for transfers between devices: none -> 27.8 us  [on_device(): lax.ppermute(other, 'pair', [(q, q ^ 1 << BITS[i]) for q in range(32)])]
    ppermute x0 -> x5, starting transfers between devices: none -> 18.1 us  [on_device(): lax.ppermute(other, 'pair', [(q, q ^ 1 << BITS[i]) for q in range(32)])]
    all_to_all x1, waiting for transfers between devices: 10.3 us -> 0.01 us  [on_device(): lax.all_to_all(sent, ('pair', 'low'), split_axis=0, concat_axis=0, tiled=...]
    pallas_call x4 -> x9, Pallas kernels: 16.3 us -> 15.5 us  [call(): pl.pallas_call(body, in_specs=[smem] * len(scalars) + [hbm] * len(held) +...]
  transfers between devices with their start and end apart: 2 -> 7, of which waited for: 2 -> 6; matrix products, arithmetic and copies ran while one was open for 1% -> 0% of each run, Pallas kernels for 0% -> 5%
where the time goes in v3:
time: 129 us; the launch traced here: 128 us
  waiting for transfers between devices  43.5 us (34%)
  starting transfers between devices  42.4 us (33%)
  blocking collectives  24.5 us (19%)
  Pallas kernels  15.5 us (12%)
  local copies, waits for them, and re-layouts  1.89 us (1%)
    ppermute x5, waiting for transfers between devices, on_device(): lax.ppermute(other, 'pair', [(q, q ^ 1 << BITS[i]) for q in range(32)])  27.8 us
    all_to_all x1, blocking collectives, on_device(): lax.all_to_all(sent, ('pair', 'low'), split_axis=0, concat_axis=0, tiled=...  24.5 us
    ppermute x5, starting transfers between devices, on_device(): lax.ppermute(other, 'pair', [(q, q ^ 1 << BITS[i]) for q in range(32)])  18.1 us
    all_to_all x1, waiting for transfers between devices, on_device(): got = lax.all_to_all(sent, 'high', split_axis=0, concat_axis=0, tiled=True)  15.7 us
    pallas_call x9, Pallas kernels, call(): pl.pallas_call(body, in_specs=[smem] * len(scalars) + [hbm] * len(held) +...  15.5 us
    all_to_all x1, starting transfers between devices, on_device(): got = lax.all_to_all(sent, 'high', split_axis=0, concat_axis=0, tiled=True)  13.2 us
    all_to_all x1, starting transfers between devices, on_device(): lax.all_to_all(sent, ('pair', 'low'), split_axis=0, concat_axis=0, tiled=...  11 us
  transfers between devices with their start and end apart: 7, of which 6 were waited for; matrix products, arithmetic and copies ran while one was open for 0% of the time, Pallas kernels for 5%

profile of v3, /device:TPU:1, one launch (start us, length us, event | category | flops | bytes accessed | tf_op | source)
XLA Modules:
  0.0 128.4 jit_solution(176982585722055075)
XLA Ops:
  0.6 6.9 %shard_map.86 = (bf16[64,136,128]{2,1,0:T(8,128)(2,1)}, f32[8,128]{1,0:T(8,128)S(1)}) custom-call(bf16[16,64,256]{2,1,0:T(8,128)(2,1)} %bitcast.16, bf16[16,64,64]{2,1,0:T(8,128)(2,1)} %amps_in.1, bf16[16,64,256]{2,1,0:T(8,128)(2,1)} %bitcast.14, s32[2,16]{1,0:T(2,128)} %bitcast.17, s32[2,16]{1,0:T(2,128)} %bitcast.19, s32[2,16]{1,0:T(2,128)} %bitcast.20), custom_call_target="tpu_custom_call" | custom-call | tf_op jit(solution)/shard_map/pallas_call | solution.py:204
  7.5 11.0 %all-to-all-start = ((bf16[64,136,128]{2,1,0:T(8,128)(2,1)}), bf16[64,136,128]{2,1,0:T(8,128)(2,1)S(1)}, u32[]{:S(2)}, u32[]{:S(2)}) async-start(bf16[64,136,128]{2,1,0:T(8,128)(2,1)} %get-tuple-element.16), calls=%async_computation | async-start | bytes 4456448 | tf_op jit(solution)/shard_map/all_to_all | solution.py:240
  18.5 3.9 %shard_map.87 = (f32[16,24,768]{2,1,0:T(8,128)S(1)}, bf16[16,24,768]{2,1,0:T(8,128)(2,1)}) custom-call(s32[1]{0:T(128)} %bitcast.11.bit, bf16[16,64,64]{2,1,0:T(8,128)(2,1)} %dens_in.1, bf16[16,64,256]{2,1,0:T(8,128)(2,1)} %bitcast.15, s32[2,16]{1,0:T(2,128)} %bitcast.18, f32[8,128]{1,0:T(8,128)S(1)} %get-tuple-element.17.token), custom_call_target="tpu_custom_call" | custom-call | tf_op jit(solution)/shard_map/pallas_call | solution.py:204
  22.4 2.5 %collective-permute-start = (bf16[16,24,768]{2,1,0:T(8,128)(2,1)}, bf16[16,24,768]{2,1,0:T(8,128)(2,1)}, u32[]{:S(2)}, u32[]{:S(2)}) collective-permute-start(bf16[16,24,768]{2,1,0:T(8,128)(2,1)} %get-tuple-element.19), channel_id=1, source_target_pairs={{0,16},{16,0},{32,48},{48,32},{64,80},{80,64},{96,112},{112,96},{1... | collective-permute-start | bytes 1769480 | tf_op jit(solution)/shard_map/ppermute | solution.py:260
  24.9 1.9 %collective-permute-done.refs_2_ = bf16[16,24,768]{2,1,0:T(8,128)(2,1)} collective-permute-done((bf16[16,24,768]{2,1,0:T(8,128)(2,1)}, bf16[16,24,768]{2,1,0:T(8,128)(2,1)}, u32[]{:S(2)}, u32[]{:S(2)}) %collective-permute-start) | collective-permute-done | bytes 589856 | tf_op jit(solution)/shard_map/ppermute | solution.py:260
  26.9 1.9 %shard_map.88 = (f32[8,24,768]{2,1,0:T(8,128)S(1)}, bf16[8,24,768]{2,1,0:T(8,128)(2,1)}) custom-call(s32[1]{0:T(128)} %bitcast.10.refs_0_, f32[16,24,768]{2,1,0:T(8,128)S(1)} %get-tuple-element.18.refs_1_, bf16[16,24,768]{2,1,0:T(8,128)(2,1)} %collective-permute-done.refs_2_), custom_call_target="tpu_custom_call" | custom-call | tf_op jit(solution)/shard_map/pallas_call | solution.py:204
  28.8 0.0 copy-start
  28.8 0.8 copy-done
  29.6 3.1 %collective-permute-start.1 = (bf16[8,24,768]{2,1,0:T(8,128)(2,1)}, bf16[8,24,768]{2,1,0:T(8,128)(2,1)S(1)}, u32[]{:S(2)}, u32[]{:S(2)}) collective-permute-start(bf16[8,24,768]{2,1,0:T(8,128)(2,1)} %get-tuple-element.21), channel_id=1, source_target_pairs={{0,32},{16,48},{32,0},{48,16},{64,96},{80,112},{96,64},{112,80},{1... | collective-permute-start | bytes 884744 | tf_op jit(solution)/shard_map/ppermute | solution.py:260
  32.7 18.1 %collective-permute-done.1.refs_2_ = bf16[8,24,768]{2,1,0:T(8,128)(2,1)S(1)} collective-permute-done((bf16[8,24,768]{2,1,0:T(8,128)(2,1)}, bf16[8,24,768]{2,1,0:T(8,128)(2,1)S(1)}, u32[]{:S(2)}, u32[]{:S(2)}) %collective-permute-start.1) | collective-permute-done | bytes 294944 | tf_op jit(solution)/shard_map/ppermute | solution.py:260
  50.8 0.0 copy-start.1
  50.8 1.1 copy-done.1
  51.9 0.1 shard_map.89
  51.9 3.2 %collective-permute-start.2 = (bf16[4,24,768]{2,1,0:T(8,128)(2,1)S(1)}, bf16[4,24,768]{2,1,0:T(8,128)(2,1)S(1)}, u32[]{:S(2)}, u32[]{:S(2)}) collective-permute-start(bf16[4,24,768]{2,1,0:T(8,128)(2,1)S(1)} %get-tuple-element.23), channel_id=1, source_target_pairs={{0,128},{16,144},{32,160},{48,176},{64,192},{80,208},{96,224},{112... | collective-permute-start | bytes 442376 | tf_op jit(solution)/shard_map/ppermute | solution.py:260
  55.1 3.2 %collective-permute-done.2.refs_2_ = bf16[4,24,768]{2,1,0:T(8,128)(2,1)S(1)} collective-permute-done((bf16[4,24,768]{2,1,0:T(8,128)(2,1)S(1)}, bf16[4,24,768]{2,1,0:T(8,128)(2,1)S(1)}, u32[]{:S(2)}, u32[]{:S(2)}) %collective-permute-start.2) | collective-permute-done | bytes 147488 | tf_op jit(solution)/shard_map/ppermute | solution.py:260
  58.3 4.5 %collective-permute-start.3 = (f32[2,24,768]{2,1,0:T(8,128)S(1)}, f32[2,24,768]{2,1,0:T(8,128)S(1)}, u32[]{:S(2)}, u32[]{:S(2)}) collective-permute-start(f32[2,24,768]{2,1,0:T(8,128)S(1)} %get-tuple-element.25), channel_id=1, source_target_pairs={{0,64},{16,80},{32,96},{48,112},{64,0},{80,16},{96,32},{112,48},{1... | collective-permute-start | bytes 442376 | tf_op jit(solution)/shard_map/ppermute | solution.py:260
  62.9 2.8 %collective-permute-done.3.refs_2_ = f32[2,24,768]{2,1,0:T(8,128)S(1)} collective-permute-done((f32[2,24,768]{2,1,0:T(8,128)S(1)}, f32[2,24,768]{2,1,0:T(8,128)S(1)}, u32[]{:S(2)}, u32[]{:S(2)}) %collective-permute-start.3) | collective-permute-done | bytes 147488 | tf_op jit(solution)/shard_map/ppermute | solution.py:260
  65.7 4.8 %collective-permute-start.4 = (f32[1,24,768]{2,1,0:T(8,128)S(1)}, f32[1,24,768]{2,1,0:T(8,128)S(1)}, u32[]{:S(2)}, u32[]{:S(2)}) collective-permute-start(f32[1,24,768]{2,1,0:T(8,128)S(1)} %get-tuple-element.27), channel_id=1, source_target_pairs={{0,256},{16,272},{32,288},{48,304},{64,320},{80,336},{96,352},{112... | collective-permute-start | bytes 221192 | tf_op jit(solution)/shard_map/ppermute | solution.py:260
  70.6 1.8 %collective-permute-done.4.other = f32[1,24,768]{2,1,0:T(8,128)S(1)} collective-permute-done((f32[1,24,768]{2,1,0:T(8,128)S(1)}, f32[1,24,768]{2,1,0:T(8,128)S(1)}, u32[]{:S(2)}, u32[]{:S(2)}) %collective-permute-start.4) | collective-permute-done | bytes 73760 | tf_op jit(solution)/shard_map/ppermute | solution.py:260
  72.3 0.0 all-to-all-done.got
  72.3 1.9 %shard_map.92 = bf16[8,120,128]{2,1,0:T(8,128)(2,1)} custom-call(bf16[64,136,128]{2,1,0:T(8,128)(2,1)S(1)} %all-to-all-done.got, f32[1,24,768]{2,1,0:T(8,128)S(1)} %get-tuple-element.26.mine, f32[1,24,768]{2,1,0:T(8,128)S(1)} %collective-permute-done.4.other), custom_call_target="tpu_custom_call" | custom-call | tf_op jit(solution)/shard_map/pallas_call | solution.py:204
  74.2 13.2 %all-to-all-start.1 = ((bf16[8,120,128]{2,1,0:T(8,128)(2,1)}), bf16[8,120,128]{2,1,0:T(8,128)(2,1)S(1)}, u32[]{:S(2)}, u32[]{:S(2)}) async-start(bf16[8,120,128]{2,1,0:T(8,128)(2,1)} %shard_map.92), calls=%async_computation.1 | async-start | bytes 491520 | tf_op jit(solution)/shard_map/all_to_all | solution.py:278
  87.4 15.7 %all-to-all-done.1.got = bf16[8,120,128]{2,1,0:T(8,128)(2,1)S(1)} async-done(((bf16[8,120,128]{2,1,0:T(8,128)(2,1)}), bf16[8,120,128]{2,1,0:T(8,128)(2,1)S(1)}, u32[]{:S(2)}, u32[]{:S(2)}) %all-to-all-start.1) | async-done | bytes 245792 | tf_op jit(solution)/shard_map/all_to_all | solution.py:278
  103.1 0.2 shard_map.93
  103.3 24.5 %all_to_all.15.refs_1_ = bf16[64,24,128]{2,1,0:T(8,128)(2,1)S(1)} all-to-all(bf16[64,24,128]{2,1,0:T(8,128)(2,1)S(1)} %shard_map.93), channel_id=1, replica_groups=mesh['pair'=32,'high'=8,'low'=2] {'pair','low'}, dimensions={0} | all-to-all | bytes 786432 | tf_op jit(solution)/shard_map/all_to_all | solution.py:285
  127.7 0.7 shard_map.94
  (2 shorter events, 0.0 us)
Async XLA Ops:
  7.5 64.8 %all-to-all-start = ((bf16[64,136,128]{2,1,0:T(8,128)(2,1)}), bf16[64,136,128]{2,1,0:T(8,128)(2,1)S(1)}, u32[]{:S(2)}, u32[]{:S(2)}) async-start(bf16[64,136,128]{2,1,0:T(8,128)(2,1)} %get-tuple-element.16), calls=%async_computation | async-start | bytes 4456448 | tf_op jit(solution)/shard_map/all_to_all | solution.py:240
  22.4 4.4 %collective-permute-start = (bf16[16,24,768]{2,1,0:T(8,128)(2,1)}, bf16[16,24,768]{2,1,0:T(8,128)(2,1)}, u32[]{:S(2)}, u32[]{:S(2)}) collective-permute-start(bf16[16,24,768]{2,1,0:T(8,128)(2,1)} %get-tuple-element.19), channel_id=1, source_target_pairs={{0,16},{16,0},{32,48},{48,32},{64,80},{80,64},{96,112},{112,96},{1... | collective-permute-start | bytes 1769480 | tf_op jit(solution)/shard_map/ppermute | solution.py:260
  28.8 0.8 copy-start
  29.6 21.2 %collective-permute-start.1 = (bf16[8,24,768]{2,1,0:T(8,128)(2,1)}, bf16[8,24,768]{2,1,0:T(8,128)(2,1)S(1)}, u32[]{:S(2)}, u32[]{:S(2)}) collective-permute-start(bf16[8,24,768]{2,1,0:T(8,128)(2,1)} %get-tuple-element.21), channel_id=1, source_target_pairs={{0,32},{16,48},{32,0},{48,16},{64,96},{80,112},{96,64},{112,80},{1... | collective-permute-start | bytes 884744 | tf_op jit(solution)/shard_map/ppermute | solution.py:260
  50.8 1.1 copy-start.1
  51.9 6.4 %collective-permute-start.2 = (bf16[4,24,768]{2,1,0:T(8,128)(2,1)S(1)}, bf16[4,24,768]{2,1,0:T(8,128)(2,1)S(1)}, u32[]{:S(2)}, u32[]{:S(2)}) collective-permute-start(bf16[4,24,768]{2,1,0:T(8,128)(2,1)S(1)} %get-tuple-element.23), channel_id=1, source_target_pairs={{0,128},{16,144},{32,160},{48,176},{64,192},{80,208},{96,224},{112... | collective-permute-start | bytes 442376 | tf_op jit(solution)/shard_map/ppermute | solution.py:260
  58.3 7.4 %collective-permute-start.3 = (f32[2,24,768]{2,1,0:T(8,128)S(1)}, f32[2,24,768]{2,1,0:T(8,128)S(1)}, u32[]{:S(2)}, u32[]{:S(2)}) collective-permute-start(f32[2,24,768]{2,1,0:T(8,128)S(1)} %get-tuple-element.25), channel_id=1, source_target_pairs={{0,64},{16,80},{32,96},{48,112},{64,0},{80,16},{96,32},{112,48},{1... | collective-permute-start | bytes 442376 | tf_op jit(solution)/shard_map/ppermute | solution.py:260
  65.7 6.6 %collective-permute-start.4 = (f32[1,24,768]{2,1,0:T(8,128)S(1)}, f32[1,24,768]{2,1,0:T(8,128)S(1)}, u32[]{:S(2)}, u32[]{:S(2)}) collective-permute-start(f32[1,24,768]{2,1,0:T(8,128)S(1)} %get-tuple-element.27), channel_id=1, source_target_pairs={{0,256},{16,272},{32,288},{48,304},{64,320},{80,336},{96,352},{112... | collective-permute-start | bytes 221192 | tf_op jit(solution)/shard_map/ppermute | solution.py:260
  74.2 28.9 %all-to-all-start.1 = ((bf16[8,120,128]{2,1,0:T(8,128)(2,1)}), bf16[8,120,128]{2,1,0:T(8,128)(2,1)S(1)}, u32[]{:S(2)}, u32[]{:S(2)}) async-start(bf16[8,120,128]{2,1,0:T(8,128)(2,1)} %shard_map.92), calls=%async_computation.1 | async-start | bytes 491520 | tf_op jit(solution)/shard_map/all_to_all | solution.py:278

commit v4 on v2

--- a/solution.py
+++ b/solution.py
@@ -17,7 +17,7 @@
 ROWS1 = 168
 ROWS2 = 112
 ROWS3 = 16
-VMEM = pltpu.CompilerParams(vmem_limit_bytes=40 * 1024 * 1024)
+VMEM = pltpu.CompilerParams(vmem_limit_bytes=20 * 1024 * 1024)
 
 
 def dot00(a, b):
@@ -28,24 +28,34 @@
     return lax.dot_general(a, b, (((1,), (0,)), ((), ())), preferred_element_type=F32)
 
 
-def virtual_kernel(blocks, core, dens, coef, mine, other, weighted_rows, coef_rows):
-    weighted_rows[...] = jnp.zeros(weighted_rows.shape, BF)
-    coef_rows[...] = jnp.zeros(coef_rows.shape, BF)
+def virtual_kernel(
+    core, dens_in, coef_in, blocks_in, ints_in, amps_in,
+    mine, other, coef, ints, amps, acc, dens, blocks, sems,
+):
+    moves = [(blocks_in, blocks), (coef_in, coef), (dens_in, dens), (ints_in, ints), (amps_in, amps)]
+    copies = [pltpu.make_async_copy(*move, sems.at[i]) for i, move in enumerate(moves)]
+    for copy in copies:
+        copy.start()
+    acc[...] = jnp.zeros(acc.shape, F32)
+    for copy in copies[:3]:
+        copy.wait()
     for p in range(PAIRS):
         c = coef[p]
         weighted = dot00(dens[p], c).astype(BF)
+        product = dot00(c, weighted)
         for h in range(2):
-            at = pl.ds(pl.multiple_of(blocks[h, p] * 128, 128), 128)
-            weighted_rows[64 * p : 64 * p + 64, at] = weighted[:, 128 * h : 128 * h + 128]
-            coef_rows[64 * p : 64 * p + 64, at] = c[:, 128 * h : 128 * h + 128]
-    left = coef_rows[...]
-    other_half = pl.ds(pl.multiple_of(384 * (1 - core[0]), 128), 384)
-    other[...] = dot00(left, weighted_rows[:, other_half]).astype(BF)
-    my_half = pl.ds(pl.multiple_of(384 * core[0], 128), 384)
-    mine[...] = dot00(left, weighted_rows[:, my_half])
-
-
-def piece_kernel(ints, amps, coef, out, pieces, rounded, sems):
+            for k in range(2):
+                at = blocks[h, p] * 6 + blocks[k, p]
+                acc[at] = acc[at] + product[128 * h : 128 * h + 128, 128 * k : 128 * k + 128]
+    for i in range(6):
+        for j in range(3):
+            mine[3 * i + j] = acc[6 * i + j + 3 * core[0]]
+            other[3 * i + j] = acc[6 * i + j + 3 - 3 * core[0]].astype(BF)
+    for copy in copies[3:]:
+        copy.wait()
+
+
+def piece_kernel(ints, amps, coef, out, pieces):
     for p in range(PAIRS):
         three_index = dot00(amps[p], ints[p]).astype(BF)
         piece = dot00(coef[p], three_index)
@@ -54,18 +64,8 @@
                 pieces[pl.ds(4 * p + 2 * h + k, 128, 64), :] = piece[
                     128 * h : 128 * h + 128, 128 * k : 128 * k + 128
                 ]
-    copies = []
-    for i in range(8):
-        for g in range(8 * i, 8 * i + 8):
-            rounded[g] = pieces[128 * g : 128 * g + 128, :].astype(BF)
-        copies.append(
-            pltpu.make_async_copy(
-                rounded.at[8 * i : 8 * i + 8], out.at[8 * i : 8 * i + 8, 0:128], sems.at[i]
-            )
-        )
-        copies[-1].start()
-    for copy in copies:
-        copy.wait()
+    for g in range(GROUP):
+        out[g, 0:128, :] = pieces[128 * g : 128 * g + 128, :].astype(BF)
 
 
 def rest_kernel(blocks, owners, offsets, filled, mine, other, out, rows, sem):
@@ -84,10 +84,14 @@
     top = sub < 4
     labels = jnp.where(sub == 4, slice_row, jnp.where(sub == 5, block_row, offset_row))
     for i in range(GROUP // 2):
-        both = mine[24 * i : 24 * i + 24, :] + other[24 * i : 24 * i + 24, :].astype(F32)
-        first = [both[0:8, 128 * j : 128 * j + 128] for j in range(3)]
-        mid = [both[8:16, 128 * j : 128 * j + 128] for j in range(3)]
-        last = [both[16:24, 128 * j : 128 * j + 128] for j in range(3)]
+        first, mid, last = (
+            [
+                mine[3 * (row // 128) + j, row % 128 : row % 128 + 8, :]
+                + other[3 * (row // 128) + j, row % 128 : row % 128 + 8, :].astype(F32)
+                for j in range(3)
+            ]
+            for row in (24 * i, 24 * i + 8, 24 * i + 16)
+        )
         moved = [pltpu.roll(m, 4, 0) for m in mid]
         even = first + [jnp.where(top, mid[0], moved[1]), jnp.where(top, mid[2], labels)]
         odd = last + [jnp.where(top, moved[0], mid[1]), jnp.where(top, moved[2], labels)]
@@ -186,26 +190,25 @@
     return pltpu.with_memory_space_constraint(x, pltpu.VMEM)
 
 
-def call(body, ins, outs, scalars, scratch=(), in_place=None, anywhere=False):
+def in_hbm(x):
+    return pltpu.with_memory_space_constraint(x, pltpu.HBM)
+
+
+def call(body, ins, outs, scalars=(), scratch=(), held=(), in_place=None):
     smem = pl.BlockSpec(memory_space=pltpu.SMEM)
     vmem = pl.BlockSpec(memory_space=pltpu.VMEM)
-    hbm = pl.BlockSpec(memory_space=pl.ANY)
-    in_specs = [smem] * len(scalars) + [vmem] * len(ins)
-    operands = [*scalars, *ins]
-    aliases = {}
-    if in_place is not None:
-        in_specs.insert(len(scalars), hbm)
-        operands.insert(len(scalars), in_place)
-        aliases = {len(scalars): 0}
+    hbm = pl.BlockSpec(memory_space=pltpu.HBM)
+    some = pl.BlockSpec(memory_space=pl.ANY)
+    lead = [] if in_place is None else [in_place]
     return pl.pallas_call(
         body,
-        in_specs=in_specs,
-        out_specs=[hbm if anywhere else vmem] * len(outs),
+        in_specs=[smem] * len(scalars) + [some] * len(lead) + [hbm] * len(held) + [vmem] * len(ins),
+        out_specs=[some if lead else vmem] * len(outs),
         out_shape=outs,
         scratch_shapes=scratch,
-        input_output_aliases=aliases,
+        input_output_aliases={len(scalars): 0} if lead else {},
         compiler_params=VMEM,
-    )(*operands)
+    )(*scalars, *lead, *map(in_hbm, held), *map(in_vmem, ins))
 
 
 def on_device(integrals, amplitudes, pno_density, pno_coef, pao_blocks, aux_slice, aux_offset):
@@ -213,27 +216,38 @@
     low = lax.axis_index("low")
     scale = 1.0 / math.sqrt(PAIRS * 32)
     sds = jax.ShapeDtypeStruct
-    coef = jnp.swapaxes(pno_coef, 1, 2)
     blocks = pao_blocks.T
-    mine, other = call(
+    mine, other, coef, ints, amps = call(
         virtual_kernel,
-        [pno_density, coef],
-        [sds((768, 384), F32), sds((768, 384), BF)],
-        [blocks, (pair % 2).reshape(1)],
-        [pltpu.VMEM((1024, 768), BF), pltpu.VMEM((1024, 768), BF)],
+        [],
+        [
+            sds((18, 128, 128), F32),
+            sds((18, 128, 128), BF),
+            sds((PAIRS, 64, 256), BF),
+            sds((PAIRS, 64, 256), BF),
+            sds((PAIRS, 64, 64), BF),
+        ],
+        [(pair % 2).reshape(1)],
+        [
+            pltpu.VMEM((36, 128, 128), F32),
+            pltpu.VMEM((PAIRS, 64, 64), BF),
+            pltpu.SMEM((2, PAIRS), jnp.int32),
+            pltpu.SemaphoreType.DMA((5,)),
+        ],
+        held=[
+            pno_density,
+            jnp.swapaxes(pno_coef, 1, 2),
+            blocks,
+            jnp.swapaxes(integrals, 1, 2),
+            amplitudes,
+        ],
     )
     other = lax.ppermute(other, "pair", [(i, i ^ 1) for i in range(32)])
     (filled,) = call(
         piece_kernel,
-        [jnp.swapaxes(integrals, 1, 2), amplitudes, coef],
+        [ints, amps, coef],
         [sds((GROUP, ROWS1, 128), BF)],
-        [],
-        [
-            pltpu.VMEM((8192, 128), F32),
-            pltpu.VMEM((GROUP, 128, 128), BF),
-            pltpu.SemaphoreType.DMA((8,)),
-        ],
-        anywhere=True,
+        scratch=[pltpu.VMEM((8192, 128), F32)],
     )
     (sent,) = call(
         rest_kernel,
@@ -242,12 +256,11 @@
         [blocks, aux_slice.T, aux_offset.T],
         [pltpu.VMEM((GROUP, ROWS1 - 128, 128), BF), pltpu.SemaphoreType.DMA(())],
         in_place=filled,
-        anywhere=True,
     )
     got = lax.all_to_all(sent, ("pair", "low"), split_axis=0, concat_axis=0, tiled=True)
     (sent,) = call(
         place_kernel,
-        [in_vmem(got)],
+        [got],
         [sds((8, ROWS2, 128), BF)],
         [],
         [pltpu.VMEM((384, 4096), BF), pltpu.VMEM((384, 256), F32)],
@@ -255,14 +268,14 @@
     got = lax.all_to_all(sent, "high", split_axis=0, concat_axis=0, tiled=True)
     (sent,) = call(
         column_kernel,
-        [in_vmem(got)],
+        [got],
         [sds((GROUP, ROWS3, 128), BF)],
         [(2 * pair + low).reshape(1)],
     )
     got = lax.all_to_all(sent, ("pair", "low"), split_axis=0, concat_axis=0, tiled=True)
     aux, virt = call(
         lambda *refs: final_kernel(*refs, scale=scale),
-        [in_vmem(got)],
+        [got],
         [sds((24, 512), F32), sds((24, 48), F32)],
         [pair.reshape(1)],
     )

time: 114 us -> 108 us (0.947)
  local copies, waits for them, and re-layouts: 5.71 us -> 0.01 us
    unnamed x18 -> x6, local copies, waits for them, and re-layouts: 5.71 us -> 0.01 us
where the time goes in v4:
time: 108 us
  blocking collectives  57.2 us (53%)
  starting transfers between devices  22.7 us (21%)
  waiting for transfers between devices  16.7 us (15%)
  Pallas kernels  10.8 us (10%)
    all_to_all x2, blocking collectives, on_device(): lax.all_to_all(sent, ('pair', 'low'), split_axis=0, concat_axis=0, tiled=...  57.2 us
    all_to_all x1, waiting for transfers between devices, on_device(): got = lax.all_to_all(sent, 'high', split_axis=0, concat_axis=0, tiled=True)  16.7 us
    all_to_all x1, starting transfers between devices, on_device(): got = lax.all_to_all(sent, 'high', split_axis=0, concat_axis=0, tiled=True)  13.9 us
    pallas_call x6, Pallas kernels, call(): pl.pallas_call(body, in_specs=[smem] * len(scalars) + [some] * len(lead)...  10.8 us
    ppermute x1, starting transfers between devices, on_device(): other = lax.ppermute(other, 'pair', [(i, i ^ 1) for i in range(32)])  8.78 us
  transfers between devices with their start and end apart: 2, of which 1 were waited for; matrix products, arithmetic and copies ran while one was open for 0% of the time, Pallas kernels for 4%

profile of v4, /device:TPU:1, one launch (start us, length us, event | category | flops | bytes accessed | tf_op | source)
XLA Modules:
  0.0 108.1 jit_solution(2392512245908503759)
XLA Ops:
  0.6 0.0 copy-start
  0.7 0.0 copy-start.1
  0.7 0.0 copy-start.2
  0.7 3.3 %shard_map.86 = (f32[18,128,128]{2,1,0:T(8,128)S(1)}, bf16[18,128,128]{2,1,0:T(8,128)(2,1)S(1)}, bf16[16,64,256]{2,1,0:T(8,128)(2,1)S(1)}, bf16[16,64,256]{2,1,0:T(8,128)(2,1)S(1)}, bf16[16,64,64]{2,1,0:T(8,128)(2,1)S(1)}) custom-call(s32[1]{0:T(128)} %bitcast.5.core, bf16[16,64,64]{2,1,0:T(8,128)(2,1)} %dens_in.1, bf16[16,64,256]{2,1,0:T(8,128)(2,1)} %bitcast.14, ...), custom_call_target="tpu_custom_call" | custom-call | tf_op jit(solution)/shard_map/pallas_call | solution.py:203
  4.0 8.8 %collective-permute-start = (bf16[18,128,128]{2,1,0:T(8,128)(2,1)S(1)}, bf16[18,128,128]{2,1,0:T(8,128)(2,1)S(1)}, u32[]{:S(2)}, u32[]{:S(2)}) collective-permute-start(bf16[18,128,128]{2,1,0:T(8,128)(2,1)S(1)} %get-tuple-element.13), channel_id=1, source_target_pairs={{0,16},{16,0},{32,48},{48,32},{64,80},{80,64},{96,112},{112,96},{1... | collective-permute-start | bytes 1769480 | tf_op jit(solution)/shard_map/ppermute | solution.py:245
  12.8 3.9 %shard_map.87.filled = bf16[64,168,128]{2,1,0:T(8,128)(2,1)S(1)} custom-call(bf16[16,64,256]{2,1,0:T(8,128)(2,1)S(1)} %get-tuple-element.9.ints, bf16[16,64,64]{2,1,0:T(8,128)(2,1)S(1)} %get-tuple-element.10.amps, bf16[16,64,256]{2,1,0:T(8,128)(2,1)S(1)} %get-tuple-element.11.coef), custom_call_target="tpu_custom_call" | custom-call | tf_op jit(solution)/shard_map/pallas_call | solution.py:203
  16.7 0.0 collective-permute-done.other
  16.7 0.0 copy-done
  16.7 0.0 copy-done.1
  16.8 0.0 copy-done.2
  16.8 0.9 shard_map.88
  17.6 39.1 %all_to_all.15.got = bf16[64,168,128]{2,1,0:T(8,128)(2,1)S(1)} all-to-all(bf16[64,168,128]{2,1,0:T(8,128)(2,1)S(1)} %shard_map.88), channel_id=1, replica_groups=mesh['pair'=32,'high'=8,'low'=2] {'pair','low'}, dimensions={0} | all-to-all | bytes 5505024 | tf_op jit(solution)/shard_map/all_to_all | solution.py:260
  56.8 1.9 %shard_map.89 = bf16[8,112,128]{2,1,0:T(8,128)(2,1)} custom-call(bf16[64,168,128]{2,1,0:T(8,128)(2,1)S(1)} %all_to_all.15.got), custom_call_target="tpu_custom_call" | custom-call | tf_op jit(solution)/shard_map/pallas_call | solution.py:203
  58.7 13.9 %all-to-all-start.1 = ((bf16[8,112,128]{2,1,0:T(8,128)(2,1)}), bf16[8,112,128]{2,1,0:T(8,128)(2,1)S(1)}, u32[]{:S(2)}, u32[]{:S(2)}) async-start(bf16[8,112,128]{2,1,0:T(8,128)(2,1)} %shard_map.89), calls=%async_computation.1 | async-start | bytes 458752 | tf_op jit(solution)/shard_map/all_to_all | solution.py:268
  72.6 16.7 %all-to-all-done.1.got = bf16[8,112,128]{2,1,0:T(8,128)(2,1)S(1)} async-done(((bf16[8,112,128]{2,1,0:T(8,128)(2,1)}), bf16[8,112,128]{2,1,0:T(8,128)(2,1)S(1)}, u32[]{:S(2)}, u32[]{:S(2)}) %all-to-all-start.1) | async-done | bytes 229408 | tf_op jit(solution)/shard_map/all_to_all | solution.py:268
  89.3 0.1 shard_map.90
  89.4 18.0 %all_to_all.16.refs_1_ = bf16[64,16,128]{2,1,0:T(8,128)(2,1)S(1)} all-to-all(bf16[64,16,128]{2,1,0:T(8,128)(2,1)S(1)} %shard_map.90), channel_id=1, replica_groups=mesh['pair'=32,'high'=8,'low'=2] {'pair','low'}, dimensions={0} | all-to-all | bytes 524288 | tf_op jit(solution)/shard_map/all_to_all | solution.py:275
  107.4 0.7 shard_map.91
Async XLA Ops:
  0.6 16.1 %copy-start = (s32[16,2]{0,1:T(2,128)S(1)}, s32[16,2]{0,1:T(2,128)}, u32[]{:S(2)}) copy-start(s32[16,2]{0,1:T(2,128)} %param.11) | copy-start | bytes 388
  0.7 16.1 %copy-start.1 = (s32[16,2]{0,1:T(2,128)S(1)}, s32[16,2]{0,1:T(2,128)}, u32[]{:S(2)}) copy-start(s32[16,2]{0,1:T(2,128)} %param.12) | copy-start | bytes 388
  0.7 16.1 %copy-start.2 = (s32[16,2]{0,1:T(2,128)S(1)}, s32[16,2]{0,1:T(2,128)}, u32[]{:S(2)}) copy-start(s32[16,2]{0,1:T(2,128)} %param.13) | copy-start | bytes 388
  4.0 12.7 %collective-permute-start = (bf16[18,128,128]{2,1,0:T(8,128)(2,1)S(1)}, bf16[18,128,128]{2,1,0:T(8,128)(2,1)S(1)}, u32[]{:S(2)}, u32[]{:S(2)}) collective-permute-start(bf16[18,128,128]{2,1,0:T(8,128)(2,1)S(1)} %get-tuple-element.13), channel_id=1, source_target_pairs={{0,16},{16,0},{32,48},{48,32},{64,80},{80,64},{96,112},{112,96},{1... | collective-permute-start | bytes 1769480 | tf_op jit(solution)/shard_map/ppermute | solution.py:245
  58.7 30.6 %all-to-all-start.1 = ((bf16[8,112,128]{2,1,0:T(8,128)(2,1)}), bf16[8,112,128]{2,1,0:T(8,128)(2,1)S(1)}, u32[]{:S(2)}, u32[]{:S(2)}) async-start(bf16[8,112,128]{2,1,0:T(8,128)(2,1)} %shard_map.89), calls=%async_computation.1 | async-start | bytes 458752 | tf_op jit(solution)/shard_map/all_to_all | solution.py:268

commit v5 on v4

v5 whole, which is shorter than its diff:
```python
import math

import jax
import jax.numpy as jnp
import numpy as np
from jax import lax
from jax.experimental import pallas as pl
from jax.experimental.pallas import tpu as pltpu
from jax.sharding import Mesh
from jax.sharding import PartitionSpec as P

NBLK = 6
ABPO = 4
BF = jnp.bfloat16
F32 = jnp.float32
PAIRS = 16
GROUP = 64
ROWS1 = 168
MEMBERS = 128


def tables():
    spare = {12: 0, 15: 1, 13: 2, 14: 3}, {0: 1, 14: 2, 1: 0, 15: 3}, {0: 2, 13: 3, 14: 0, 15: 1}
    octets = np.zeros((6, 16), np.int32)
    owner = np.zeros((32, 8), np.int32)
    content = np.full((16, 8), 6, np.int32)
    for half in range(2):
        for b in range(3):
            block, left = 3 * half + b, 3 - b
            others = [t for t in range(4) if t != left]
            for o in range(16):
                p = (64 * block + 4 * o) // 12
                if o in spare[b]:
                    octets[block, o] = 4 * spare[b][o] + left
                else:
                    rank = (64 * block + 4 * o - 12 * p) // 4
                    octets[block, o] = 4 * (p % 4) + others[rank]
                    owner[p] = others + [0, 0, left, half, 0]
                    for t in others:
                        content[4 * (p % 4) + t, p // 4] = block
        special = {
            4: [3, 4, 5, 2, 1, 0, half, 0],
            5: [3, 2, 4, 1, 0, 0, half, 0],
            10: [2, 4, 1, 3, 0, 0, half, 0],
            15: [1, 5, 4, 2, 3, 0, half, 0],
        }
        for p, row in special.items():
            owner[p + 16 * half] = row
            for t in range(1, 4):
                content[4 * (p % 4) + t, (p + 16 * half) // 4] = 3 * half + 3 - t
    return octets, owner, content


OCTETS, OWNER, CONTENT = tables()
ROUND1 = [(a + h, b + h) for h in (0, 16) for a, b in ((4, 5), (5, 15), (10, 4), (15, 10))]
ROUND2 = [(a + h, b + h) for h in (0, 16) for a, b in ((4, 15), (15, 4))]
VMEM = pltpu.CompilerParams(vmem_limit_bytes=20 * 1024 * 1024)


def dot00(a, b):
    return lax.dot_general(a, b, (((0,), (0,)), ((), ())), preferred_element_type=F32)


def dot10(a, b):
    return lax.dot_general(a, b, (((1,), (0,)), ((), ())), preferred_element_type=F32)


def virtual_kernel(
    core, dens_in, coef_in, blocks_in, ints_in, amps_in,
    mine, other, coef, ints, amps, acc, dens, blocks, sems,
):
    moves = [(blocks_in, blocks), (coef_in, coef), (dens_in, dens), (ints_in, ints), (amps_in, amps)]
    copies = [pltpu.make_async_copy(*move, sems.at[i]) for i, move in enumerate(moves)]
    for copy in copies:
        copy.start()
    acc[...] = jnp.zeros(acc.shape, F32)
    for copy in copies[:3]:
        copy.wait()
    for p in range(PAIRS):
        c = coef[p]
        weighted = dot00(dens[p], c).astype(BF)
        product = dot00(c, weighted)
        for h in range(2):
            for k in range(2):
                at = blocks[h, p] * 6 + blocks[k, p]
                acc[at] = acc[at] + product[128 * h : 128 * h + 128, 128 * k : 128 * k + 128]
    for i in range(6):
        for j in range(3):
            mine[3 * i + j] = acc[6 * i + j + 3 * core[0]]
            other[3 * i + j] = acc[6 * i + j + 3 - 3 * core[0]].astype(BF)
    for copy in copies[3:]:
        copy.wait()


def piece_kernel(blocks, octets, ints, amps, coef, out, pieces):
    for p in range(PAIRS):
        three_index = dot00(amps[p], ints[p]).astype(BF)
        piece = dot00(coef[p], three_index)
        for h in range(2):
            block = blocks[h, p]
            for o in range(16):
                start = octets[block, o] * 512 + 4 * p + 2 * h
                for k in range(2):
                    pieces[pl.ds(start + k, 8, 64), :] = piece[
                        128 * h + 8 * o : 128 * h + 8 * o + 8, 128 * k : 128 * k + 128
                    ]
    for g in range(GROUP):
        high, low = g // 8, g % 8
        at = (4 * (low // 2) + high // 2) * 512 + (2 * (high % 2) + low % 2) * 128
        out[g, 0:128, :] = pieces[at : at + 128, :].astype(BF)


def rest_kernel(blocks, owners, offsets, filled, mine, other, out, rows, sem):
    lane = lax.broadcasted_iota(jnp.int32, (1, 128), 1) % 64
    slice_row = jnp.zeros((1, 128), F32)
    block_row = jnp.zeros((1, 128), F32)
    offset_row = jnp.zeros((1, 128), F32)
    for p in range(PAIRS):
        for h in range(2):
            for k in range(2):
                here = lane == 4 * p + 2 * h + k
                slice_row = jnp.where(here, owners[k, p].astype(F32), slice_row)
                block_row = jnp.where(here, blocks[h, p].astype(F32), block_row)
                offset_row = jnp.where(here, offsets[k, p].astype(F32), offset_row)
    sub = lax.broadcasted_iota(jnp.int32, (8, 128), 0)
    top = sub < 4
    labels = jnp.where(sub == 4, slice_row, jnp.where(sub == 5, block_row, offset_row))
    for i in range(GROUP // 2):
        first, mid, last = (
            [
                mine[3 * (row // 128) + j, row % 128 : row % 128 + 8, :]
                + other[3 * (row // 128) + j, row % 128 : row % 128 + 8, :].astype(F32)
                for j in range(3)
            ]
            for row in (24 * i, 24 * i + 8, 24 * i + 16)
        )
        moved = [pltpu.roll(m, 4, 0) for m in mid]
        even = first + [jnp.where(top, mid[0], moved[1]), jnp.where(top, mid[2], labels)]
        odd = last + [jnp.where(top, moved[0], mid[1]), jnp.where(top, moved[2], labels)]
        to = 2 * (4 * (2 * int(OWNER[i, 5]) + int(OWNER[i, 6])) + i % 4)
        rows[to] = jnp.concatenate(even, 0).astype(BF)
        rows[to + 1] = jnp.concatenate(odd, 0).astype(BF)
    copy = pltpu.make_async_copy(rows, out.at[:, 128:ROWS1], sem)
    copy.start()
    copy.wait()


def place_kernel(place, content, got, out, hot, acc, tiles):
    lane = lax.broadcasted_iota(jnp.int32, (1, 128), 1)
    cell = lax.broadcasted_iota(jnp.int32, (384, 128), 0)
    for i in range(GROUP // 2):
        first = got[2 * i, 160:168, :].astype(F32)
        second = got[2 * i + 1, 160:168, :].astype(F32)
        both = jnp.where(lane < 64, first, second)
        target = both[4:5] * 24.0 + both[5:6] * 4.0 + both[6:7]
        hot[:, 128 * i : 128 * i + 128] = (cell == target.astype(jnp.int32)).astype(BF)
    data = jnp.concatenate(
        [got[:, 0:64, :].reshape(4096, 128), got[:, 64:128, :].reshape(4096, 128)], 1
    )
    acc[...] = dot10(hot[...], data)
    top = lax.broadcasted_iota(jnp.int32, (8, 128), 0) < 4
    for z in range(16):
        for i in range(3):
            a = acc[24 * z + 8 * i : 24 * z + 8 * i + 8, 0:128]
            b = acc[24 * z + 8 * i : 24 * z + 8 * i + 8, 128:256]
            tiles[7 * z + 2 * i] = jnp.where(top, a, pltpu.roll(b, 4, 0))
            tiles[7 * z + 2 * i + 1] = jnp.where(top, pltpu.roll(a, 4, 0), b)
    wide = lax.broadcasted_iota(jnp.int32, (8, 128), 1)
    for half in range(2):
        mine = [g for g in range(GROUP) if (g // 2) % 2 == half]
        total = got[mine[0], 128:168, :].astype(F32)
        for g in mine[1:]:
            total = total + got[g, 128:168, :].astype(F32)
        whole = [total[0:8], total[8:16], total[16:24]]
        part = [total[24:32], pltpu.roll(total[24:32], 4, 0), total[32:40]]
        for m in range(8):
            at, off = (48 * m) // 128, (48 * m) % 128
            cut = 128 - off
            ends = []
            for group, base in ((whole, 0), (part, 64)):
                shift = (base - off) % 128
                end = pltpu.roll(group[at], shift, 1) if shift else group[at]
                if cut < 48:
                    beyond = pltpu.roll(group[at + 1], shift, 1) if shift else group[at + 1]
                    end = jnp.where(wide < base + cut, end, beyond)
                ends.append(end)
            tiles[7 * (8 * half + m) + 6] = jnp.where(wide < 64, ends[0], ends[1])
    for q in range(8):
        which = content[place[0], q]
        for z in range(16):
            out[16 * q + z] = tiles[7 * z + which].astype(BF)


def sum_kernel(place, owner, got, sums, first, second, virt_out, *, scale):
    p = place[0]
    for i in range(16):
        total = got[16 * (i // 2) + i % 2].astype(F32)
        for z in range(1, 8):
            total = total + got[16 * (i // 2) + 2 * z + i % 2].astype(F32)
        sums[i] = total * scale
    for j in range(4):
        first[j] = sums[4 * owner[p, 3] + j]
        second[j] = sums[4 * owner[p, 4] + j]
    sub = lax.broadcasted_iota(jnp.int32, (8, 128), 0)
    at = 4 * owner[p, 5] + 2 * owner[p, 6]
    even, odd = sums[at], sums[at + 1]
    mid = jnp.where(sub < 4, pltpu.roll(even, 64, 1), pltpu.roll(pltpu.roll(odd, 64, 1), 4, 0))
    virt_out[0:8, :] = even[:, 0:48]
    virt_out[8:16, :] = mid[:, 0:48]
    virt_out[16:24, :] = odd[:, 0:48]


def final_kernel(place, owner, sums, first, second, aux_out, stack):
    p = place[0]
    stack[0:16] = sums[...]
    stack[16:20] = first[...]
    stack[20:24] = second[...]
    for r in range(3):
        at = 4 * owner[p, r]
        for j in range(4):
            tile = stack[at + j]
            for y in range(2):
                row = 8 * r + 2 * j + y
                for o in range(ABPO):
                    aux_out[row : row + 1, 128 * o : 128 * o + 128] = tile[
                        4 * y + o : 4 * y + o + 1
                    ]


def in_vmem(x):
    return pltpu.with_memory_space_constraint(x, pltpu.VMEM)


def in_hbm(x):
    return pltpu.with_memory_space_constraint(x, pltpu.HBM)


def call(body, ins, outs, scalars=(), scratch=(), held=(), in_place=None):
    smem = pl.BlockSpec(memory_space=pltpu.SMEM)
    vmem = pl.BlockSpec(memory_space=pltpu.VMEM)
    hbm = pl.BlockSpec(memory_space=pltpu.HBM)
    some = pl.BlockSpec(memory_space=pl.ANY)
    lead = [] if in_place is None else [in_place]
    return pl.pallas_call(
        body,
        in_specs=[smem] * len(scalars) + [some] * len(lead) + [hbm] * len(held) + [vmem] * len(ins),
        out_specs=[some if lead else vmem] * len(outs),
        out_shape=outs,
        scratch_shapes=scratch,
        input_output_aliases={len(scalars): 0} if lead else {},
        compiler_params=VMEM,
    )(*scalars, *lead, *map(in_hbm, held), *map(in_vmem, ins))


def on_device(integrals, amplitudes, pno_density, pno_coef, pao_blocks, aux_slice, aux_offset):
    pair_high = lax.axis_index("pair_high")
    pair_low = lax.axis_index("pair_low")
    pair = 4 * pair_high + pair_low
    both = ("pair_high", "pair_low")
    scale = 1.0 / math.sqrt(PAIRS * 32)
    sds = jax.ShapeDtypeStruct
    blocks = pao_blocks.T
    mine, other, coef, ints, amps = call(
        virtual_kernel,
        [],
        [
            sds((18, 128, 128), F32),
            sds((18, 128, 128), BF),
            sds((PAIRS, 64, 256), BF),
            sds((PAIRS, 64, 256), BF),
            sds((PAIRS, 64, 64), BF),
        ],
        [(pair % 2).reshape(1)],
        [
            pltpu.VMEM((36, 128, 128), F32),
            pltpu.VMEM((PAIRS, 64, 64), BF),
            pltpu.SMEM((2, PAIRS), jnp.int32),
            pltpu.SemaphoreType.DMA((5,)),
        ],
        held=[
            pno_density,
            jnp.swapaxes(pno_coef, 1, 2),
            blocks,
            jnp.swapaxes(integrals, 1, 2),
            amplitudes,
        ],
    )
    other = lax.ppermute(other, both, [(i, i ^ 1) for i in range(32)])
    (filled,) = call(
        piece_kernel,
        [ints, amps, coef],
        [sds((GROUP, ROWS1, 128), BF)],
        [blocks, jnp.asarray(OCTETS)],
        scratch=[pltpu.VMEM((8192, 128), F32)],
    )
    (sent,) = call(
        rest_kernel,
        [mine, other],
        [sds((GROUP, ROWS1, 128), BF)],
        [blocks, aux_slice.T, aux_offset.T],
        [pltpu.VMEM((GROUP, ROWS1 - 128, 128), BF), pltpu.SemaphoreType.DMA(())],
        in_place=filled,
    )
    got = lax.all_to_all(sent, (*both, "low"), split_axis=0, concat_axis=0, tiled=True)
    (sent,) = call(
        place_kernel,
        [got],
        [sds((MEMBERS, 8, 128), BF)],
        [(4 * pair_low + pair_high // 2).reshape(1), jnp.asarray(CONTENT)],
        [
            pltpu.VMEM((384, 4096), BF),
            pltpu.VMEM((384, 256), F32),
            pltpu.VMEM((112, 8, 128), F32),
        ],
    )
    axes = ("pair_high", "high", "low")
    got = lax.all_to_all(sent, axes, split_axis=0, concat_axis=0, tiled=True)
    place = [pair.reshape(1), jnp.asarray(OWNER)]
    parcel = sds((4, 8, 128), F32)
    sums, first, second, virt = call(
        lambda *refs: sum_kernel(*refs, scale=scale),
        [got],
        [sds((16, 8, 128), F32), parcel, parcel, sds((24, 48), F32)],
        place,
    )
    first = lax.ppermute(first, both, ROUND1)
    second = lax.ppermute(second, both, ROUND2)
    (aux,) = call(
        final_kernel,
        [sums, first, second],
        [sds((24, 512), F32)],
        place,
        [pltpu.VMEM((24, 8, 128), F32)],
    )
    return aux.T, virt.T


def solution(mesh):
    names = ("pair_high", "pair_low", "high", "low")
    split = Mesh(mesh.devices.reshape(8, 4, 8, 2), names)
    in_specs = (P(names, None, None),) * 4 + (P(names, None),) * 3
    out_specs = (P(("high", "low"), ("pair_high", "pair_low")),) * 2
    return jax.shard_map(
        on_device, mesh=split, in_specs=in_specs, out_specs=out_specs, check_vma=False
    )
```

time: 108 us -> 117 us (1.083)
  the two profiles are of different devices: /device:TPU:1 before, /device:TPU:15 now
where the time goes in v5:
time: 117 us
  blocking collectives  39.8 us (34%)
  waiting for transfers between devices  37.3 us (32%)
  starting transfers between devices  21.4 us (18%)
  Pallas kernels  16.2 us (14%)
  local copies, waits for them, and re-layouts  1.38 us (1%)
    all_to_all x1, blocking collectives, on_device(): got = lax.all_to_all(sent, axes, split_axis=0, concat_axis=0, tiled=True)  39.8 us
    all_to_all x1, waiting for transfers between devices, on_device(): lax.all_to_all(sent, (*both, 'low'), split_axis=0, concat_axis=0, tiled=T...  33.3 us
    pallas_call x6, Pallas kernels, call(): pl.pallas_call(body, in_specs=[smem] * len(scalars) + [some] * len(lead)...  16.2 us
    all_to_all x1, starting transfers between devices, on_device(): lax.all_to_all(sent, (*both, 'low'), split_axis=0, concat_axis=0, tiled=T...  9.74 us
    ppermute x1, starting transfers between devices, on_device(): first = lax.ppermute(first, both, ROUND1)  7.14 us
    ppermute x1, waiting for transfers between devices, on_device(): second = lax.ppermute(second, both, ROUND2)  4.02 us
    ppermute x1, starting transfers between devices, on_device(): other = lax.ppermute(other, both, [(i, i ^ 1) for i in range(32)])  2.58 us
  transfers between devices with their start and end apart: 4, of which 2 were waited for; matrix products, arithmetic and copies ran while one was open for 0% of the time, Pallas kernels for 5%

profile of v5, /device:TPU:15, one launch (start us, length us, event | category | flops | bytes accessed | tf_op | source)
XLA Modules:
  0.0 116.8 jit_solution(3572249766881476804)
XLA Ops:
  0.6 0.0 copy-start.4
  0.7 0.0 copy-start.5
  0.7 3.3 %shard_map.113 = (f32[18,128,128]{2,1,0:T(8,128)S(1)}, bf16[18,128,128]{2,1,0:T(8,128)(2,1)S(1)}, bf16[16,64,256]{2,1,0:T(8,128)(2,1)S(1)}, bf16[16,64,256]{2,1,0:T(8,128)(2,1)S(1)}, bf16[16,64,64]{2,1,0:T(8,128)(2,1)S(1)}) custom-call(s32[1]{0:T(128)} %bitcast.5.core, bf16[16,64,64]{2,1,0:T(8,128)(2,1)} %dens_in.1, bf16[16,64,256]{2,1,0:T(8,128)(2,1)} %bitcast.15, ...), custom_call_target="tpu_custom_call" | custom-call | tf_op jit(solution)/shard_map/pallas_call | solution.py:244
  4.0 2.6 %collective-permute-start = (bf16[18,128,128]{2,1,0:T(8,128)(2,1)S(1)}, bf16[18,128,128]{2,1,0:T(8,128)(2,1)S(1)}, u32[]{:S(2)}, u32[]{:S(2)}) collective-permute-start(bf16[18,128,128]{2,1,0:T(8,128)(2,1)S(1)} %get-tuple-element.15), channel_id=1, source_target_pairs={{0,16},{16,0},{32,48},{48,32},{64,80},{80,64},{96,112},{112,96},{1... | collective-permute-start | bytes 1769480 | tf_op jit(solution)/shard_map/ppermute | solution.py:288
  6.6 0.0 copy-start.1
  6.6 0.7 copy-done.1
  7.3 0.0 copy-start.3
  7.3 0.7 copy-done.3
  8.0 6.2 %shard_map.114.filled = bf16[64,168,128]{2,1,0:T(8,128)(2,1)} custom-call(s32[2,16]{1,0:T(2,128)S(1)} %bitcast.11, s32[6,16]{1,0:T(8,128)S(1)} %copy-done.3, bf16[16,64,256]{2,1,0:T(8,128)(2,1)S(1)} %get-tuple-element.11.ints, bf16[16,64,64]{2,1,0:T(8,128)(2,1)S(1)} %get-tuple-element.12.amps, bf16[16,64,256]{2,1,0:T(8,128)(2,1)S(1)} %get-tuple-element.13.coef), custom_call_target="tpu_custom_call" | custom-call | tf_op jit(solution)/shard_map/pallas_call | solution.py:244
  14.2 0.0 collective-permute-done.other
  14.2 0.0 copy-done.4
  14.2 0.0 copy-done.5
  14.2 1.7 %shard_map.115 = bf16[64,168,128]{2,1,0:T(8,128)(2,1)} custom-call(s32[2,16]{1,0:T(2,128)S(1)} %bitcast.12, s32[2,16]{1,0:T(2,128)S(1)} %bitcast.13, s32[2,16]{1,0:T(2,128)S(1)} %bitcast.14, bf16[64,168,128]{2,1,0:T(8,128)(2,1)} %shard_map.114.filled, f32[18,128,128]{2,1,0:T(8,128)S(1)} %get-tuple-element.14.mine, ...), custom_call_target="tpu_custom_call", output_to_operand_aliasing={{}: (3, {})} | custom-call | tf_op jit(solution)/shard_map/pallas_call | solution.py:244
  15.9 0.0 copy-start.2
  15.9 9.7 %all-to-all-start = ((bf16[64,168,128]{2,1,0:T(8,128)(2,1)}), bf16[64,168,128]{2,1,0:T(8,128)(2,1)S(1)}, u32[]{:S(2)}, u32[]{:S(2)}) async-start(bf16[64,168,128]{2,1,0:T(8,128)(2,1)} %shard_map.115), calls=%async_computation | async-start | bytes 5505024 | tf_op jit(solution)/shard_map/all_to_all | solution.py:304
  25.7 0.0 copy-start
  25.7 33.3 %all-to-all-done.got = bf16[64,168,128]{2,1,0:T(8,128)(2,1)S(1)} async-done(((bf16[64,168,128]{2,1,0:T(8,128)(2,1)}), bf16[64,168,128]{2,1,0:T(8,128)(2,1)S(1)}, u32[]{:S(2)}, u32[]{:S(2)}) %all-to-all-start) | async-done | bytes 2752544 | tf_op jit(solution)/shard_map/all_to_all | solution.py:304
  59.0 0.0 copy-done.2
  59.0 2.0 %shard_map.116 = bf16[128,8,128]{2,1,0:T(8,128)(2,1)S(1)} custom-call(s32[1]{0:T(128)} %bitcast.1.place, s32[16,8]{1,0:T(8,128)S(1)} %copy-done.2, bf16[64,168,128]{2,1,0:T(8,128)(2,1)S(1)} %all-to-all-done.got), custom_call_target="tpu_custom_call" | custom-call | tf_op jit(solution)/shard_map/pallas_call | solution.py:244
  61.0 39.8 %all_to_all.10.refs_2_ = bf16[128,8,128]{2,1,0:T(8,128)(2,1)S(1)} all-to-all(bf16[128,8,128]{2,1,0:T(8,128)(2,1)S(1)} %shard_map.116), channel_id=1, replica_groups=mesh['pair_high'=8,'pair_low'=4,'high'=8,'low'=2] {'pair_high','high','l..., dimensions={0} | all-to-all | bytes 524288 | tf_op jit(solution)/shard_map/all_to_all | solution.py:317
  100.8 0.0 copy-done
  100.8 1.5 %shard_map.117 = (f32[16,8,128]{2,1,0:T(8,128)S(1)}, f32[4,8,128]{2,1,0:T(8,128)S(1)}, f32[4,8,128]{2,1,0:T(8,128)S(1)}, f32[24,48]{1,0:T(8,128)}) custom-call(s32[1]{0:T(128)} %bitcast.refs_0_.place, s32[32,8]{1,0:T(8,128)S(1)} %copy-done, bf16[128,8,128]{2,1,0:T(8,128)(2,1)S(1)} %all_to_all.10.refs_2_), custom_call_target="tpu_custom_call" | custom-call | tf_op jit(solution)/shard_map/pallas_call | solution.py:244
  102.3 7.1 %collective-permute-start.1 = (f32[4,8,128]{2,1,0:T(8,128)S(1)}, f32[4,8,128]{2,1,0:T(8,128)S(1)}, u32[]{:S(2)}, u32[]{:S(2)}) collective-permute-start(f32[4,8,128]{2,1,0:T(8,128)S(1)} %get-tuple-element.17), channel_id=1, source_target_pairs={{64,80},{80,240},{160,64},{240,160},{320,336},{336,496},{416,320},... | collective-permute-start | bytes 49160 | tf_op jit(solution)/shard_map/ppermute | solution.py:326
  109.4 1.9 %collective-permute-start.2 = (f32[4,8,128]{2,1,0:T(8,128)S(1)}, f32[4,8,128]{2,1,0:T(8,128)S(1)}, u32[]{:S(2)}, u32[]{:S(2)}) collective-permute-start(f32[4,8,128]{2,1,0:T(8,128)S(1)} %get-tuple-element.18), channel_id=1, source_target_pairs={{64,240},{240,64},{320,496},{496,320},{65,241},{241,65},{321,497},... | collective-permute-start | bytes 49160 | tf_op jit(solution)/shard_map/ppermute | solution.py:327
  111.4 0.0 collective-permute-done.1.first
  111.4 4.0 %collective-permute-done.2.second = f32[4,8,128]{2,1,0:T(8,128)S(1)} collective-permute-done((f32[4,8,128]{2,1,0:T(8,128)S(1)}, f32[4,8,128]{2,1,0:T(8,128)S(1)}, u32[]{:S(2)}, u32[]{:S(2)}) %collective-permute-start.2) | collective-permute-done | bytes 16416 | tf_op jit(solution)/shard_map/ppermute | solution.py:327
  115.4 1.5 %shard_map.118 = f32[24,512]{1,0:T(8,128)} custom-call(s32[1]{0:T(128)} %bitcast.refs_0_.place, s32[32,8]{1,0:T(8,128)S(1)} %copy-done, f32[16,8,128]{2,1,0:T(8,128)S(1)} %get-tuple-element.16.sums, f32[4,8,128]{2,1,0:T(8,128)S(1)} %collective-permute-done.1.first, f32[4,8,128]{2,1,0:T(8,128)S(1)} %collective-permute-done.2.second), custom_call_target="tpu_custom_call" | custom-call | tf_op jit(solution)/shard_map/pallas_call | solution.py:244
Async XLA Ops:
  0.6 13.6 %copy-start.4 = (s32[16,2]{0,1:T(2,128)S(1)}, s32[16,2]{0,1:T(2,128)}, u32[]{:S(2)}) copy-start(s32[16,2]{0,1:T(2,128)} %param.15) | copy-start | bytes 388
  0.7 13.5 %copy-start.5 = (s32[16,2]{0,1:T(2,128)S(1)}, s32[16,2]{0,1:T(2,128)}, u32[]{:S(2)}) copy-start(s32[16,2]{0,1:T(2,128)} %param.16) | copy-start | bytes 388
  4.0 10.2 %collective-permute-start = (bf16[18,128,128]{2,1,0:T(8,128)(2,1)S(1)}, bf16[18,128,128]{2,1,0:T(8,128)(2,1)S(1)}, u32[]{:S(2)}, u32[]{:S(2)}) collective-permute-start(bf16[18,128,128]{2,1,0:T(8,128)(2,1)S(1)} %get-tuple-element.15), channel_id=1, source_target_pairs={{0,16},{16,0},{32,48},{48,32},{64,80},{80,64},{96,112},{112,96},{1... | collective-permute-start | bytes 1769480 | tf_op jit(solution)/shard_map/ppermute | solution.py:288
  6.6 0.7 copy-start.1
  7.3 0.7 copy-start.3
  15.9 43.1 %copy-start.2 = (s32[16,8]{1,0:T(8,128)S(1)}, s32[16,8]{1,0:T(8,128)}, u32[]{:S(2)}) copy-start(s32[16,8]{1,0:T(8,128)} %constant.45.clone.content) | copy-start | bytes 1540
  15.9 43.1 %all-to-all-start = ((bf16[64,168,128]{2,1,0:T(8,128)(2,1)}), bf16[64,168,128]{2,1,0:T(8,128)(2,1)S(1)}, u32[]{:S(2)}, u32[]{:S(2)}) async-start(bf16[64,168,128]{2,1,0:T(8,128)(2,1)} %shard_map.115), calls=%async_computation | async-start | bytes 5505024 | tf_op jit(solution)/shard_map/all_to_all | solution.py:304
  25.7 75.1 %copy-start = (s32[32,8]{1,0:T(8,128)S(1)}, s32[32,8]{1,0:T(8,128)}, u32[]{:S(2)}) copy-start(s32[32,8]{1,0:T(8,128)} %constant.46.clone.refs_1_.owner) | copy-start | bytes 3076
  102.3 9.1 %collective-permute-start.1 = (f32[4,8,128]{2,1,0:T(8,128)S(1)}, f32[4,8,128]{2,1,0:T(8,128)S(1)}, u32[]{:S(2)}, u32[]{:S(2)}) collective-permute-start(f32[4,8,128]{2,1,0:T(8,128)S(1)} %get-tuple-element.17), channel_id=1, source_target_pairs={{64,80},{80,240},{160,64},{240,160},{320,336},{336,496},{416,320},... | collective-permute-start | bytes 49160 | tf_op jit(solution)/shard_map/ppermute | solution.py:326
  109.4 6.0 %collective-permute-start.2 = (f32[4,8,128]{2,1,0:T(8,128)S(1)}, f32[4,8,128]{2,1,0:T(8,128)S(1)}, u32[]{:S(2)}, u32[]{:S(2)}) collective-permute-start(f32[4,8,128]{2,1,0:T(8,128)S(1)} %get-tuple-element.18), channel_id=1, source_target_pairs={{64,240},{240,64},{320,496},{496,320},{65,241},{241,65},{321,497},... | collective-permute-start | bytes 49160 | tf_op jit(solution)/shard_map/ppermute | solution.py:327

commit v6 on v4

--- a/solution.py
+++ b/solution.py
@@ -16,7 +16,31 @@
 GROUP = 64
 ROWS1 = 168
 ROWS2 = 112
-ROWS3 = 16
+STRIDE = 68
+
+
+def matching():
+    free = [
+        [q for q in range(32) if all((64 * b + 2 * q + z) // 12 != p for z in (0, 1) for b in range(6))]
+        for p in range(32)
+    ]
+    chosen = {}
+
+    def place(p, seen):
+        for q in free[p]:
+            if q not in seen:
+                seen.add(q)
+                if q not in chosen or place(chosen[q], seen):
+                    chosen[q] = p
+                    return True
+        return False
+
+    assert all(place(p, set()) for p in range(32))
+    return [2 * q + z for p in range(32) for q in range(32) if chosen[q] == p for z in (0, 1)]
+
+
+TAKES = matching()
+HOLDER = [TAKES.index(pair) for pair in range(GROUP)]
 VMEM = pltpu.CompilerParams(vmem_limit_bytes=20 * 1024 * 1024)
 
 
@@ -61,11 +85,13 @@
         piece = dot00(coef[p], three_index)
         for h in range(2):
             for k in range(2):
-                pieces[pl.ds(4 * p + 2 * h + k, 128, 64), :] = piece[
+                pieces[pl.ds(4 * p + 2 * h + k, 128, STRIDE), :] = piece[
                     128 * h : 128 * h + 128, 128 * k : 128 * k + 128
                 ]
     for g in range(GROUP):
-        out[g, 0:128, :] = pieces[128 * g : 128 * g + 128, :].astype(BF)
+        for y in range(2):
+            at = (2 * TAKES[g] + y) * STRIDE
+            out[g, 64 * y : 64 * y + 64, :] = pieces[at : at + 64, :].astype(BF)
 
 
 def rest_kernel(blocks, owners, offsets, filled, mine, other, out, rows, sem):
@@ -142,7 +168,7 @@
             out[at] = jnp.concatenate(rows, 0).astype(BF)
 
 
-def column_kernel(place, got, out):
+def column_kernel(place, takes, got, out):
     total = got[0].astype(F32)
     for z in range(1, 8):
         total = total + got[z].astype(F32)
@@ -153,7 +179,7 @@
         a, b = total[8 * i : 8 * i + 8], total[48 + 8 * i : 56 + 8 * i]
         tiles.append(jnp.where(sub < 4, a, pltpu.roll(b, 4, 0)))
         tiles.append(jnp.where(sub < 4, pltpu.roll(a, 4, 0), b))
-    column = 2 * place[0]
+    column = 2 * takes[place[0]]
     whole, part = total[96:104], total[104:112]
     packed = [
         jnp.where(lane < 64, whole, pltpu.roll(part, 64, 1)),
@@ -165,21 +191,23 @@
             tile = tiles[6 * low + b_first]
             if b_last != b_first:
                 tile = jnp.where(column >= 24 * p - 128 * b_first, tile, tiles[6 * low + b_last])
-            out[2 * p + low] = jnp.concatenate([tile, packed[low]], 0).astype(BF)
-
-
-def final_kernel(place, got, aux_out, virt_out, *, scale):
+            out[2 * p + low] = tile.astype(BF)
+    for low in range(2):
+        out[place[0] // 2 * 2 + low] = packed[low].astype(BF)
+
+
+def final_kernel(place, holder, got, aux_out, virt_out, *, scale):
     p = place[0]
     for j in range(12):
-        tile = got[lax.rem(12 * p + j, 64), 0:8, :].astype(F32) * scale
+        tile = got[holder[lax.rem(12 * p + j, 64)]].astype(F32) * scale
         for y in range(2):
             for o in range(ABPO):
                 aux_out[2 * j + y : 2 * j + y + 1, 128 * o : 128 * o + 128] = tile[
                     4 * y + o : 4 * y + o + 1
                 ]
     sub = lax.broadcasted_iota(jnp.int32, (8, 128), 0)
-    first = got[2 * p, 8:16, :].astype(F32) * scale
-    last = got[2 * p + 1, 8:16, :].astype(F32) * scale
+    first = got[2 * p].astype(F32) * scale
+    last = got[2 * p + 1].astype(F32) * scale
     mid = jnp.where(sub < 4, pltpu.roll(first, 64, 1), pltpu.roll(pltpu.roll(last, 64, 1), 4, 0))
     virt_out[0:8, :] = first[:, 0:48]
     virt_out[8:16, :] = mid[:, 0:48]
@@ -247,7 +275,7 @@
         piece_kernel,
         [ints, amps, coef],
         [sds((GROUP, ROWS1, 128), BF)],
-        scratch=[pltpu.VMEM((8192, 128), F32)],
+        scratch=[pltpu.VMEM((128 * STRIDE, 128), F32)],
     )
     (sent,) = call(
         rest_kernel,
@@ -269,15 +297,15 @@
     (sent,) = call(
         column_kernel,
         [got],
-        [sds((GROUP, ROWS3, 128), BF)],
-        [(2 * pair + low).reshape(1)],
+        [sds((GROUP, 8, 128), BF)],
+        [(2 * pair + low).reshape(1), jnp.array(TAKES, jnp.int32)],
     )
     got = lax.all_to_all(sent, ("pair", "low"), split_axis=0, concat_axis=0, tiled=True)
     aux, virt = call(
         lambda *refs: final_kernel(*refs, scale=scale),
         [got],
         [sds((24, 512), F32), sds((24, 48), F32)],
-        [pair.reshape(1)],
+        [pair.reshape(1), jnp.array(HOLDER, jnp.int32)],
     )
     return aux.T, virt.T
 

time: 108 us -> 106 us (0.981)
  blocking collectives: 57.2 us -> 55.8 us
    all_to_all x2, blocking collectives: 57.2 us -> 55.8 us  [on_device(): lax.all_to_all(sent, ('pair', 'low'), split_axis=0, concat_axis=0, tiled=...]
  transfers between devices with their start and end apart: 2 -> 2, of which waited for: 1 -> 1; matrix products, arithmetic and copies ran while one was open for 0% -> 0% of each run, Pallas kernels for 4% -> 2%
where the time goes in v6:
time: 106 us
  blocking collectives  55.8 us (53%)
  starting transfers between devices  22.7 us (21%)
  waiting for transfers between devices  16.7 us (16%)
  Pallas kernels  10 us (9%)
    all_to_all x2, blocking collectives, on_device(): lax.all_to_all(sent, ('pair', 'low'), split_axis=0, concat_axis=0, tiled=...  55.8 us
    all_to_all x1, waiting for transfers between devices, on_device(): got = lax.all_to_all(sent, 'high', split_axis=0, concat_axis=0, tiled=True)  16.7 us
    all_to_all x1, starting transfers between devices, on_device(): got = lax.all_to_all(sent, 'high', split_axis=0, concat_axis=0, tiled=True)  13.9 us
    pallas_call x6, Pallas kernels, call(): pl.pallas_call(body, in_specs=[smem] * len(scalars) + [some] * len(lead)...  10 us
    ppermute x1, starting transfers between devices, on_device(): other = lax.ppermute(other, 'pair', [(i, i ^ 1) for i in range(32)])  8.78 us
  transfers between devices with their start and end apart: 2, of which 1 were waited for; matrix products, arithmetic and copies ran while one was open for 0% of the time, Pallas kernels for 2%

profile of v6, /device:TPU:1, one launch (start us, length us, event | category | flops | bytes accessed | tf_op | source)
XLA Modules:
  0.0 106.0 jit_solution(1025094868061372167)
XLA Ops:
  0.6 0.0 copy-start
  0.7 0.0 copy-start.1
  0.7 0.0 copy-start.2
  0.7 3.3 %shard_map.104 = (f32[18,128,128]{2,1,0:T(8,128)S(1)}, bf16[18,128,128]{2,1,0:T(8,128)(2,1)S(1)}, bf16[16,64,256]{2,1,0:T(8,128)(2,1)S(1)}, bf16[16,64,256]{2,1,0:T(8,128)(2,1)S(1)}, bf16[16,64,64]{2,1,0:T(8,128)(2,1)S(1)}) custom-call(s32[1]{0:T(128)} %bitcast.5.core, bf16[16,64,64]{2,1,0:T(8,128)(2,1)} %dens_in.1, bf16[16,64,256]{2,1,0:T(8,128)(2,1)} %bitcast.14, ...), custom_call_target="tpu_custom_call" | custom-call | tf_op jit(solution)/shard_map/pallas_call | solution.py:231
  4.0 8.8 %collective-permute-start = (bf16[18,128,128]{2,1,0:T(8,128)(2,1)S(1)}, bf16[18,128,128]{2,1,0:T(8,128)(2,1)S(1)}, u32[]{:S(2)}, u32[]{:S(2)}) collective-permute-start(bf16[18,128,128]{2,1,0:T(8,128)(2,1)S(1)} %get-tuple-element.13), channel_id=1, source_target_pairs={{0,16},{16,0},{32,48},{48,32},{64,80},{80,64},{96,112},{112,96},{1... | collective-permute-start | bytes 1769480 | tf_op jit(solution)/shard_map/ppermute | solution.py:273
  12.8 2.1 %shard_map.105.filled = bf16[64,168,128]{2,1,0:T(8,128)(2,1)S(1)} custom-call(bf16[16,64,256]{2,1,0:T(8,128)(2,1)S(1)} %get-tuple-element.9.ints, bf16[16,64,64]{2,1,0:T(8,128)(2,1)S(1)} %get-tuple-element.10.amps, bf16[16,64,256]{2,1,0:T(8,128)(2,1)S(1)} %get-tuple-element.11.coef), custom_call_target="tpu_custom_call" | custom-call | tf_op jit(solution)/shard_map/pallas_call | solution.py:231
  14.9 0.0 collective-permute-done.other
  14.9 0.0 copy-done
  14.9 0.0 copy-done.1
  14.9 0.0 copy-done.2
  14.9 0.9 shard_map.106
  15.8 39.1 %all_to_all.15.got = bf16[64,168,128]{2,1,0:T(8,128)(2,1)S(1)} all-to-all(bf16[64,168,128]{2,1,0:T(8,128)(2,1)S(1)} %shard_map.106), channel_id=1, replica_groups=mesh['pair'=32,'high'=8,'low'=2] {'pair','low'}, dimensions={0} | all-to-all | bytes 5505024 | tf_op jit(solution)/shard_map/all_to_all | solution.py:288
  54.9 0.0 copy-start.4
  54.9 0.0 copy-start.3
  54.9 1.9 %shard_map.107 = bf16[8,112,128]{2,1,0:T(8,128)(2,1)} custom-call(bf16[64,168,128]{2,1,0:T(8,128)(2,1)S(1)} %all_to_all.15.got), custom_call_target="tpu_custom_call" | custom-call | tf_op jit(solution)/shard_map/pallas_call | solution.py:231
  56.9 13.9 %all-to-all-start.1 = ((bf16[8,112,128]{2,1,0:T(8,128)(2,1)}), bf16[8,112,128]{2,1,0:T(8,128)(2,1)S(1)}, u32[]{:S(2)}, u32[]{:S(2)}) async-start(bf16[8,112,128]{2,1,0:T(8,128)(2,1)} %shard_map.107), calls=%async_computation.1 | async-start | bytes 458752 | tf_op jit(solution)/shard_map/all_to_all | solution.py:296
  70.8 16.7 %all-to-all-done.1.got = bf16[8,112,128]{2,1,0:T(8,128)(2,1)S(1)} async-done(((bf16[8,112,128]{2,1,0:T(8,128)(2,1)}), bf16[8,112,128]{2,1,0:T(8,128)(2,1)S(1)}, u32[]{:S(2)}, u32[]{:S(2)}) %all-to-all-start.1) | async-done | bytes 229408 | tf_op jit(solution)/shard_map/all_to_all | solution.py:296
  87.4 0.0 copy-done.4
  87.5 0.6 shard_map.108
  88.1 16.7 %all_to_all.16.refs_2_ = bf16[64,8,128]{2,1,0:T(8,128)(2,1)S(1)} all-to-all(bf16[64,8,128]{2,1,0:T(8,128)(2,1)S(1)} %shard_map.108), channel_id=1, replica_groups=mesh['pair'=32,'high'=8,'low'=2] {'pair','low'}, dimensions={0} | all-to-all | bytes 262144 | tf_op jit(solution)/shard_map/all_to_all | solution.py:303
  104.8 0.0 copy-done.3
  104.8 1.2 %shard_map.109 = (f32[24,512]{1,0:T(8,128)}, f32[24,48]{1,0:T(8,128)}) custom-call(s32[1]{0:T(128)} %bitcast.refs_0_, s32[64]{0:T(128)S(1)} %copy-done.3, bf16[64,8,128]{2,1,0:T(8,128)(2,1)S(1)} %all_to_all.16.refs_2_), custom_call_target="tpu_custom_call" | custom-call | tf_op jit(solution)/shard_map/pallas_call | solution.py:231
Async XLA Ops:
  0.6 14.2 %copy-start = (s32[16,2]{0,1:T(2,128)S(1)}, s32[16,2]{0,1:T(2,128)}, u32[]{:S(2)}) copy-start(s32[16,2]{0,1:T(2,128)} %param.13) | copy-start | bytes 388
  0.7 14.2 %copy-start.1 = (s32[16,2]{0,1:T(2,128)S(1)}, s32[16,2]{0,1:T(2,128)}, u32[]{:S(2)}) copy-start(s32[16,2]{0,1:T(2,128)} %param.14) | copy-start | bytes 388
  0.7 14.2 %copy-start.2 = (s32[16,2]{0,1:T(2,128)S(1)}, s32[16,2]{0,1:T(2,128)}, u32[]{:S(2)}) copy-start(s32[16,2]{0,1:T(2,128)} %param.15) | copy-start | bytes 388
  4.0 10.8 %collective-permute-start = (bf16[18,128,128]{2,1,0:T(8,128)(2,1)S(1)}, bf16[18,128,128]{2,1,0:T(8,128)(2,1)S(1)}, u32[]{:S(2)}, u32[]{:S(2)}) collective-permute-start(bf16[18,128,128]{2,1,0:T(8,128)(2,1)S(1)} %get-tuple-element.13), channel_id=1, source_target_pairs={{0,16},{16,0},{32,48},{48,32},{64,80},{80,64},{96,112},{112,96},{1... | collective-permute-start | bytes 1769480 | tf_op jit(solution)/shard_map/ppermute | solution.py:273
  54.9 32.5 %copy-start.4 = (s32[64]{0:T(128)S(1)}, s32[64]{0:T(128)}, u32[]{:S(2)}) copy-start(s32[64]{0:T(128)} %constant.27.clone.takes) | copy-start | bytes 772
  54.9 49.9 %copy-start.3 = (s32[64]{0:T(128)S(1)}, s32[64]{0:T(128)}, u32[]{:S(2)}) copy-start(s32[64]{0:T(128)} %constant.28.clone.refs_1_) | copy-start | bytes 772
  56.9 30.6 %all-to-all-start.1 = ((bf16[8,112,128]{2,1,0:T(8,128)(2,1)}), bf16[8,112,128]{2,1,0:T(8,128)(2,1)S(1)}, u32[]{:S(2)}, u32[]{:S(2)}) async-start(bf16[8,112,128]{2,1,0:T(8,128)(2,1)} %shard_map.107), calls=%async_computation.1 | async-start | bytes 458752 | tf_op jit(solution)/shard_map/all_to_all | solution.py:296

commit v7 on v4

--- a/solution.py
+++ b/solution.py
@@ -16,8 +16,14 @@
 GROUP = 64
 ROWS1 = 168
 ROWS2 = 112
-ROWS3 = 16
+STRIDE = 68
+
 VMEM = pltpu.CompilerParams(vmem_limit_bytes=20 * 1024 * 1024)
+
+
+def taken(g):
+    p = g // 2
+    return 2 * ((6 * p + 8 + p // 16) % 32) + g % 2
 
 
 def dot00(a, b):
@@ -29,10 +35,14 @@
 
 
 def virtual_kernel(
-    core, dens_in, coef_in, blocks_in, ints_in, amps_in,
-    mine, other, coef, ints, amps, acc, dens, blocks, sems,
+    core, dens_in, coef_in, blocks_in, owners_in, offsets_in, ints_in, amps_in,
+    mine, other, coef, ints, amps, labels,
+    acc, dens, weighted, blocks, owners, offsets, sems,
 ):
-    moves = [(blocks_in, blocks), (coef_in, coef), (dens_in, dens), (ints_in, ints), (amps_in, amps)]
+    moves = [
+        (blocks_in, blocks), (coef_in, coef), (dens_in, dens), (owners_in, owners),
+        (offsets_in, offsets), (ints_in, ints), (amps_in, amps),
+    ]
     copies = [pltpu.make_async_copy(*move, sems.at[i]) for i, move in enumerate(moves)]
     for copy in copies:
         copy.start()
@@ -40,9 +50,9 @@
     for copy in copies[:3]:
         copy.wait()
     for p in range(PAIRS):
-        c = coef[p]
-        weighted = dot00(dens[p], c).astype(BF)
-        product = dot00(c, weighted)
+        weighted[p] = dot00(dens[p], coef[p]).astype(BF)
+    for p in range(PAIRS):
+        product = dot00(coef[p], weighted[p])
         for h in range(2):
             for k in range(2):
                 at = blocks[h, p] * 6 + blocks[k, p]
@@ -53,6 +63,21 @@
             other[3 * i + j] = acc[6 * i + j + 3 - 3 * core[0]].astype(BF)
     for copy in copies[3:]:
         copy.wait()
+    lane = lax.broadcasted_iota(jnp.int32, (1, 128), 1) % 64
+    slice_row = jnp.zeros((1, 128), jnp.int32)
+    block_row = jnp.zeros((1, 128), jnp.int32)
+    offset_row = jnp.zeros((1, 128), jnp.int32)
+    for p in range(PAIRS):
+        for h in range(2):
+            for k in range(2):
+                here = lane == 4 * p + 2 * h + k
+                slice_row = jnp.where(here, owners[k, p], slice_row)
+                block_row = jnp.where(here, blocks[h, p], block_row)
+                offset_row = jnp.where(here, offsets[k, p], offset_row)
+    sub = lax.broadcasted_iota(jnp.int32, (8, 128), 0)
+    labels[...] = jnp.where(
+        sub == 4, slice_row, jnp.where(sub == 5, block_row, offset_row)
+    ).astype(F32)
 
 
 def piece_kernel(ints, amps, coef, out, pieces):
@@ -61,28 +86,19 @@
         piece = dot00(coef[p], three_index)
         for h in range(2):
             for k in range(2):
-                pieces[pl.ds(4 * p + 2 * h + k, 128, 64), :] = piece[
+                pieces[pl.ds(4 * p + 2 * h + k, 128, STRIDE), :] = piece[
                     128 * h : 128 * h + 128, 128 * k : 128 * k + 128
                 ]
     for g in range(GROUP):
-        out[g, 0:128, :] = pieces[128 * g : 128 * g + 128, :].astype(BF)
-
-
-def rest_kernel(blocks, owners, offsets, filled, mine, other, out, rows, sem):
-    lane = lax.broadcasted_iota(jnp.int32, (1, 128), 1) % 64
-    slice_row = jnp.zeros((1, 128), F32)
-    block_row = jnp.zeros((1, 128), F32)
-    offset_row = jnp.zeros((1, 128), F32)
-    for p in range(PAIRS):
-        for h in range(2):
-            for k in range(2):
-                here = lane == 4 * p + 2 * h + k
-                slice_row = jnp.where(here, owners[k, p].astype(F32), slice_row)
-                block_row = jnp.where(here, blocks[h, p].astype(F32), block_row)
-                offset_row = jnp.where(here, offsets[k, p].astype(F32), offset_row)
+        for y in range(2):
+            at = (2 * taken(g) + y) * STRIDE
+            out[g, 64 * y : 64 * y + 64, :] = pieces[at : at + 64, :].astype(BF)
+
+
+def rest_kernel(filled, mine, other, label_rows, out, rows, sem):
     sub = lax.broadcasted_iota(jnp.int32, (8, 128), 0)
+    labels = label_rows[...]
     top = sub < 4
-    labels = jnp.where(sub == 4, slice_row, jnp.where(sub == 5, block_row, offset_row))
     for i in range(GROUP // 2):
         first, mid, last = (
             [
@@ -153,7 +169,9 @@
         a, b = total[8 * i : 8 * i + 8], total[48 + 8 * i : 56 + 8 * i]
         tiles.append(jnp.where(sub < 4, a, pltpu.roll(b, 4, 0)))
         tiles.append(jnp.where(sub < 4, pltpu.roll(a, 4, 0), b))
-    column = 2 * place[0]
+    p = place[0] >> 1
+    column = 4 * ((6 * p + 8 + (p >> 4)) & 31) + 2 * (place[0] & 1)
+    own = 2 * p
     whole, part = total[96:104], total[104:112]
     packed = [
         jnp.where(lane < 64, whole, pltpu.roll(part, 64, 1)),
@@ -165,21 +183,25 @@
             tile = tiles[6 * low + b_first]
             if b_last != b_first:
                 tile = jnp.where(column >= 24 * p - 128 * b_first, tile, tiles[6 * low + b_last])
-            out[2 * p + low] = jnp.concatenate([tile, packed[low]], 0).astype(BF)
+            out[2 * p + low] = tile.astype(BF)
+    for low in range(2):
+        out[own + low] = packed[low].astype(BF)
 
 
 def final_kernel(place, got, aux_out, virt_out, *, scale):
     p = place[0]
     for j in range(12):
-        tile = got[lax.rem(12 * p + j, 64), 0:8, :].astype(F32) * scale
+        q = (6 * p + j // 2) & 31
+        odd = q & 1
+        tile = got[32 * odd + 2 * ((11 * (((q - odd) >> 1) + 12)) & 15) + j % 2].astype(F32) * scale
         for y in range(2):
             for o in range(ABPO):
                 aux_out[2 * j + y : 2 * j + y + 1, 128 * o : 128 * o + 128] = tile[
                     4 * y + o : 4 * y + o + 1
                 ]
     sub = lax.broadcasted_iota(jnp.int32, (8, 128), 0)
-    first = got[2 * p, 8:16, :].astype(F32) * scale
-    last = got[2 * p + 1, 8:16, :].astype(F32) * scale
+    first = got[2 * p].astype(F32) * scale
+    last = got[2 * p + 1].astype(F32) * scale
     mid = jnp.where(sub < 4, pltpu.roll(first, 64, 1), pltpu.roll(pltpu.roll(last, 64, 1), 4, 0))
     virt_out[0:8, :] = first[:, 0:48]
     virt_out[8:16, :] = mid[:, 0:48]
@@ -216,8 +238,8 @@
     low = lax.axis_index("low")
     scale = 1.0 / math.sqrt(PAIRS * 32)
     sds = jax.ShapeDtypeStruct
-    blocks = pao_blocks.T
-    mine, other, coef, ints, amps = call(
+    names = pltpu.SMEM((2, PAIRS), jnp.int32)
+    mine, other, coef, ints, amps, labels = call(
         virtual_kernel,
         [],
         [
@@ -226,18 +248,24 @@
             sds((PAIRS, 64, 256), BF),
             sds((PAIRS, 64, 256), BF),
             sds((PAIRS, 64, 64), BF),
+            sds((8, 128), F32),
         ],
         [(pair % 2).reshape(1)],
         [
             pltpu.VMEM((36, 128, 128), F32),
             pltpu.VMEM((PAIRS, 64, 64), BF),
-            pltpu.SMEM((2, PAIRS), jnp.int32),
-            pltpu.SemaphoreType.DMA((5,)),
+            pltpu.VMEM((PAIRS, 64, 256), BF),
+            names,
+            names,
+            names,
+            pltpu.SemaphoreType.DMA((7,)),
         ],
         held=[
             pno_density,
             jnp.swapaxes(pno_coef, 1, 2),
-            blocks,
+            pao_blocks.T,
+            aux_slice.T,
+            aux_offset.T,
             jnp.swapaxes(integrals, 1, 2),
             amplitudes,
         ],
@@ -247,14 +275,13 @@
         piece_kernel,
         [ints, amps, coef],
         [sds((GROUP, ROWS1, 128), BF)],
-        scratch=[pltpu.VMEM((8192, 128), F32)],
+        scratch=[pltpu.VMEM((128 * STRIDE, 128), F32)],
     )
     (sent,) = call(
         rest_kernel,
-        [mine, other],
+        [mine, other, labels],
         [sds((GROUP, ROWS1, 128), BF)],
-        [blocks, aux_slice.T, aux_offset.T],
-        [pltpu.VMEM((GROUP, ROWS1 - 128, 128), BF), pltpu.SemaphoreType.DMA(())],
+        scratch=[pltpu.VMEM((GROUP, ROWS1 - 128, 128), BF), pltpu.SemaphoreType.DMA(())],
         in_place=filled,
     )
     got = lax.all_to_all(sent, ("pair", "low"), split_axis=0, concat_axis=0, tiled=True)
@@ -269,7 +296,7 @@
     (sent,) = call(
         column_kernel,
         [got],
-        [sds((GROUP, ROWS3, 128), BF)],
+        [sds((GROUP, 8, 128), BF)],
         [(2 * pair + low).reshape(1)],
     )
     got = lax.all_to_all(sent, ("pair", "low"), split_axis=0, concat_axis=0, tiled=True)

time: 108 us -> 104 us (0.963)
  Pallas kernels: 10.8 us -> 7.31 us
  blocking collectives: 57.2 us -> 55.8 us
    pallas_call x6, Pallas kernels: 10.8 us -> 7.31 us  [call(): pl.pallas_call(body, in_specs=[smem] * len(scalars) + [some] * len(lead)...]
    all_to_all x2, blocking collectives: 57.2 us -> 55.8 us  [on_device(): lax.all_to_all(sent, ('pair', 'low'), split_axis=0, concat_axis=0, tiled=...]
  transfers between devices with their start and end apart: 2 -> 2, of which waited for: 1 -> 1; matrix products, arithmetic and copies ran while one was open for 0% -> 0% of each run, Pallas kernels for 4% -> 2%
where the time goes in v7:
time: 104 us; the launch traced here: 103 us
  blocking collectives  55.8 us (54%)
  starting transfers between devices  22.7 us (22%)
  waiting for transfers between devices  16.7 us (16%)
  Pallas kernels  7.31 us (7%)
    all_to_all x2, blocking collectives, on_device(): lax.all_to_all(sent, ('pair', 'low'), split_axis=0, concat_axis=0, tiled=...  55.8 us
    all_to_all x1, waiting for transfers between devices, on_device(): got = lax.all_to_all(sent, 'high', split_axis=0, concat_axis=0, tiled=True)  16.7 us
    all_to_all x1, starting transfers between devices, on_device(): got = lax.all_to_all(sent, 'high', split_axis=0, concat_axis=0, tiled=True)  13.9 us
    ppermute x1, starting transfers between devices, on_device(): other = lax.ppermute(other, 'pair', [(i, i ^ 1) for i in range(32)])  8.79 us
    pallas_call x6, Pallas kernels, call(): pl.pallas_call(body, in_specs=[smem] * len(scalars) + [some] * len(lead)...  7.31 us
  transfers between devices with their start and end apart: 2, of which 1 were waited for; matrix products, arithmetic and copies ran while one was open for 0% of the time, Pallas kernels for 2%

profile of v7, /device:TPU:1, one launch (start us, length us, event | category | flops | bytes accessed | tf_op | source)
XLA Modules:
  0.0 103.2 jit_solution(714038566831063191)
XLA Ops:
  0.6 2.4 %shard_map.86 = (f32[18,128,128]{2,1,0:T(8,128)S(1)}, bf16[18,128,128]{2,1,0:T(8,128)(2,1)S(1)}, bf16[16,64,256]{2,1,0:T(8,128)(2,1)S(1)}, bf16[16,64,256]{2,1,0...) custom-call(s32[1]{0:T(128)} %bitcast.2.core, bf16[16,64,64]{2,1,0:T(8,128)(2,1)} %dens_in.1, ...), custom_call_target="tpu_custom_call" | custom-call | tf_op jit(solution)/shard_map/pallas_call | solution.py:225
  3.0 8.8 %collective-permute-start = (bf16[18,128,128]{2,1,0:T(8,128)(2,1)S(1)}, bf16[18,128,128]{2,1,0:T(8,128)(2,1)S(1)}, u32[]{:S(2)}, u32[]{:S(2)}) collective-permute-start(bf16[18,128,128]{2,1,0:T(8,128)(2,1)S(1)} %get-tuple-element.14), channel_id=1, source_target_pairs={{0,16},{16,0},{32,48},{48,32},{64,80},{80,64},{96,112},{112,96},{1... | collective-permute-start | bytes 1769480 | tf_op jit(solution)/shard_map/ppermute | solution.py:273
  11.8 2.1 %shard_map.87.filled = bf16[64,168,128]{2,1,0:T(8,128)(2,1)S(1)} custom-call(bf16[16,64,256]{2,1,0:T(8,128)(2,1)S(1)} %get-tuple-element.10.ints, bf16[16,64,64]{2,1,0:T(8,128)(2,1)S(1)} %get-tuple-element.11.amps, bf16[16,64,256]{2,1,0:T(8,128)(2,1)S(1)} %get-tuple-element.12.coef), custom_call_target="tpu_custom_call" | custom-call | tf_op jit(solution)/shard_map/pallas_call | solution.py:225
  13.9 0.0 collective-permute-done.other
  13.9 0.2 shard_map.88
  14.1 39.1 %all_to_all.15.got = bf16[64,168,128]{2,1,0:T(8,128)(2,1)S(1)} all-to-all(bf16[64,168,128]{2,1,0:T(8,128)(2,1)S(1)} %shard_map.88), channel_id=1, replica_groups=mesh['pair'=32,'high'=8,'low'=2] {'pair','low'}, dimensions={0} | all-to-all | bytes 5505024 | tf_op jit(solution)/shard_map/all_to_all | solution.py:287
  53.3 1.9 %shard_map.89 = bf16[8,112,128]{2,1,0:T(8,128)(2,1)} custom-call(bf16[64,168,128]{2,1,0:T(8,128)(2,1)S(1)} %all_to_all.15.got), custom_call_target="tpu_custom_call" | custom-call | tf_op jit(solution)/shard_map/pallas_call | solution.py:225
  55.2 13.9 %all-to-all-start.1 = ((bf16[8,112,128]{2,1,0:T(8,128)(2,1)}), bf16[8,112,128]{2,1,0:T(8,128)(2,1)S(1)}, u32[]{:S(2)}, u32[]{:S(2)}) async-start(bf16[8,112,128]{2,1,0:T(8,128)(2,1)} %shard_map.89), calls=%async_computation.1 | async-start | bytes 458752 | tf_op jit(solution)/shard_map/all_to_all | solution.py:295
  69.1 16.7 %all-to-all-done.1.got = bf16[8,112,128]{2,1,0:T(8,128)(2,1)S(1)} async-done(((bf16[8,112,128]{2,1,0:T(8,128)(2,1)}), bf16[8,112,128]{2,1,0:T(8,128)(2,1)S(1)}, u32[]{:S(2)}, u32[]{:S(2)}) %all-to-all-start.1) | async-done | bytes 229408 | tf_op jit(solution)/shard_map/all_to_all | solution.py:295
  85.8 0.1 shard_map.90
  85.9 16.7 %all_to_all.16.refs_1_ = bf16[64,8,128]{2,1,0:T(8,128)(2,1)S(1)} all-to-all(bf16[64,8,128]{2,1,0:T(8,128)(2,1)S(1)} %shard_map.90), channel_id=1, replica_groups=mesh['pair'=32,'high'=8,'low'=2] {'pair','low'}, dimensions={0} | all-to-all | bytes 262144 | tf_op jit(solution)/shard_map/all_to_all | solution.py:302
  102.5 0.7 shard_map.91
Async XLA Ops:
  3.0 10.9 %collective-permute-start = (bf16[18,128,128]{2,1,0:T(8,128)(2,1)S(1)}, bf16[18,128,128]{2,1,0:T(8,128)(2,1)S(1)}, u32[]{:S(2)}, u32[]{:S(2)}) collective-permute-start(bf16[18,128,128]{2,1,0:T(8,128)(2,1)S(1)} %get-tuple-element.14), channel_id=1, source_target_pairs={{0,16},{16,0},{32,48},{48,32},{64,80},{80,64},{96,112},{112,96},{1... | collective-permute-start | bytes 1769480 | tf_op jit(solution)/shard_map/ppermute | solution.py:273
  55.2 30.6 %all-to-all-start.1 = ((bf16[8,112,128]{2,1,0:T(8,128)(2,1)}), bf16[8,112,128]{2,1,0:T(8,128)(2,1)S(1)}, u32[]{:S(2)}, u32[]{:S(2)}) async-start(bf16[8,112,128]{2,1,0:T(8,128)(2,1)} %shard_map.89), calls=%async_computation.1 | async-start | bytes 458752 | tf_op jit(solution)/shard_map/all_to_all | solution.py:295

commit v8 on v7

--- a/solution.py
+++ b/solution.py
@@ -35,9 +35,9 @@
 
 
 def virtual_kernel(
-    core, dens_in, coef_in, blocks_in, owners_in, offsets_in, ints_in, amps_in,
-    mine, other, coef, ints, amps, labels,
-    acc, dens, weighted, blocks, owners, offsets, sems,
+    place, dens_in, coef_in, blocks_in, owners_in, offsets_in, ints_in, amps_in,
+    acc, other, coef, ints, amps, labels,
+    dens, weighted, blocks, owners, offsets, sems,
 ):
     moves = [
         (blocks_in, blocks), (coef_in, coef), (dens_in, dens), (owners_in, owners),
@@ -57,10 +57,10 @@
             for k in range(2):
                 at = blocks[h, p] * 6 + blocks[k, p]
                 acc[at] = acc[at] + product[128 * h : 128 * h + 128, 128 * k : 128 * k + 128]
+    core = (place[0] >> 1) & 1
     for i in range(6):
         for j in range(3):
-            mine[3 * i + j] = acc[6 * i + j + 3 * core[0]]
-            other[3 * i + j] = acc[6 * i + j + 3 - 3 * core[0]].astype(BF)
+            other[3 * i + j] = acc[6 * i + j + 3 - 3 * core].astype(BF)
     for copy in copies[3:]:
         copy.wait()
     lane = lax.broadcasted_iota(jnp.int32, (1, 128), 1) % 64
@@ -80,10 +80,11 @@
     ).astype(F32)
 
 
-def piece_kernel(ints, amps, coef, out, pieces):
-    for p in range(PAIRS):
-        three_index = dot00(amps[p], ints[p]).astype(BF)
-        piece = dot00(coef[p], three_index)
+def piece_kernel(ints, amps, coef, out, pieces, three_index):
+    for p in range(PAIRS):
+        three_index[p] = dot00(amps[p], ints[p]).astype(BF)
+    for p in range(PAIRS):
+        piece = dot00(coef[p], three_index[p])
         for h in range(2):
             for k in range(2):
                 pieces[pl.ds(4 * p + 2 * h + k, 128, STRIDE), :] = piece[
@@ -95,14 +96,15 @@
             out[g, 64 * y : 64 * y + 64, :] = pieces[at : at + 64, :].astype(BF)
 
 
-def rest_kernel(filled, mine, other, label_rows, out, rows, sem):
+def rest_kernel(place, filled, acc, other, label_rows, out, rows, sem):
+    half = 3 * ((place[0] >> 1) & 1)
     sub = lax.broadcasted_iota(jnp.int32, (8, 128), 0)
     labels = label_rows[...]
     top = sub < 4
     for i in range(GROUP // 2):
         first, mid, last = (
             [
-                mine[3 * (row // 128) + j, row % 128 : row % 128 + 8, :]
+                acc[6 * (row // 128) + j + half, row % 128 : row % 128 + 8, :]
                 + other[3 * (row // 128) + j, row % 128 : row % 128 + 8, :].astype(F32)
                 for j in range(3)
             ]
@@ -189,7 +191,7 @@
 
 
 def final_kernel(place, got, aux_out, virt_out, *, scale):
-    p = place[0]
+    p = place[0] >> 1
     for j in range(12):
         q = (6 * p + j // 2) & 31
         odd = q & 1
@@ -234,25 +236,23 @@
 
 
 def on_device(integrals, amplitudes, pno_density, pno_coef, pao_blocks, aux_slice, aux_offset):
-    pair = lax.axis_index("pair")
-    low = lax.axis_index("low")
+    place = [(2 * lax.axis_index("pair") + lax.axis_index("low")).reshape(1)]
     scale = 1.0 / math.sqrt(PAIRS * 32)
     sds = jax.ShapeDtypeStruct
     names = pltpu.SMEM((2, PAIRS), jnp.int32)
-    mine, other, coef, ints, amps, labels = call(
+    acc, other, coef, ints, amps, labels = call(
         virtual_kernel,
         [],
         [
-            sds((18, 128, 128), F32),
+            sds((36, 128, 128), F32),
             sds((18, 128, 128), BF),
             sds((PAIRS, 64, 256), BF),
             sds((PAIRS, 64, 256), BF),
             sds((PAIRS, 64, 64), BF),
             sds((8, 128), F32),
         ],
-        [(pair % 2).reshape(1)],
+        place,
         [
-            pltpu.VMEM((36, 128, 128), F32),
             pltpu.VMEM((PAIRS, 64, 64), BF),
             pltpu.VMEM((PAIRS, 64, 256), BF),
             names,
@@ -275,12 +275,13 @@
         piece_kernel,
         [ints, amps, coef],
         [sds((GROUP, ROWS1, 128), BF)],
-        scratch=[pltpu.VMEM((128 * STRIDE, 128), F32)],
+        scratch=[pltpu.VMEM((128 * STRIDE, 128), F32), pltpu.VMEM((PAIRS, 64, 256), BF)],
     )
     (sent,) = call(
         rest_kernel,
-        [mine, other, labels],
+        [acc, other, labels],
         [sds((GROUP, ROWS1, 128), BF)],
+        place,
         scratch=[pltpu.VMEM((GROUP, ROWS1 - 128, 128), BF), pltpu.SemaphoreType.DMA(())],
         in_place=filled,
     )
@@ -297,14 +298,14 @@
         column_kernel,
         [got],
         [sds((GROUP, 8, 128), BF)],
-        [(2 * pair + low).reshape(1)],
+        place,
     )
     got = lax.all_to_all(sent, ("pair", "low"), split_axis=0, concat_axis=0, tiled=True)
     aux, virt = call(
         lambda *refs: final_kernel(*refs, scale=scale),
         [got],
         [sds((24, 512), F32), sds((24, 48), F32)],
-        [pair.reshape(1)],
+        place,
     )
     return aux.T, virt.T
 

time: 104 us -> 102 us (0.981)
  blocking collectives: 55.8 us -> 86.5 us
  waiting for transfers between devices: 16.7 us -> 0.55 us
  starting transfers between devices: 22.7 us -> 8.79 us
  Pallas kernels: 7.31 us -> 5.58 us
    all_to_all x0 -> x1, blocking collectives: none -> 30.3 us  [on_device(): got = lax.all_to_all(sent, 'high', split_axis=0, concat_axis=0, tiled=True)]
    all_to_all x1 -> x0, waiting for transfers between devices: 16.7 us -> none  [on_device(): got = lax.all_to_all(sent, 'high', split_axis=0, concat_axis=0, tiled=True)]
    all_to_all x1 -> x0, starting transfers between devices: 13.9 us -> none  [on_device(): got = lax.all_to_all(sent, 'high', split_axis=0, concat_axis=0, tiled=True)]
    pallas_call x6, Pallas kernels: 7.31 us -> 5.58 us  [call(): pl.pallas_call(body, in_specs=[smem] * len(scalars) + [some] * len(lead)...]
  transfers between devices with their start and end apart: 2 -> 1, of which waited for: 1 -> 1; matrix products, arithmetic and copies ran while one was open for 0% -> 0% of each run, Pallas kernels for 2% -> 1%
where the time goes in v8:
time: 102 us
  blocking collectives  86.5 us (85%)
  starting transfers between devices  8.79 us (9%)
  Pallas kernels  5.58 us (5%)
    all_to_all x2, blocking collectives, on_device(): lax.all_to_all(sent, ('pair', 'low'), split_axis=0, concat_axis=0, tiled=...  56.2 us
    all_to_all x1, blocking collectives, on_device(): got = lax.all_to_all(sent, 'high', split_axis=0, concat_axis=0, tiled=True)  30.3 us
    ppermute x1, starting transfers between devices, on_device(): other = lax.ppermute(other, 'pair', [(i, i ^ 1) for i in range(32)])  8.79 us
    pallas_call x6, Pallas kernels, call(): pl.pallas_call(body, in_specs=[smem] * len(scalars) + [some] * len(lead)...  5.58 us
  transfers between devices with their start and end apart: 1, of which 1 were waited for; matrix products, arithmetic and copies ran while one was open for 0% of the time, Pallas kernels for 1%

profile of v8, /device:TPU:1, one launch (start us, length us, event | category | flops | bytes accessed | tf_op | source)
XLA Modules:
  0.0 102.1 jit_solution(14437836543770931057)
XLA Ops:
  0.6 2.3 %shard_map.86 = (f32[36,128,128]{2,1,0:T(8,128)S(1)}, bf16[18,128,128]{2,1,0:T(8,128)(2,1)S(1)}, bf16[16,64,256]{2,1,0:T(8,128)(2,1)S(1)}, bf16[16,64,256]{2,1,0...) custom-call(s32[1]{0:T(128)} %bitcast.place.refs_0_, bf16[16,64,64]{2,1,0:T(8,128)(2,1)} %dens_in.1, ...), custom_call_target="tpu_custom_call" | custom-call | tf_op jit(solution)/shard_map/pallas_call | solution.py:227
  2.9 8.8 %collective-permute-start = (bf16[18,128,128]{2,1,0:T(8,128)(2,1)S(1)}, bf16[18,128,128]{2,1,0:T(8,128)(2,1)S(1)}, u32[]{:S(2)}, u32[]{:S(2)}) collective-permute-start(bf16[18,128,128]{2,1,0:T(8,128)(2,1)S(1)} %get-tuple-element.14), channel_id=1, source_target_pairs={{0,16},{16,0},{32,48},{48,32},{64,80},{80,64},{96,112},{112,96},{1... | collective-permute-start | bytes 1769480 | tf_op jit(solution)/shard_map/ppermute | solution.py:273
  11.7 1.0 %shard_map.87.filled = bf16[64,168,128]{2,1,0:T(8,128)(2,1)S(1)} custom-call(bf16[16,64,256]{2,1,0:T(8,128)(2,1)S(1)} %get-tuple-element.10.ints, bf16[16,64,64]{2,1,0:T(8,128)(2,1)S(1)} %get-tuple-element.11.amps, bf16[16,64,256]{2,1,0:T(8,128)(2,1)S(1)} %get-tuple-element.12.coef), custom_call_target="tpu_custom_call" | custom-call | tf_op jit(solution)/shard_map/pallas_call | solution.py:227
  12.8 0.6 collective-permute-done.other
  13.3 0.2 shard_map.88
  13.6 39.5 %all_to_all.15.got = bf16[64,168,128]{2,1,0:T(8,128)(2,1)S(1)} all-to-all(bf16[64,168,128]{2,1,0:T(8,128)(2,1)S(1)} %shard_map.88), channel_id=1, replica_groups=mesh['pair'=32,'high'=8,'low'=2] {'pair','low'}, dimensions={0} | all-to-all | bytes 5505024 | tf_op jit(solution)/shard_map/all_to_all | solution.py:288
  53.1 1.3 %shard_map.89 = bf16[8,112,128]{2,1,0:T(8,128)(2,1)S(1)} custom-call(bf16[64,168,128]{2,1,0:T(8,128)(2,1)S(1)} %all_to_all.15.got), custom_call_target="tpu_custom_call" | custom-call | tf_op jit(solution)/shard_map/pallas_call | solution.py:227
  54.3 30.3 %all_to_all.16.got = bf16[8,112,128]{2,1,0:T(8,128)(2,1)S(1)} all-to-all(bf16[8,112,128]{2,1,0:T(8,128)(2,1)S(1)} %shard_map.89), channel_id=1, replica_groups=mesh['pair'=32,'high'=8,'low'=2] {'high'}, dimensions={0} | all-to-all | bytes 458752 | tf_op jit(solution)/shard_map/all_to_all | solution.py:296
  84.6 0.1 shard_map.90
  84.7 16.7 %all_to_all.17.refs_1_ = bf16[64,8,128]{2,1,0:T(8,128)(2,1)S(1)} all-to-all(bf16[64,8,128]{2,1,0:T(8,128)(2,1)S(1)} %shard_map.90), channel_id=1, replica_groups=mesh['pair'=32,'high'=8,'low'=2] {'pair','low'}, dimensions={0} | all-to-all | bytes 262144 | tf_op jit(solution)/shard_map/all_to_all | solution.py:303
  101.4 0.7 shard_map.91
Async XLA Ops:
  2.9 10.4 %collective-permute-start = (bf16[18,128,128]{2,1,0:T(8,128)(2,1)S(1)}, bf16[18,128,128]{2,1,0:T(8,128)(2,1)S(1)}, u32[]{:S(2)}, u32[]{:S(2)}) collective-permute-start(bf16[18,128,128]{2,1,0:T(8,128)(2,1)S(1)} %get-tuple-element.14), channel_id=1, source_target_pairs={{0,16},{16,0},{32,48},{48,32},{64,80},{80,64},{96,112},{112,96},{1... | collective-permute-start | bytes 1769480 | tf_op jit(solution)/shard_map/ppermute | solution.py:273

commit v9 on v8

--- a/solution.py
+++ b/solution.py
@@ -19,6 +19,11 @@
 STRIDE = 68
 
 VMEM = pltpu.CompilerParams(vmem_limit_bytes=20 * 1024 * 1024)
+
+
+def seat(g):
+    p = g // 2
+    return 8 * (p % 8) + 2 * (p // 8) + g % 2
 
 
 def taken(g):
@@ -93,7 +98,7 @@
     for g in range(GROUP):
         for y in range(2):
             at = (2 * taken(g) + y) * STRIDE
-            out[g, 64 * y : 64 * y + 64, :] = pieces[at : at + 64, :].astype(BF)
+            out[seat(g), 64 * y : 64 * y + 64, :] = pieces[at : at + 64, :].astype(BF)
 
 
 def rest_kernel(place, filled, acc, other, label_rows, out, rows, sem):
@@ -113,8 +118,8 @@
         moved = [pltpu.roll(m, 4, 0) for m in mid]
         even = first + [jnp.where(top, mid[0], moved[1]), jnp.where(top, mid[2], labels)]
         odd = last + [jnp.where(top, moved[0], mid[1]), jnp.where(top, moved[2], labels)]
-        rows[2 * i] = jnp.concatenate(even, 0).astype(BF)
-        rows[2 * i + 1] = jnp.concatenate(odd, 0).astype(BF)
+        rows[seat(2 * i)] = jnp.concatenate(even, 0).astype(BF)
+        rows[seat(2 * i + 1)] = jnp.concatenate(odd, 0).astype(BF)
     copy = pltpu.make_async_copy(rows, out.at[:, 128:ROWS1], sem)
     copy.start()
     copy.wait()
@@ -135,7 +140,7 @@
     acc[...] = dot10(hot[...], data)
     lanes8 = lax.broadcasted_iota(jnp.int32, (8, 128), 1)
     for half in range(2):
-        mine = [g for g in range(GROUP) if (g // 2) % 2 == half]
+        mine = [g for g in range(GROUP) if (g // 8) % 2 == half]
         total = got[mine[0], 128:168, :].astype(F32)
         for g in mine[1:]:
             total = total + got[g, 128:168, :].astype(F32)
@@ -173,7 +178,7 @@
         tiles.append(jnp.where(sub < 4, pltpu.roll(a, 4, 0), b))
     p = place[0] >> 1
     column = 4 * ((6 * p + 8 + (p >> 4)) & 31) + 2 * (place[0] & 1)
-    own = 2 * p
+    own = 8 * (p & 7) + 2 * (p >> 3)
     whole, part = total[96:104], total[104:112]
     packed = [
         jnp.where(lane < 64, whole, pltpu.roll(part, 64, 1)),
@@ -185,7 +190,7 @@
             tile = tiles[6 * low + b_first]
             if b_last != b_first:
                 tile = jnp.where(column >= 24 * p - 128 * b_first, tile, tiles[6 * low + b_last])
-            out[2 * p + low] = tile.astype(BF)
+            out[seat(2 * p + low)] = tile.astype(BF)
     for low in range(2):
         out[own + low] = packed[low].astype(BF)
 
@@ -195,15 +200,17 @@
     for j in range(12):
         q = (6 * p + j // 2) & 31
         odd = q & 1
-        tile = got[32 * odd + 2 * ((11 * (((q - odd) >> 1) + 12)) & 15) + j % 2].astype(F32) * scale
+        holder = 16 * odd + ((11 * (((q - odd) >> 1) + 12)) & 15)
+        tile = got[8 * (holder & 7) + 2 * (holder >> 3) + j % 2].astype(F32) * scale
         for y in range(2):
             for o in range(ABPO):
                 aux_out[2 * j + y : 2 * j + y + 1, 128 * o : 128 * o + 128] = tile[
                     4 * y + o : 4 * y + o + 1
                 ]
     sub = lax.broadcasted_iota(jnp.int32, (8, 128), 0)
-    first = got[2 * p].astype(F32) * scale
-    last = got[2 * p + 1].astype(F32) * scale
+    own = 8 * (p & 7) + 2 * (p >> 3)
+    first = got[own].astype(F32) * scale
+    last = got[own + 1].astype(F32) * scale
     mid = jnp.where(sub < 4, pltpu.roll(first, 64, 1), pltpu.roll(pltpu.roll(last, 64, 1), 4, 0))
     virt_out[0:8, :] = first[:, 0:48]
     virt_out[8:16, :] = mid[:, 0:48]
@@ -236,7 +243,8 @@
 
 
 def on_device(integrals, amplitudes, pno_density, pno_coef, pao_blocks, aux_slice, aux_offset):
-    place = [(2 * lax.axis_index("pair") + lax.axis_index("low")).reshape(1)]
+    pair = 8 * lax.axis_index("y") + lax.axis_index("x")
+    place = [(2 * pair + lax.axis_index("low")).reshape(1)]
     scale = 1.0 / math.sqrt(PAIRS * 32)
     sds = jax.ShapeDtypeStruct
     names = pltpu.SMEM((2, PAIRS), jnp.int32)
@@ -270,7 +278,7 @@
             amplitudes,
         ],
     )
-    other = lax.ppermute(other, "pair", [(i, i ^ 1) for i in range(32)])
+    other = lax.ppermute(other, ("y", "x"), [(i, i ^ 1) for i in range(32)])
     (filled,) = call(
         piece_kernel,
         [ints, amps, coef],
@@ -285,7 +293,7 @@
         scratch=[pltpu.VMEM((GROUP, ROWS1 - 128, 128), BF), pltpu.SemaphoreType.DMA(())],
         in_place=filled,
     )
-    got = lax.all_to_all(sent, ("pair", "low"), split_axis=0, concat_axis=0, tiled=True)
+    got = lax.all_to_all(sent, ("x", "y", "low"), split_axis=0, concat_axis=0, tiled=True)
     (sent,) = call(
         place_kernel,
         [got],
@@ -300,7 +308,7 @@
         [sds((GROUP, 8, 128), BF)],
         place,
     )
-    got = lax.all_to_all(sent, ("pair", "low"), split_axis=0, concat_axis=0, tiled=True)
+    got = lax.all_to_all(sent, ("x", "y", "low"), split_axis=0, concat_axis=0, tiled=True)
     aux, virt = call(
         lambda *refs: final_kernel(*refs, scale=scale),
         [got],
@@ -311,10 +319,10 @@
 
 
 def solution(mesh):
-    split = Mesh(mesh.devices.reshape(32, 8, 2), ("pair", "high", "low"))
-    every = ("pair", "high", "low")
+    every = ("y", "x", "high", "low")
+    split = Mesh(mesh.devices.reshape(4, 8, 8, 2), every)
     in_specs = (P(every, None, None),) * 4 + (P(every, None),) * 3
-    out_specs = (P(("high", "low"), "pair"),) * 2
+    out_specs = (P(("high", "low"), ("y", "x")),) * 2
     return jax.shard_map(
         on_device, mesh=split, in_specs=in_specs, out_specs=out_specs, check_vma=False
     )

time: 102 us -> 102 us (level)
    all_to_all x2, blocking collectives: 56.2 us -> 55.1 us  [on_device(): lax.all_to_all(sent, ('x', 'y', 'low'), split_axis=0, concat_axis=0, tile...]
where the time goes in v9:
time: 102 us
  blocking collectives  86.3 us (85%)
  starting transfers between devices  8.79 us (9%)
  Pallas kernels  5.56 us (5%)
    all_to_all x2, blocking collectives, on_device(): lax.all_to_all(sent, ('x', 'y', 'low'), split_axis=0, concat_axis=0, tile...  55.1 us
    all_to_all x1, blocking collectives, on_device(): got = lax.all_to_all(sent, 'high', split_axis=0, concat_axis=0, tiled=True)  31.2 us
    ppermute x1, starting transfers between devices, on_device(): other = lax.ppermute(other, ('y', 'x'), [(i, i ^ 1) for i in range(32)])  8.79 us
    pallas_call x6, Pallas kernels, call(): pl.pallas_call(body, in_specs=[smem] * len(scalars) + [some] * len(lead)...  5.56 us
  transfers between devices with their start and end apart: 1, of which 1 were waited for; matrix products, arithmetic and copies ran while one was open for 0% of the time, Pallas kernels for 1%

profile of v9, /device:TPU:1, one launch (start us, length us, event | category | flops | bytes accessed | tf_op | source)
XLA Modules:
  0.0 101.9 jit_solution(15696903226645843692)
XLA Ops:
  0.6 2.3 %shard_map.86 = (f32[36,128,128]{2,1,0:T(8,128)S(1)}, bf16[18,128,128]{2,1,0:T(8,128)(2,1)S(1)}, bf16[16,64,256]{2,1,0:T(8,128)(2,1)S(1)}, bf16[16,64,256]{2,1,0...) custom-call(s32[1]{0:T(128)} %bitcast.place.refs_0_, bf16[16,64,64]{2,1,0:T(8,128)(2,1)} %dens_in.1, ...), custom_call_target="tpu_custom_call" | custom-call | tf_op jit(solution)/shard_map/pallas_call | solution.py:234
  2.9 8.8 %collective-permute-start = (bf16[18,128,128]{2,1,0:T(8,128)(2,1)S(1)}, bf16[18,128,128]{2,1,0:T(8,128)(2,1)S(1)}, u32[]{:S(2)}, u32[]{:S(2)}) collective-permute-start(bf16[18,128,128]{2,1,0:T(8,128)(2,1)S(1)} %get-tuple-element.14), channel_id=1, source_target_pairs={{0,16},{16,0},{32,48},{48,32},{64,80},{80,64},{96,112},{112,96},{1... | collective-permute-start | bytes 1769480 | tf_op jit(solution)/shard_map/ppermute | solution.py:281
  11.7 1.0 %shard_map.87.filled = bf16[64,168,128]{2,1,0:T(8,128)(2,1)S(1)} custom-call(bf16[16,64,256]{2,1,0:T(8,128)(2,1)S(1)} %get-tuple-element.10.ints, bf16[16,64,64]{2,1,0:T(8,128)(2,1)S(1)} %get-tuple-element.11.amps, bf16[16,64,256]{2,1,0:T(8,128)(2,1)S(1)} %get-tuple-element.12.coef), custom_call_target="tpu_custom_call" | custom-call | tf_op jit(solution)/shard_map/pallas_call | solution.py:234
  12.8 0.6 collective-permute-done.other
  13.3 0.2 shard_map.88
  13.6 40.2 %all_to_all.15.got = bf16[64,168,128]{2,1,0:T(8,128)(2,1)S(1)} all-to-all(bf16[64,168,128]{2,1,0:T(8,128)(2,1)S(1)} %shard_map.88), channel_id=1, replica_groups=mesh['y'=4,'x'=8,'high'=8,'low'=2] {'x','y','low'}, dimensions={0} | all-to-all | bytes 5505024 | tf_op jit(solution)/shard_map/all_to_all | solution.py:296
  53.8 1.3 %shard_map.89 = bf16[8,112,128]{2,1,0:T(8,128)(2,1)S(1)} custom-call(bf16[64,168,128]{2,1,0:T(8,128)(2,1)S(1)} %all_to_all.15.got), custom_call_target="tpu_custom_call" | custom-call | tf_op jit(solution)/shard_map/pallas_call | solution.py:234
  55.0 31.2 %all_to_all.16.got = bf16[8,112,128]{2,1,0:T(8,128)(2,1)S(1)} all-to-all(bf16[8,112,128]{2,1,0:T(8,128)(2,1)S(1)} %shard_map.89), channel_id=1, replica_groups=mesh['y'=4,'x'=8,'high'=8,'low'=2] {'high'}, dimensions={0} | all-to-all | bytes 458752 | tf_op jit(solution)/shard_map/all_to_all | solution.py:304
  86.2 0.1 shard_map.90
  86.3 14.9 %all_to_all.17.refs_1_ = bf16[64,8,128]{2,1,0:T(8,128)(2,1)S(1)} all-to-all(bf16[64,8,128]{2,1,0:T(8,128)(2,1)S(1)} %shard_map.90), channel_id=1, replica_groups=mesh['y'=4,'x'=8,'high'=8,'low'=2] {'x','y','low'}, dimensions={0} | all-to-all | bytes 262144 | tf_op jit(solution)/shard_map/all_to_all | solution.py:311
  101.2 0.7 shard_map.91
Async XLA Ops:
  2.9 10.4 %collective-permute-start = (bf16[18,128,128]{2,1,0:T(8,128)(2,1)S(1)}, bf16[18,128,128]{2,1,0:T(8,128)(2,1)S(1)}, u32[]{:S(2)}, u32[]{:S(2)}) collective-permute-start(bf16[18,128,128]{2,1,0:T(8,128)(2,1)S(1)} %get-tuple-element.14), channel_id=1, source_target_pairs={{0,16},{16,0},{32,48},{48,32},{64,80},{80,64},{96,112},{112,96},{1... | collective-permute-start | bytes 1769480 | tf_op jit(solution)/shard_map/ppermute | solution.py:281

commit v10 on v9

--- a/solution.py
+++ b/solution.py
@@ -125,19 +125,25 @@
     copy.wait()
 
 
-def place_kernel(got, out, hot, acc):
+def place_kernel(got, out, acc):
     lane = lax.broadcasted_iota(jnp.int32, (1, 128), 1)
     cell = lax.broadcasted_iota(jnp.int32, (384, 128), 0)
-    for i in range(GROUP // 2):
+
+    def hot(i):
         first = got[2 * i, 160:168, :].astype(F32)
         second = got[2 * i + 1, 160:168, :].astype(F32)
         both = jnp.where(lane < 64, first, second)
         target = both[4:5] * 24.0 + both[5:6] * 4.0 + both[6:7]
-        hot[:, 128 * i : 128 * i + 128] = (cell == target.astype(jnp.int32)).astype(BF)
-    data = jnp.concatenate(
-        [got[:, 0:64, :].reshape(4096, 128), got[:, 64:128, :].reshape(4096, 128)], 1
-    )
-    acc[...] = dot10(hot[...], data)
+        return (cell == target.astype(jnp.int32)).astype(BF)
+
+    for q in range(8):
+        eight = slice(8 * q, 8 * q + 8)
+        rows = jnp.concatenate([hot(i) for i in range(4 * q, 4 * q + 4)], 1)
+        data = jnp.concatenate(
+            [got[eight, 0:64, :].reshape(512, 128), got[eight, 64:128, :].reshape(512, 128)], 1
+        )
+        part = dot10(rows, data)
+        acc[...] = part if q == 0 else acc[...] + part
     lanes8 = lax.broadcasted_iota(jnp.int32, (8, 128), 1)
     for half in range(2):
         mine = [g for g in range(GROUP) if (g // 8) % 2 == half]
@@ -299,7 +305,7 @@
         [got],
         [sds((8, ROWS2, 128), BF)],
         [],
-        [pltpu.VMEM((384, 4096), BF), pltpu.VMEM((384, 256), F32)],
+        scratch=[pltpu.VMEM((384, 256), F32)],
     )
     got = lax.all_to_all(sent, "high", split_axis=0, concat_axis=0, tiled=True)
     (sent,) = call(

time: 102 us -> 102 us (level)
  no operation moved by 1% of the time
where the time goes in v10:
time: 102 us
  blocking collectives  86.3 us (85%)
  starting transfers between devices  8.79 us (9%)
  Pallas kernels  5.3 us (5%)
    all_to_all x2, blocking collectives, on_device(): lax.all_to_all(sent, ('x', 'y', 'low'), split_axis=0, concat_axis=0, tile...  55.1 us
    all_to_all x1, blocking collectives, on_device(): got = lax.all_to_all(sent, 'high', split_axis=0, concat_axis=0, tiled=True)  31.2 us
    ppermute x1, starting transfers between devices, on_device(): other = lax.ppermute(other, ('y', 'x'), [(i, i ^ 1) for i in range(32)])  8.79 us
    pallas_call x6, Pallas kernels, call(): pl.pallas_call(body, in_specs=[smem] * len(scalars) + [some] * len(lead)...  5.3 us
  transfers between devices with their start and end apart: 1, of which 1 were waited for; matrix products, arithmetic and copies ran while one was open for 0% of the time, Pallas kernels for 1%

profile of v10, /device:TPU:1, one launch (start us, length us, event | category | flops | bytes accessed | tf_op | source)
XLA Modules:
  0.0 101.6 jit_solution(4812555735198056834)
XLA Ops:
  0.6 2.3 %shard_map.86 = (f32[36,128,128]{2,1,0:T(8,128)S(1)}, bf16[18,128,128]{2,1,0:T(8,128)(2,1)S(1)}, bf16[16,64,256]{2,1,0:T(8,128)(2,1)S(1)}, bf16[16,64,256]{2,1,0...) custom-call(s32[1]{0:T(128)} %bitcast.place.refs_0_, bf16[16,64,64]{2,1,0:T(8,128)(2,1)} %dens_in.1, ...), custom_call_target="tpu_custom_call" | custom-call | tf_op jit(solution)/shard_map/pallas_call | solution.py:240
  2.9 8.8 %collective-permute-start = (bf16[18,128,128]{2,1,0:T(8,128)(2,1)S(1)}, bf16[18,128,128]{2,1,0:T(8,128)(2,1)S(1)}, u32[]{:S(2)}, u32[]{:S(2)}) collective-permute-start(bf16[18,128,128]{2,1,0:T(8,128)(2,1)S(1)} %get-tuple-element.14), channel_id=1, source_target_pairs={{0,16},{16,0},{32,48},{48,32},{64,80},{80,64},{96,112},{112,96},{1... | collective-permute-start | bytes 1769480 | tf_op jit(solution)/shard_map/ppermute | solution.py:287
  11.7 1.0 %shard_map.87.filled = bf16[64,168,128]{2,1,0:T(8,128)(2,1)S(1)} custom-call(bf16[16,64,256]{2,1,0:T(8,128)(2,1)S(1)} %get-tuple-element.10.ints, bf16[16,64,64]{2,1,0:T(8,128)(2,1)S(1)} %get-tuple-element.11.amps, bf16[16,64,256]{2,1,0:T(8,128)(2,1)S(1)} %get-tuple-element.12.coef), custom_call_target="tpu_custom_call" | custom-call | tf_op jit(solution)/shard_map/pallas_call | solution.py:240
  12.8 0.6 collective-permute-done.other
  13.3 0.2 shard_map.88
  13.6 40.2 %all_to_all.15.got = bf16[64,168,128]{2,1,0:T(8,128)(2,1)S(1)} all-to-all(bf16[64,168,128]{2,1,0:T(8,128)(2,1)S(1)} %shard_map.88), channel_id=1, replica_groups=mesh['y'=4,'x'=8,'high'=8,'low'=2] {'x','y','low'}, dimensions={0} | all-to-all | bytes 5505024 | tf_op jit(solution)/shard_map/all_to_all | solution.py:302
  53.8 1.0 shard_map.89
  54.8 31.2 %all_to_all.16.got = bf16[8,112,128]{2,1,0:T(8,128)(2,1)S(1)} all-to-all(bf16[8,112,128]{2,1,0:T(8,128)(2,1)S(1)} %shard_map.89), channel_id=1, replica_groups=mesh['y'=4,'x'=8,'high'=8,'low'=2] {'high'}, dimensions={0} | all-to-all | bytes 458752 | tf_op jit(solution)/shard_map/all_to_all | solution.py:310
  86.0 0.1 shard_map.90
  86.1 14.9 %all_to_all.17.refs_1_ = bf16[64,8,128]{2,1,0:T(8,128)(2,1)S(1)} all-to-all(bf16[64,8,128]{2,1,0:T(8,128)(2,1)S(1)} %shard_map.90), channel_id=1, replica_groups=mesh['y'=4,'x'=8,'high'=8,'low'=2] {'x','y','low'}, dimensions={0} | all-to-all | bytes 262144 | tf_op jit(solution)/shard_map/all_to_all | solution.py:317
  100.9 0.7 shard_map.91
Async XLA Ops:
  2.9 10.4 %collective-permute-start = (bf16[18,128,128]{2,1,0:T(8,128)(2,1)S(1)}, bf16[18,128,128]{2,1,0:T(8,128)(2,1)S(1)}, u32[]{:S(2)}, u32[]{:S(2)}) collective-permute-start(bf16[18,128,128]{2,1,0:T(8,128)(2,1)S(1)} %get-tuple-element.14), channel_id=1, source_target_pairs={{0,16},{16,0},{32,48},{48,32},{64,80},{80,64},{96,112},{112,96},{1... | collective-permute-start | bytes 1769480 | tf_op jit(solution)/shard_map/ppermute | solution.py:287

commit v11 on v10

--- a/solution.py
+++ b/solution.py
@@ -40,20 +40,18 @@
 
 
 def virtual_kernel(
-    place, dens_in, coef_in, blocks_in, owners_in, offsets_in, ints_in, amps_in,
-    acc, other, coef, ints, amps, labels,
-    dens, weighted, blocks, owners, offsets, sems,
+    place, dens_in, coef_in, blocks_in, ints_in, amps_in,
+    acc, other, coef, ints, amps, dens, weighted, blocks, sems,
 ):
-    moves = [
-        (blocks_in, blocks), (coef_in, coef), (dens_in, dens), (owners_in, owners),
-        (offsets_in, offsets), (ints_in, ints), (amps_in, amps),
-    ]
+    moves = [(blocks_in, blocks), (coef_in, coef), (dens_in, dens), (ints_in, ints), (amps_in, amps)]
     copies = [pltpu.make_async_copy(*move, sems.at[i]) for i, move in enumerate(moves)]
-    for copy in copies:
+    for copy in copies[:3]:
         copy.start()
     acc[...] = jnp.zeros(acc.shape, F32)
     for copy in copies[:3]:
         copy.wait()
+    for copy in copies[3:]:
+        copy.start()
     for p in range(PAIRS):
         weighted[p] = dot00(dens[p], coef[p]).astype(BF)
     for p in range(PAIRS):
@@ -68,14 +66,33 @@
             other[3 * i + j] = acc[6 * i + j + 3 - 3 * core].astype(BF)
     for copy in copies[3:]:
         copy.wait()
+
+
+def piece_kernel(
+    blocks_in, owners_in, offsets_in, ints, amps, coef,
+    out, labels, pieces, three_index, blocks, owners, offsets, sems,
+):
+    moves = [(blocks_in, blocks), (owners_in, owners), (offsets_in, offsets)]
+    copies = [pltpu.make_async_copy(*move, sems.at[i]) for i, move in enumerate(moves)]
+    for copy in copies:
+        copy.start()
+    for p in range(PAIRS):
+        three_index[p] = dot00(amps[p], ints[p]).astype(BF)
+    for copy in copies:
+        copy.wait()
     lane = lax.broadcasted_iota(jnp.int32, (1, 128), 1) % 64
     slice_row = jnp.zeros((1, 128), jnp.int32)
     block_row = jnp.zeros((1, 128), jnp.int32)
     offset_row = jnp.zeros((1, 128), jnp.int32)
     for p in range(PAIRS):
+        piece = dot00(coef[p], three_index[p])
         for h in range(2):
             for k in range(2):
-                here = lane == 4 * p + 2 * h + k
+                slot = 4 * p + 2 * h + k
+                pieces[pl.ds(slot, 128, STRIDE), :] = piece[
+                    128 * h : 128 * h + 128, 128 * k : 128 * k + 128
+                ]
+                here = lane == slot
                 slice_row = jnp.where(here, owners[k, p], slice_row)
                 block_row = jnp.where(here, blocks[h, p], block_row)
                 offset_row = jnp.where(here, offsets[k, p], offset_row)
@@ -83,18 +100,6 @@
     labels[...] = jnp.where(
         sub == 4, slice_row, jnp.where(sub == 5, block_row, offset_row)
     ).astype(F32)
-
-
-def piece_kernel(ints, amps, coef, out, pieces, three_index):
-    for p in range(PAIRS):
-        three_index[p] = dot00(amps[p], ints[p]).astype(BF)
-    for p in range(PAIRS):
-        piece = dot00(coef[p], three_index[p])
-        for h in range(2):
-            for k in range(2):
-                pieces[pl.ds(4 * p + 2 * h + k, 128, STRIDE), :] = piece[
-                    128 * h : 128 * h + 128, 128 * k : 128 * k + 128
-                ]
     for g in range(GROUP):
         for y in range(2):
             at = (2 * taken(g) + y) * STRIDE
@@ -254,7 +259,7 @@
     scale = 1.0 / math.sqrt(PAIRS * 32)
     sds = jax.ShapeDtypeStruct
     names = pltpu.SMEM((2, PAIRS), jnp.int32)
-    acc, other, coef, ints, amps, labels = call(
+    acc, other, coef, ints, amps = call(
         virtual_kernel,
         [],
         [
@@ -263,33 +268,36 @@
             sds((PAIRS, 64, 256), BF),
             sds((PAIRS, 64, 256), BF),
             sds((PAIRS, 64, 64), BF),
-            sds((8, 128), F32),
         ],
         place,
         [
             pltpu.VMEM((PAIRS, 64, 64), BF),
             pltpu.VMEM((PAIRS, 64, 256), BF),
             names,
-            names,
-            names,
-            pltpu.SemaphoreType.DMA((7,)),
+            pltpu.SemaphoreType.DMA((5,)),
         ],
         held=[
             pno_density,
             jnp.swapaxes(pno_coef, 1, 2),
             pao_blocks.T,
-            aux_slice.T,
-            aux_offset.T,
             jnp.swapaxes(integrals, 1, 2),
             amplitudes,
         ],
     )
     other = lax.ppermute(other, ("y", "x"), [(i, i ^ 1) for i in range(32)])
-    (filled,) = call(
+    filled, labels = call(
         piece_kernel,
         [ints, amps, coef],
-        [sds((GROUP, ROWS1, 128), BF)],
-        scratch=[pltpu.VMEM((128 * STRIDE, 128), F32), pltpu.VMEM((PAIRS, 64, 256), BF)],
+        [sds((GROUP, ROWS1, 128), BF), sds((8, 128), F32)],
+        scratch=[
+            pltpu.VMEM((128 * STRIDE, 128), F32),
+            pltpu.VMEM((PAIRS, 64, 256), BF),
+            names,
+            names,
+            names,
+            pltpu.SemaphoreType.DMA((3,)),
+        ],
+        held=[pao_blocks.T, aux_slice.T, aux_offset.T],
     )
     (sent,) = call(
         rest_kernel,

time: 102 us -> 103 us (level)
  Pallas kernels: 5.3 us -> 6.94 us
    pallas_call x6, Pallas kernels: 5.3 us -> 6.94 us  [call(): pl.pallas_call(body, in_specs=[smem] * len(scalars) + [some] * len(lead)...]
  transfers between devices with their start and end apart: 1 -> 1, of which waited for: 1 -> 0; matrix products, arithmetic and copies ran while one was open for 0% -> 0% of each run, Pallas kernels for 1% -> 2%
where the time goes in v11:
time: 103 us; the launch traced here: 102 us
  blocking collectives  86.1 us (84%)
  starting transfers between devices  8.79 us (9%)
  Pallas kernels  6.94 us (7%)
    all_to_all x2, blocking collectives, on_device(): lax.all_to_all(sent, ('x', 'y', 'low'), split_axis=0, concat_axis=0, tile...  54.9 us
    all_to_all x1, blocking collectives, on_device(): got = lax.all_to_all(sent, 'high', split_axis=0, concat_axis=0, tiled=True)  31.2 us
    ppermute x1, starting transfers between devices, on_device(): other = lax.ppermute(other, ('y', 'x'), [(i, i ^ 1) for i in range(32)])  8.79 us
    pallas_call x6, Pallas kernels, call(): pl.pallas_call(body, in_specs=[smem] * len(scalars) + [some] * len(lead)...  6.94 us
  transfers between devices with their start and end apart: 1, of which 0 were waited for; matrix products, arithmetic and copies ran while one was open for 0% of the time, Pallas kernels for 2%

profile of v11, /device:TPU:1, one launch (start us, length us, event | category | flops | bytes accessed | tf_op | source)
XLA Modules:
  0.0 102.5 jit_solution(1579706391914383672)
XLA Ops:
  0.6 3.2 %shard_map.86 = (f32[36,128,128]{2,1,0:T(8,128)S(1)}, bf16[18,128,128]{2,1,0:T(8,128)(2,1)S(1)}, bf16[16,64,256]{2,1,0:T(8,128)(2,1)S(1)}, bf16[16,64,256]{2,1,0:T(8,128)(2,1)S(1)}, bf16[16,64,64]{2,1,0:T(8,128)(2,1)S(1)}) custom-call(s32[1]{0:T(128)} %bitcast.place.refs_0_, bf16[16,64,64]{2,1,0:T(8,128)(2,1)} %dens_in.1, bf16[16,64,256]{2,1,0:T(8,128)(2,1)} %bitcast.8, ...), custom_call_target="tpu_custom_call" | custom-call | tf_op jit(solution)/shard_map/pallas_call | solution.py:245
  3.8 8.8 %collective-permute-start = (bf16[18,128,128]{2,1,0:T(8,128)(2,1)S(1)}, bf16[18,128,128]{2,1,0:T(8,128)(2,1)S(1)}, u32[]{:S(2)}, u32[]{:S(2)}) collective-permute-start(bf16[18,128,128]{2,1,0:T(8,128)(2,1)S(1)} %get-tuple-element.16), channel_id=1, source_target_pairs={{0,16},{16,0},{32,48},{48,32},{64,80},{80,64},{96,112},{112,96},{1... | collective-permute-start | bytes 1769480 | tf_op jit(solution)/shard_map/ppermute | solution.py:287
  12.6 1.8 %shard_map.87 = (bf16[64,168,128]{2,1,0:T(8,128)(2,1)S(1)}, f32[8,128]{1,0:T(8,128)S(1)}) custom-call(s32[2,16]{1,0:T(2,128)} %bitcast.11, s32[2,16]{1,0:T(2,128)} %bitcast.12, s32[2,16]{1,0:T(2,128)} %bitcast.13, bf16[16,64,256]{2,1,0:T(8,128)(2,1)S(1)} %get-tuple-element.11.ints, bf16[16,64,64]{2,1,0:T(8,128)(2,1)S(1)} %get-tuple-element.12.amps, ...), custom_call_target="tpu_custom_call" | custom-call | tf_op jit(solution)/shard_map/pallas_call | solution.py:245
  14.4 0.0 collective-permute-done.other
  14.4 0.2 shard_map.88
  14.6 40.0 %all_to_all.15.got = bf16[64,168,128]{2,1,0:T(8,128)(2,1)S(1)} all-to-all(bf16[64,168,128]{2,1,0:T(8,128)(2,1)S(1)} %shard_map.88), channel_id=1, replica_groups=mesh['y'=4,'x'=8,'high'=8,'low'=2] {'x','y','low'}, dimensions={0} | all-to-all | bytes 5505024 | tf_op jit(solution)/shard_map/all_to_all | solution.py:310
  54.6 1.0 shard_map.89
  55.6 31.2 %all_to_all.16.got = bf16[8,112,128]{2,1,0:T(8,128)(2,1)S(1)} all-to-all(bf16[8,112,128]{2,1,0:T(8,128)(2,1)S(1)} %shard_map.89), channel_id=1, replica_groups=mesh['y'=4,'x'=8,'high'=8,'low'=2] {'high'}, dimensions={0} | all-to-all | bytes 458752 | tf_op jit(solution)/shard_map/all_to_all | solution.py:318
  86.8 0.1 shard_map.90
  86.9 14.9 %all_to_all.17.refs_1_ = bf16[64,8,128]{2,1,0:T(8,128)(2,1)S(1)} all-to-all(bf16[64,8,128]{2,1,0:T(8,128)(2,1)S(1)} %shard_map.90), channel_id=1, replica_groups=mesh['y'=4,'x'=8,'high'=8,'low'=2] {'x','y','low'}, dimensions={0} | all-to-all | bytes 262144 | tf_op jit(solution)/shard_map/all_to_all | solution.py:325
  101.8 0.7 shard_map.91
Async XLA Ops:
  3.8 10.6 %collective-permute-start = (bf16[18,128,128]{2,1,0:T(8,128)(2,1)S(1)}, bf16[18,128,128]{2,1,0:T(8,128)(2,1)S(1)}, u32[]{:S(2)}, u32[]{:S(2)}) collective-permute-start(bf16[18,128,128]{2,1,0:T(8,128)(2,1)S(1)} %get-tuple-element.16), channel_id=1, source_target_pairs={{0,16},{16,0},{32,48},{48,32},{64,80},{80,64},{96,112},{112,96},{1... | collective-permute-start | bytes 1769480 | tf_op jit(solution)/shard_map/ppermute | solution.py:287

commit v12 on v10

--- a/solution.py
+++ b/solution.py
@@ -45,7 +45,7 @@
     dens, weighted, blocks, owners, offsets, sems,
 ):
     moves = [
-        (blocks_in, blocks), (coef_in, coef), (dens_in, dens), (owners_in, owners),
+        (coef_in, coef), (dens_in, dens), (blocks_in, blocks), (owners_in, owners),
         (offsets_in, offsets), (ints_in, ints), (amps_in, amps),
     ]
     copies = [pltpu.make_async_copy(*move, sems.at[i]) for i, move in enumerate(moves)]

time: 102 us -> 102 us (level)
  no operation moved by 1% of the time
where the time goes in v12:
time: 102 us
  blocking collectives  86.3 us (85%)
  starting transfers between devices  8.79 us (9%)
  Pallas kernels  5.31 us (5%)
    all_to_all x2, blocking collectives, on_device(): lax.all_to_all(sent, ('x', 'y', 'low'), split_axis=0, concat_axis=0, tile...  55.1 us
    all_to_all x1, blocking collectives, on_device(): got = lax.all_to_all(sent, 'high', split_axis=0, concat_axis=0, tiled=True)  31.2 us
    ppermute x1, starting transfers between devices, on_device(): other = lax.ppermute(other, ('y', 'x'), [(i, i ^ 1) for i in range(32)])  8.79 us
    pallas_call x6, Pallas kernels, call(): pl.pallas_call(body, in_specs=[smem] * len(scalars) + [some] * len(lead)...  5.31 us
  transfers between devices with their start and end apart: 1, of which 1 were waited for; matrix products, arithmetic and copies ran while one was open for 0% of the time, Pallas kernels for 1%

profile of v12, /device:TPU:1, one launch (start us, length us, event | category | flops | bytes accessed | tf_op | source)
XLA Modules:
  0.0 101.6 jit_solution(4460206936125531784)
XLA Ops:
  0.6 2.3 %shard_map.86 = (f32[36,128,128]{2,1,0:T(8,128)S(1)}, bf16[18,128,128]{2,1,0:T(8,128)(2,1)S(1)}, bf16[16,64,256]{2,1,0:T(8,128)(2,1)S(1)}, bf16[16,64,256]{2,1,0...) custom-call(s32[1]{0:T(128)} %bitcast.place.refs_0_, bf16[16,64,64]{2,1,0:T(8,128)(2,1)} %dens_in.1, ...), custom_call_target="tpu_custom_call" | custom-call | tf_op jit(solution)/shard_map/pallas_call | solution.py:240
  2.9 8.8 %collective-permute-start = (bf16[18,128,128]{2,1,0:T(8,128)(2,1)S(1)}, bf16[18,128,128]{2,1,0:T(8,128)(2,1)S(1)}, u32[]{:S(2)}, u32[]{:S(2)}) collective-permute-start(bf16[18,128,128]{2,1,0:T(8,128)(2,1)S(1)} %get-tuple-element.14), channel_id=1, source_target_pairs={{0,16},{16,0},{32,48},{48,32},{64,80},{80,64},{96,112},{112,96},{1... | collective-permute-start | bytes 1769480 | tf_op jit(solution)/shard_map/ppermute | solution.py:287
  11.7 1.0 %shard_map.87.filled = bf16[64,168,128]{2,1,0:T(8,128)(2,1)S(1)} custom-call(bf16[16,64,256]{2,1,0:T(8,128)(2,1)S(1)} %get-tuple-element.10.ints, bf16[16,64,64]{2,1,0:T(8,128)(2,1)S(1)} %get-tuple-element.11.amps, bf16[16,64,256]{2,1,0:T(8,128)(2,1)S(1)} %get-tuple-element.12.coef), custom_call_target="tpu_custom_call" | custom-call | tf_op jit(solution)/shard_map/pallas_call | solution.py:240
  12.8 0.6 collective-permute-done.other
  13.3 0.2 shard_map.88
  13.6 40.2 %all_to_all.15.got = bf16[64,168,128]{2,1,0:T(8,128)(2,1)S(1)} all-to-all(bf16[64,168,128]{2,1,0:T(8,128)(2,1)S(1)} %shard_map.88), channel_id=1, replica_groups=mesh['y'=4,'x'=8,'high'=8,'low'=2] {'x','y','low'}, dimensions={0} | all-to-all | bytes 5505024 | tf_op jit(solution)/shard_map/all_to_all | solution.py:302
  53.8 1.0 shard_map.89
  54.8 31.2 %all_to_all.16.got = bf16[8,112,128]{2,1,0:T(8,128)(2,1)S(1)} all-to-all(bf16[8,112,128]{2,1,0:T(8,128)(2,1)S(1)} %shard_map.89), channel_id=1, replica_groups=mesh['y'=4,'x'=8,'high'=8,'low'=2] {'high'}, dimensions={0} | all-to-all | bytes 458752 | tf_op jit(solution)/shard_map/all_to_all | solution.py:310
  86.0 0.1 shard_map.90
  86.1 14.9 %all_to_all.17.refs_1_ = bf16[64,8,128]{2,1,0:T(8,128)(2,1)S(1)} all-to-all(bf16[64,8,128]{2,1,0:T(8,128)(2,1)S(1)} %shard_map.90), channel_id=1, replica_groups=mesh['y'=4,'x'=8,'high'=8,'low'=2] {'x','y','low'}, dimensions={0} | all-to-all | bytes 262144 | tf_op jit(solution)/shard_map/all_to_all | solution.py:317
  100.9 0.7 shard_map.91
Async XLA Ops:
  2.9 10.4 %collective-permute-start = (bf16[18,128,128]{2,1,0:T(8,128)(2,1)S(1)}, bf16[18,128,128]{2,1,0:T(8,128)(2,1)S(1)}, u32[]{:S(2)}, u32[]{:S(2)}) collective-permute-start(bf16[18,128,128]{2,1,0:T(8,128)(2,1)S(1)} %get-tuple-element.14), channel_id=1, source_target_pairs={{0,16},{16,0},{32,48},{48,32},{64,80},{80,64},{96,112},{112,96},{1... | collective-permute-start | bytes 1769480 | tf_op jit(solution)/shard_map/ppermute | solution.py:287
